TPU v7x, 256 devices: a whole 4x4x8 slice. The times are simulated.
256 devices in a mesh: dp: 16 (over z_hi, x, core), fsdp: 16 (over y, z_lo).
Axes of the slice: x: 4, y: 4, z: 8 (z_hi: 2, z_lo: 4; z = z_hi * 4 + z_lo), core: 2. Of those that a mesh axis runs over, the one named last changes fastest.
Arguments:
- token_ids: int32 [32768], P('dp'), may hold values from 0 to 30527, as said below
- embed_table: bfloat16 [30528, 768], P('fsdp'), may hold values from -16 to 16, as said below
- w_qkv: bfloat16 [768, 2304], P('fsdp'), may hold values from -2 to 2
- w_out: bfloat16 [768, 768], P('fsdp'), may hold values from -0.21875 to 0.21875
- ln_gain: float32 [768], replicated, may hold values from 0.5 to 1.5
- ln_bias: float32 [768], replicated, may hold values from -1 to 1
- centroids_t: bfloat16 [768, 32768], P('fsdp', 'dp'), may hold values from -24 to 24
- assignments: int32 [32768], replicated, may hold values from 0 to 32767, as said below
Outputs:
- token_loss: float32 [32768], P(('dp', 'fsdp'))
- new_centroids: float32 [32768, 768], P(('dp', 'fsdp'))
Inputs may be any that keep to these rules, and one draw needn't show every extreme that they name: `token_ids`: id 0 is padding; a passage may end in a run of padding. `embed_table`: token embeddings of order one. `assignments`: cluster sizes are skewed.
All inputs are finite; a program needn't handle non-finite values.
Results may differ from a plain program's by a relative error of at most 0.0055.
Values may be sent and summed in bfloat16 or wider, within the bound.
No kernel may reach another device: no remote copies, remote signals or barrier semaphores. Data moves between devices by JAX's collectives and lax.ppermute only.
A program may use at most 64 MiB of HBM per device.

v0:
```python
import math

import jax
import jax.numpy as jnp
from jax import lax
from jax.sharding import Mesh
from jax.sharding import PartitionSpec as P

HEADS = 12
HEAD = 64
SEQ = 128
FSDP = ("fsdp_0", "fsdp_1")
DP_FSDP = ("dp", "fsdp_0", "fsdp_1")


def in_blocks(shard, dim, devices):
    before, after = (shard.shape[:dim], shard.shape[dim + 1 :])
    return jnp.moveaxis(shard.reshape(*before, devices, -1, *after), dim, 0)


def sent_and_summed(shard, axis, dim):
    devices = lax.axis_size(axis)
    parts = lax.all_to_all(in_blocks(shard, dim, devices), axis, 0, 0, tiled=True)
    return jnp.sum(parts.astype(jnp.float32), axis=0)


def in_one_piece(arrays, axis, dim, along):
    both = jnp.concatenate(arrays, axis=along)
    filled, at, done = (lax.all_gather(both, axis, axis=dim, tiled=True), 0, [])
    for a in arrays:
        done.append(lax.slice_in_dim(filled, at, at + a.shape[along], axis=along))
        at += a.shape[along]
    return tuple(done)


def sent_together(arrays, axis, split_dim, concat_dim, along):
    widths = [a.shape[along] for a in arrays]
    both = jnp.concatenate(arrays, axis=along)
    filled = lax.all_to_all(both, axis, split_axis=split_dim, concat_axis=concat_dim, tiled=True)
    return tuple(jnp.split(filled, [sum(widths[:k]) for k in range(1, len(widths))], axis=along))


def scatter_axes(shard, axes, dim):
    if not axes:
        return shard
    nearer = lax.psum_scatter(shard, axes[0], scatter_dimension=dim, tiled=True)
    return scatter_axes(nearer, axes[1:], dim)


def layer_norm(values, ln_gain, ln_bias):
    center = values - jnp.mean(values, axis=-1, keepdims=True)
    spread = jnp.mean(center * center, axis=-1, keepdims=True)
    return center * lax.rsqrt(spread + 1e-05) * ln_gain + ln_bias


def encode(inputs, qkv_full, out_full, ln_gain, ln_bias):
    passages = inputs.shape[0] // SEQ
    packed = jnp.dot(inputs, qkv_full, preferred_element_type=jnp.float32).astype(jnp.bfloat16)
    packed = packed.reshape(passages, SEQ, 3, HEADS, HEAD)
    scores = jnp.einsum(
        "bqhd,bkhd->bhqk", packed[:, :, 0], packed[:, :, 1], preferred_element_type=jnp.float32
    ) * (1.0 / math.sqrt(HEAD))
    probs = jax.nn.softmax(scores, axis=-1).astype(jnp.bfloat16)
    context = jnp.einsum(
        "bhqk,bkhd->bqhd", probs, packed[:, :, 2], preferred_element_type=jnp.float32
    )
    context = context.astype(jnp.bfloat16).reshape(inputs.shape[0], HEADS * HEAD)
    mixed = jnp.dot(context, out_full, preferred_element_type=jnp.float32) + inputs.astype(
        jnp.float32
    )
    return layer_norm(mixed, ln_gain, ln_bias).astype(jnp.bfloat16)


def shards(token_ids, embed_table, w_qkv, w_out, ln_gain, ln_bias, centroids_t, assignments):
    dp_size = lax.axis_size("dp")
    fsdp_size = lax.axis_size(FSDP)
    dp_rank = lax.axis_index("dp")
    fsdp_rank = lax.axis_index(FSDP)
    vocab_rows = embed_table.shape[0]
    local_ids = token_ids - fsdp_rank * vocab_rows
    inside = (local_ids >= 0) & (local_ids < vocab_rows)
    looked = jnp.take(embed_table, jnp.clip(local_ids, 0, vocab_rows - 1), axis=0)
    looked = jnp.where(inside[:, None], looked, jnp.zeros_like(looked))
    inputs = sent_and_summed(looked, FSDP, 0).astype(jnp.bfloat16)
    qkv_full, out_full, cent_full = in_one_piece((w_qkv, w_out, centroids_t), FSDP, 0, 1)
    encoded = encode(inputs, qkv_full, out_full, ln_gain, ln_bias)
    own_rows = encoded.shape[0]
    width = encoded.shape[1]
    block_width = cent_full.shape[1]
    per_dev = block_width // fsdp_size
    slab = lax.all_gather(encoded, "dp", axis=0, tiled=True)
    slab_assign = lax.dynamic_index_in_dim(
        assignments.reshape(dp_size, fsdp_size, own_rows), fsdp_rank, 1, keepdims=False
    ).reshape(-1)
    owned = slab_assign - dp_rank * block_width
    slab_rows = slab.shape[0]
    step_rows = math.gcd(slab_rows, 512)
    columns = jnp.arange(block_width, dtype=jnp.int32)

    def visit(totals, pieces):
        block_rows, local = pieces
        logits = jnp.dot(block_rows, cent_full, preferred_element_type=jnp.float32)
        peak = jnp.max(logits, axis=1)
        mass = jnp.sum(jnp.exp(logits - peak[:, None]), axis=1)
        hits = local[:, None] == columns[None, :]
        picked = jnp.sum(jnp.where(hits, logits, 0.0), axis=1)
        totals = totals + lax.dot_general(
            hits.astype(jnp.bfloat16),
            block_rows,
            (((0,), (0,)), ((), ())),
            preferred_element_type=jnp.float32,
        )
        return (totals, (peak, mass, picked))

    start = jnp.zeros((block_width, width), jnp.float32)
    partial_value, stats = lax.scan(
        visit,
        start,
        (
            slab.reshape(slab_rows // step_rows, step_rows, width),
            owned.reshape(slab_rows // step_rows, step_rows),
        ),
    )
    peaks, masses, picks = (stats[0].reshape(-1), stats[1].reshape(-1), stats[2].reshape(-1))
    got_peaks, got_masses, got_picks = sent_together(
        (
            peaks.reshape(dp_size, own_rows),
            masses.reshape(dp_size, own_rows),
            picks.reshape(dp_size, own_rows),
        ),
        "dp",
        0,
        0,
        1,
    )
    peak_own = jnp.max(got_peaks, axis=0)
    mass_own = jnp.sum(got_masses * jnp.exp(got_peaks - peak_own[None, :]), axis=0)
    pick_own = jnp.sum(got_picks, axis=0)
    token_loss = jnp.log(mass_own) + peak_own - pick_own
    totals = scatter_axes(partial_value, FSDP, 0)
    base = dp_rank * block_width + fsdp_rank * per_dev
    targets = base + jnp.arange(per_dev, dtype=jnp.int32)
    counts = jnp.sum((assignments[:, None] == targets[None, :]).astype(jnp.int32), axis=0)
    previous = lax.dynamic_slice_in_dim(cent_full, fsdp_rank * per_dev, per_dev, 1).T.astype(
        jnp.float32
    )
    new_centroids = jnp.where(
        counts[:, None] > 0, totals / jnp.maximum(counts, 1)[:, None].astype(jnp.float32), previous
    )
    return (token_loss, new_centroids)


def solution(mesh):
    finer = Mesh(mesh.devices.reshape(mesh.shape["dp"], 4, 4), ("dp", "fsdp_0", "fsdp_1"))
    placed = (P("dp"), P(FSDP, None), P(FSDP, None), P(FSDP, None), P(), P(), P(FSDP, "dp"), P())
    return jax.shard_map(
        shards,
        mesh=finer,
        in_specs=placed,
        out_specs=(P(DP_FSDP), P(DP_FSDP, None)),
        check_vma=False,
    )
```

profile of v0, /device:TPU:1, one launch (start us, length us, event | category | flops | bytes accessed | tf_op | source)
XLA Modules:
  0.0 507.1 jit_solution(12758839840471704334)
XLA Ops:
  7.2 0.0 copy-start
  7.2 0.0 all-gather.3.cloned.1.call-start
  7.2 2.1 pad_maximum_fusion
  9.3 0.0 all-gather.3.cloned.1.call-update
  9.3 0.0 all-gather.5.cloned.1.call-start
  9.4 0.7 fusion.19
  10.1 0.0 copy-done
  10.1 0.0 copy-start.3
  10.1 9.5 %gather_fusion = bf16[2048,768]{1,0:T(8,128)(2,1)} fusion(bf16[1908,768]{1,0:T(8,128)(2,1)S(1)} %copy-done, s32[2048]{0:T(1024)S(1)} %fusion.19), kind=kCustom, calls=%fused_computation | custom fusion | bytes 6299648 | tf_op jit(solution)/shard_map/jit(_take)/gather | solution.py:82
  19.5 0.0 copy-done.3
  19.6 2.3 select_select_fusion
  21.8 157.9 %all_to_all.17 = bf16[16,128,768]{2,1,0:T(8,128)(2,1)} all-to-all(bf16[16,128,768]{2,1,0:T(8,128)(2,1)S(1)} %select_select_fusion), channel_id=1, replica_groups=mesh['dp'=16,'fsdp_0'=4,'fsdp_1'=4] {'fsdp_0','fsdp_1'}, dimensions={0} | all-to-all | bytes 6291456 | tf_op jit(solution)/shard_map/all_to_all | solution.py:23
  179.7 2.3 reduce_sum.84
  182.1 0.0 copy-start.1
  182.1 69.7 %all-gather.3.cloned.1.call-done = bf16[768,5120]{1,0:T(8,128)(2,1)} async-done(((bf16[48,5120]{1,0:T(8,128)(2,1)}), bf16[768,5120]{1,0:T(8,128)(2,1)}) %all-gather.3.cloned.1.call-update) | async-done | bytes 7864336 | tf_op jit(solution)/shard_map/all_gather | solution.py:29
  251.8 3.5 convolution_convert_fusion
  255.3 1.4 copy.28
  256.7 0.0 copy-start.4
  256.7 0.0 copy-start.5
  256.7 1.3 convolution_multiply_fusion
  258.0 0.4 fusion.23
  258.4 2.5 convolution_convert_fusion.1
  260.9 1.8 fusion.24
  262.7 0.2 multiply_reduce_fusion
  263.0 0.8 add_convert_fusion
  263.8 0.0 all-gather.5.cloned.1.call-update
  263.8 0.0 reduce-scatter.3.cloned.1.call-start
  263.9 0.9 subtract_reduce_fusion
  264.8 3.9 slice.31
  268.7 66.8 %all-gather.5.cloned.1.call-done = bf16[2048,768]{1,0:T(8,128)(2,1)} async-done(((bf16[128,768]{1,0:T(8,128)(2,1)}), bf16[2048,768]{1,0:T(8,128)(2,1)}) %all-gather.5.cloned.1.call-update) | async-done | bytes 3145744 | tf_op jit(solution)/shard_map/all_gather | solution.py:91
  335.5 51.3 %while.17 = (s32[]{:T(128)}, f32[2048,768]{1,0:T(8,128)}, f32[4,512]{1,0:T(4,128)S(1)}, f32[4,512]{1,0:T(4,128)S(1)}, f32[4,512]{1,0:T(4,128)S(1)}, /*index=5*/s...) while((s32[]{:T(128)}, f32[2048,768]{1,0:T(8,128)}, ...), condition=%wide.region_9.10_spmd.clone, body=%wide.region_5.9_spmd.clone.sunk | while | flops 3231709696 | bytes 25719936 | solution.py:116
  335.5 4.0 fusion.35
  339.5 1.4 fusion.36
  340.9 0.1 dynamic_update_slice.17
  341.0 0.1 dynamic_update_slice.18
  341.0 5.8 %select_add_fusion.2 = f32[2048,768]{1,0:T(8,128)} fusion(f32[2048,768]{1,0:T(8,128)} %get-tuple-element.199, pred[]{:T(512)S(6)} %compare.3, s32[512]{0:T(512)S(1)} %bitcast.70, bf16[4,512,768]{2,1,0:T(8,128)(2,1)} %get-tuple-element.214, s32[]{:T(128)} %get-tuple-element.198), kind=kOutput, calls=%fused_computation.2.clone.1 | convolution fusion | flops 1614807040 | bytes 13371905 | tf_op jit(solution)/shard_map/while/body/eval_jaxpr/dot_general | solution.py:107
  346.9 4.0 fusion.35
  350.9 1.4 fusion.36
  352.3 0.1 dynamic_update_slice.17
  352.4 0.1 dynamic_update_slice.18
  352.4 7.7 %select_add_fusion.2 = f32[2048,768]{1,0:T(8,128)} fusion(f32[2048,768]{1,0:T(8,128)} %get-tuple-element.199, pred[]{:T(512)S(6)} %compare.3, s32[512]{0:T(512)S(1)} %bitcast.70, bf16[4,512,768]{2,1,0:T(8,128)(2,1)} %get-tuple-element.214, s32[]{:T(128)} %get-tuple-element.198), kind=kOutput, calls=%fused_computation.2.clone.1 | convolution fusion | flops 1614807040 | bytes 13371905 | tf_op jit(solution)/shard_map/while/body/eval_jaxpr/dot_general | solution.py:107
  360.2 4.0 fusion.35
  364.2 1.4 fusion.36
  365.6 0.1 dynamic_update_slice.17
  365.7 0.1 dynamic_update_slice.18
  365.7 7.7 %select_add_fusion.2 = f32[2048,768]{1,0:T(8,128)} fusion(f32[2048,768]{1,0:T(8,128)} %get-tuple-element.199, pred[]{:T(512)S(6)} %compare.3, s32[512]{0:T(512)S(1)} %bitcast.70, bf16[4,512,768]{2,1,0:T(8,128)(2,1)} %get-tuple-element.214, s32[]{:T(128)} %get-tuple-element.198), kind=kOutput, calls=%fused_computation.2.clone.1 | convolution fusion | flops 1614807040 | bytes 13371905 | tf_op jit(solution)/shard_map/while/body/eval_jaxpr/dot_general | solution.py:107
  373.5 4.0 fusion.35
  377.5 1.4 fusion.36
  378.9 0.1 dynamic_update_slice.17
  379.0 0.1 dynamic_update_slice.18
  379.0 7.7 %select_add_fusion.2 = f32[2048,768]{1,0:T(8,128)} fusion(f32[2048,768]{1,0:T(8,128)} %get-tuple-element.199, pred[]{:T(512)S(6)} %compare.3, s32[512]{0:T(512)S(1)} %bitcast.70, bf16[4,512,768]{2,1,0:T(8,128)(2,1)} %get-tuple-element.214, s32[]{:T(128)} %get-tuple-element.198), kind=kOutput, calls=%fused_computation.2.clone.1 | convolution fusion | flops 1614807040 | bytes 13371905 | tf_op jit(solution)/shard_map/while/body/eval_jaxpr/dot_general | solution.py:107
  386.8 6.6 %copy.30 = f32[2048,768]{0,1:T(8,128)} copy(f32[2048,768]{1,0:T(8,128)} %get-tuple-element.55) | data formatting | bytes 12582912 | tf_op jit(solution)/shard_map/while | solution.py:116
  393.4 0.0 reduce-scatter.3.cloned.1.call-update
  393.4 0.0 reduce-scatter.5.cloned.1.call-start
  393.5 62.0 %reduce-scatter.3.cloned.1.call-done = f32[512,768]{0,1:T(8,128)} async-done(((f32[2048,768]{0,1:T(8,128)}), f32[512,768]{0,1:T(8,128)}) %reduce-scatter.3.cloned.1.call-update) | async-done | bytes 1572880 | tf_op jit(solution)/shard_map/reduce_scatter | solution.py:46
  455.5 0.0 reduce-scatter.5.cloned.1.call-update
  455.5 5.6 %convert_reduce_fusion = s32[128]{0:T(128)S(1)} fusion(s32[128]{0:T(128)S(1)} %iota_add_fusion, s32[32768]{0:T(1024)S(1)} %copy-done.2), kind=kLoop, calls=%fused_computation.18 | loop fusion | flops 12582784 | bytes 132096 | tf_op jit(solution)/shard_map/reduce_sum | solution.py:143
  461.2 0.6 all_to_all.12
  461.8 10.1 %all-to-all-start.1 = ((f32[16,1,384]{2,1,0:T(1,128)}), f32[16,1,384]{2,1,0:T(1,128)S(1)}, u32[]{:S(2)}, u32[]{:S(2)}) async-start(f32[16,1,384]{2,1,0:T(1,128)} %all_to_all.12), calls=%async_computation.1 | async-start | bytes 49152 | tf_op jit(solution)/shard_map/all_to_all | solution.py:39
  471.9 9.7 %all-to-all-done.1 = f32[16,1,384]{2,1,0:T(1,128)S(1)} async-done(((f32[16,1,384]{2,1,0:T(1,128)}), f32[16,1,384]{2,1,0:T(1,128)S(1)}, u32[]{:S(2)}, u32[]{:S(2)}) %all-to-all-start.1) | async-done | bytes 24608 | tf_op jit(solution)/shard_map/all_to_all | solution.py:39
  481.7 0.5 add_subtract_fusion
  482.2 16.4 %reduce-scatter.5.cloned.1.call-done = f32[128,768]{0,1:T(8,128)} async-done(((f32[512,768]{0,1:T(8,128)}), f32[128,768]{0,1:T(8,128)}) %reduce-scatter.5.cloned.1.call-update) | async-done | bytes 393232 | tf_op jit(solution)/shard_map/reduce_scatter | solution.py:46
  498.6 1.1 bitcast_select_fusion
  499.6 0.9 copy.31
  (31 shorter events, 0.3 us)
Async XLA Ops:
  7.2 2.9 copy-start
  7.2 244.6 %all-gather.3.cloned.1.call-start = ((), (), s32[]{:S(2)}) async-start(), calls=%async_computation.4 | async-start | bytes 8355840 | tf_op jit(solution)/shard_map/all_gather | solution.py:29
  9.3 326.2 %all-gather.5.cloned.1.call-start = ((), (), s32[]{:S(2)}) async-start(), calls=%async_computation.5 | async-start | bytes 3342336 | tf_op jit(solution)/shard_map/all_gather | solution.py:91
  10.1 9.5 %copy-start.3 = (s32[2048]{0:T(1024)S(1)}, s32[2048]{0:T(1024)}, u32[]{:S(2)}) copy-start(s32[2048]{0:T(1024)} %param.10) | copy-start | bytes 24580
  182.1 69.7 %copy-start.1 = (bf16[128,768]{1,0:T(8,128)(2,1)}, bf16[128,768]{1,0:T(8,128)(2,1)S(1)}, u32[]{:S(2)}) copy-start(bf16[128,768]{1,0:T(8,128)(2,1)S(1)} %reduce_sum.84) | copy-start | bytes 589828
  256.7 6.3 %copy-start.4 = (f32[768]{0:T(1024)S(1)}, f32[768]{0:T(1024)}, u32[]{:S(2)}) copy-start(f32[768]{0:T(1024)} %param.15) | copy-start | bytes 9220
  256.7 6.3 %copy-start.5 = (f32[768]{0:T(1024)S(1)}, f32[768]{0:T(1024)}, u32[]{:S(2)}) copy-start(f32[768]{0:T(1024)} %param.14) | copy-start | bytes 9220
  263.8 191.7 %reduce-scatter.3.cloned.1.call-start = ((), (), s32[]{:S(2)}) async-start(), calls=%async_computation.6 | async-start | bytes 7864320 | tf_op jit(solution)/shard_map/reduce_scatter | solution.py:46
  393.4 62.1 %copy-start.2 = (s32[32768]{0:T(1024)S(1)}, s32[32768]{0:T(1024)}, u32[]{:S(2)}) copy-start(s32[32768]{0:T(1024)} %param.17) | copy-start | bytes 393220
  393.4 105.2 %reduce-scatter.5.cloned.1.call-start = ((), (), s32[]{:S(2)}) async-start(), calls=%async_computation.7 | async-start | bytes 1966080 | tf_op jit(solution)/shard_map/reduce_scatter | solution.py:46
  461.8 19.8 %all-to-all-start.1 = ((f32[16,1,384]{2,1,0:T(1,128)}), f32[16,1,384]{2,1,0:T(1,128)S(1)}, u32[]{:S(2)}, u32[]{:S(2)}) async-start(f32[16,1,384]{2,1,0:T(1,128)} %all_to_all.12), calls=%async_computation.1 | async-start | bytes 49152 | tf_op jit(solution)/shard_map/all_to_all | solution.py:39
Sparse Core Ops, SparseCore 0:
  9.8 241.9 all-gather.2
  263.9 71.5 all-gather.4
  393.5 61.9 reduce-scatter.2
  457.9 40.6 reduce-scatter.4
where the time goes:
time: 508 us; the launch traced here: 507 us
  waiting for transfers between devices  225 us (44%)
  blocking collectives  158 us (31%)
  matrix products  54.5 us (11%)
  local copies, waits for them, and re-layouts  23.6 us (5%)
  other arithmetic  22.2 us (4%)
  between operations  14 us (3%)
  starting transfers between devices  10.2 us (2%)
    all_to_all x1, blocking collectives, sent_and_summed(): lax.all_to_all(in_blocks(shard, dim, devices), axis, 0, 0, tiled=True)  158 us
    reduce_scatter x2, waiting for transfers between devices, scatter_axes(): nearer = lax.psum_scatter(shard, axes[0], scatter_dimension=dim, tiled=True)  78.4 us
    all_gather x1, waiting for transfers between devices, in_one_piece(): filled, at, done = (lax.all_gather(both, axis, axis=dim, tiled=True), 0, [])  69.7 us
    all_gather x1, waiting for transfers between devices, shards(): slab = lax.all_gather(encoded, 'dp', axis=0, tiled=True)  66.8 us
    dot_general x4, matrix products, visit(): lax.dot_general(hits.astype(jnp.bfloat16), block_rows, (((0,), (0,)), (()...  28.8 us
    dot_general x4, matrix products, visit(): logits = jnp.dot(block_rows, cent_full, preferred_element_type=jnp.float32)  16.1 us
  transfers between devices with their start and end apart: 5, of which 5 were waited for; matrix products, arithmetic and copies ran while one was open for 5% of the time, Pallas kernels for 0%

commit v1 on v0

v1 whole, which is shorter than its diff:
```python
import jax
import jax.numpy as jnp
from jax import lax
from jax.experimental import pallas as pl
from jax.experimental.pallas import tpu as pltpu
from jax.sharding import Mesh
from jax.sharding import PartitionSpec as P

HEADS = 12
HEAD = 64
SEQ = 128
DP = ("zh", "x", "core")
FS = ("y", "zl")
ALL = DP + FS
LIST = 24
SLOTS = 47
BLOCK = SLOTS + 1
F32 = jnp.float32
BF16 = jnp.bfloat16


def iota(shape, dim):
    return lax.broadcasted_iota(jnp.int32, shape, dim)


def dot(a, b, dims=((1,), (0,))):
    return lax.dot_general(a, b, (dims, ((), ())), preferred_element_type=F32)


def lists_kernel(info_ref, ids_ref, table_ref, rows_ref, count_ref):
    vocab = table_ref.shape[0]
    passages = ids_ref.shape[0]
    base = info_ref[0] * vocab
    first_slot = info_ref[1] * LIST
    earlier = iota((SEQ, SEQ), 0) < iota((SEQ, SEQ), 1)
    later = iota((SEQ, SEQ), 0) > iota((SEQ, SEQ), 1)
    owners = iota((passages, SEQ), 0) * vocab
    most = jnp.zeros((passages, 1), F32)
    found = []
    for p in range(passages):
        row = ids_ref[p : p + 1, :]
        across = jnp.broadcast_to(row, (SEQ, SEQ))
        down = across.T
        same = across == down
        new_row = jnp.max(jnp.where(same & earlier, 1.0, 0.0), axis=0, keepdims=True) < 0.5
        new_down = jnp.max(jnp.where(same & later, 1.0, 0.0), axis=1, keepdims=True) < 0.5
        mine_down = (down >= base) & (down < base + vocab)
        before = jnp.where(new_down & mine_down & (down < across), 1.0, 0.0)
        slot = jnp.sum(before, axis=0, keepdims=True).astype(jnp.int32) - first_slot
        mine = (row >= base) & (row < base + vocab)
        chosen = (iota((LIST, SEQ), 0) == slot) & mine
        found.append(jnp.max(jnp.where(chosen, (row - base).astype(F32), -1.0), axis=1, keepdims=True))
        held = (row >= owners) & (row < owners + vocab) & new_row
        most = jnp.maximum(most, jnp.sum(jnp.where(held, 1.0, 0.0), axis=1, keepdims=True))
    wanted = jnp.concatenate(found, axis=0).astype(jnp.int32)
    whole = vocab // 16 * 16
    hits = jnp.where(wanted == iota((wanted.shape[0], whole), 1), 1.0, 0.0).astype(BF16)
    rows = dot(hits, table_ref[0:whole, :])
    if whole < vocab:
        tail = table_ref[whole:vocab, :].astype(F32)
        for k in range(vocab - whole):
            rows = rows + jnp.where(wanted == whole + k, tail[k : k + 1, :], 0.0)
    rows_ref[...] = rows.astype(BF16).reshape(rows_ref.shape)
    count_ref[...] = jnp.broadcast_to(jnp.max(most, axis=0, keepdims=True), count_ref.shape).astype(
        jnp.int32
    )


def listed_rows(info, ids, table):
    passages = ids.shape[0]
    return pl.pallas_call(
        lists_kernel,
        out_shape=(
            jax.ShapeDtypeStruct((passages, LIST, table.shape[1]), BF16),
            jax.ShapeDtypeStruct((8, 128), jnp.int32),
        ),
        in_specs=[
            pl.BlockSpec(memory_space=pltpu.SMEM),
            pl.BlockSpec(memory_space=pltpu.VMEM),
            pl.BlockSpec(memory_space=pltpu.VMEM),
        ],
        out_specs=(pl.BlockSpec(memory_space=pltpu.VMEM), pl.BlockSpec(memory_space=pltpu.VMEM)),
        compiler_params=pltpu.CompilerParams(vmem_limit_bytes=40 << 20),
    )(info, ids, table)


def expand_kernel(info_ref, row_ref, vocab_ref, got_ref, out_ref):
    owners, _, width = got_ref.shape
    vocab = vocab_ref[0]
    first_slot = info_ref[1] * LIST
    row = row_ref[...]
    across = jnp.broadcast_to(row, (SEQ, SEQ))
    down = across.T

    def owner_of(ids):
        owner = jnp.zeros(ids.shape, jnp.int32)
        for k in range(1, owners):
            owner = owner + jnp.where(ids >= k * vocab, 1, 0)
        return owner

    owner_across = jnp.broadcast_to(owner_of(row), (SEQ, SEQ))
    owner_down = owner_across.T
    earlier = iota((SEQ, SEQ), 0) < iota((SEQ, SEQ), 1)
    new_row = jnp.max(jnp.where((across == down) & earlier, 1.0, 0.0), axis=0, keepdims=True) < 0.5
    before = jnp.where(new_row & (owner_across == owner_down) & (across < down), 1.0, 0.0)
    slot = jnp.sum(before, axis=1, keepdims=True).astype(jnp.int32) - first_slot
    place = owner_down[:, 0:1] * LIST + slot
    place = jnp.where((slot >= 0) & (slot < LIST), place, -1)
    hits = jnp.where(place == iota((SEQ, owners * LIST), 1), 1.0, 0.0).astype(BF16)
    out_ref[...] = dot(hits, got_ref[...].reshape(owners * LIST, width)).astype(BF16)


def expanded(info, row, vocab, got):
    return pl.pallas_call(
        expand_kernel,
        out_shape=jax.ShapeDtypeStruct((SEQ, got.shape[2]), BF16),
        in_specs=[
            pl.BlockSpec(memory_space=pltpu.SMEM),
            pl.BlockSpec(memory_space=pltpu.VMEM),
            pl.BlockSpec(memory_space=pltpu.SMEM),
            pl.BlockSpec(memory_space=pltpu.VMEM),
        ],
        out_specs=pl.BlockSpec(memory_space=pltpu.VMEM),
    )(info, row, vocab, got)


def encode_kernel(x_ref, w_ref, gain_ref, bias_ref, out_ref, packed_ref, context_ref):
    x = x_ref[...]
    part = w_ref.shape[2]
    width = x.shape[1]
    for j in range(6):
        packed_ref[:, j * part : (j + 1) * part] = dot(x, w_ref[j]).astype(BF16)
    left = iota((SEQ, 2 * HEAD), 1) < HEAD
    zero = jnp.zeros((SEQ, 2 * HEAD), BF16)
    for b in range(x.shape[0] // SEQ):
        rows = slice(b * SEQ, (b + 1) * SEQ)
        for pair in range(HEADS // 2):
            at = pair * 2 * HEAD
            q = packed_ref[rows, at : at + 2 * HEAD] * jnp.asarray(HEAD**-0.5, BF16)
            k = packed_ref[rows, width + at : width + at + 2 * HEAD]
            v = packed_ref[rows, 2 * width + at : 2 * width + at + 2 * HEAD]
            outs = []
            for one in (jnp.where(left, q, zero), jnp.where(left, zero, q)):
                s = dot(one, k, ((1,), (1,)))
                e = jnp.exp(s - jnp.max(s, axis=1, keepdims=True))
                probs = (e * (1.0 / jnp.sum(e, axis=1, keepdims=True))).astype(BF16)
                outs.append(dot(probs, v))
            context_ref[rows, at : at + 2 * HEAD] = jnp.where(left, outs[0], outs[1]).astype(BF16)
    context = context_ref[...]
    half = width // 2
    mixed = [
        dot(context, w_ref[6 + i]) + x[:, i * half : (i + 1) * half].astype(F32) for i in range(2)
    ]
    mean = sum(jnp.sum(m, axis=1, keepdims=True) for m in mixed) * (1.0 / width)
    center = [m - mean for m in mixed]
    spread = sum(jnp.sum(c * c, axis=1, keepdims=True) for c in center) * (1.0 / width)
    scale = lax.rsqrt(spread + 1e-05)
    for i in range(2):
        cols = slice(i * half, (i + 1) * half)
        out_ref[:, cols] = (center[i] * scale * gain_ref[:, cols] + bias_ref[:, cols]).astype(BF16)


def encoded(x, w, gain, bias):
    tokens, width = x.shape
    step = 2 * SEQ
    return pl.pallas_call(
        encode_kernel,
        grid=(tokens // step,),
        out_shape=jax.ShapeDtypeStruct((tokens, width), BF16),
        in_specs=[
            pl.BlockSpec((step, width), lambda i: (i, 0)),
            pl.BlockSpec(w.shape, lambda i: (0, 0, 0), pipeline_mode=pl.Buffered(1)),
            pl.BlockSpec((1, width), lambda i: (0, 0)),
            pl.BlockSpec((1, width), lambda i: (0, 0)),
        ],
        out_specs=pl.BlockSpec((step, width), lambda i: (i, 0)),
        scratch_shapes=[pltpu.VMEM((step, 3 * width), BF16), pltpu.VMEM((step, width), BF16)],
        compiler_params=pltpu.CompilerParams(vmem_limit_bytes=40 << 20),
    )(x, w, gain.reshape(1, width), bias.reshape(1, width))


def score_kernel(x_ref, local_ref, cent_ref, out_ref):
    rows = x_ref.shape[0]
    block = cent_ref.shape[1]
    s = dot(x_ref[...], cent_ref[...])
    peak = jnp.max(s, axis=1, keepdims=True)
    mass = jnp.sum(jnp.exp(s - peak), axis=1, keepdims=True)
    local = jnp.concatenate(
        [jnp.broadcast_to(local_ref[b], (SEQ, SEQ)).T[:, 0:1] for b in range(rows // SEQ)], axis=0
    )
    picked = jnp.sum(jnp.where(local == iota((rows, block), 1), s, 0.0), axis=1, keepdims=True)
    both = jnp.where(iota((rows, 128), 1) == 0, peak + jnp.log(mass), picked)
    for b in range(rows // SEQ):
        out_ref[b] = both[b * SEQ : (b + 1) * SEQ, :].T[0:8, :]


def scored(x, local, cent):
    tokens, width = x.shape
    step = 2 * SEQ
    per = step // SEQ
    return pl.pallas_call(
        score_kernel,
        grid=(tokens // step,),
        out_shape=jax.ShapeDtypeStruct((tokens // SEQ, 8, SEQ), F32),
        in_specs=[
            pl.BlockSpec((step, width), lambda i: (i, 0)),
            pl.BlockSpec((per, 1, SEQ), lambda i: (i, 0, 0)),
            pl.BlockSpec(cent.shape, lambda i: (0, 0), pipeline_mode=pl.Buffered(1)),
        ],
        out_specs=pl.BlockSpec((per, 8, SEQ), lambda i: (i, 0, 0)),
        compiler_params=pltpu.CompilerParams(vmem_limit_bytes=40 << 20),
    )(x, local.reshape(tokens // SEQ, 1, SEQ), cent)


def pack_kernel(info_ref, local_ref, mine_ref, other_ref, out_ref, hits_ref):
    dests, _, width = out_ref.shape
    per = 128
    tokens = local_ref.shape[1]
    first_slot = info_ref[1] * SLOTS
    local = local_ref[...]
    ones = jnp.ones((tokens, per), BF16)
    upper = iota((per, per), 0) < iota((per, per), 1)
    diagonal = iota((per, per), 0) == iota((per, per), 1)
    most = jnp.zeros((1, 1), F32)
    for g in range(dests):
        hits = jnp.where(local - g * per == iota((per, tokens), 0), 1.0, 0.0).astype(BF16)
        present = jnp.where(dot(hits, ones) > 0.5, 1.0, 0.0)
        rank = jnp.sum(jnp.where(upper, present, 0.0), axis=0, keepdims=True).astype(jnp.int32)
        here = jnp.sum(jnp.where(diagonal, present, 0.0), axis=0, keepdims=True)
        most = jnp.maximum(most, jnp.sum(here, axis=1, keepdims=True))
        slot = iota((BLOCK, per), 0)
        chosen = (slot < SLOTS) & (slot == rank - first_slot) & (here > 0.5)
        packing = jnp.where(chosen, 1.0, 0.0).astype(BF16)
        hits_ref[g * BLOCK : (g + 1) * BLOCK, :] = dot(packing, hits).astype(BF16)
    half = tokens // 2
    sums = dot(hits_ref[:, 0:half], mine_ref[...]) + dot(hits_ref[:, half:], other_ref[...])
    sums = sums.astype(BF16).reshape(dests, BLOCK, width)
    last = iota((dests, BLOCK, width), 1) == SLOTS
    out_ref[...] = jnp.where(last, most.reshape(1, 1, 1).astype(BF16), sums)


def packed_sums(info, local, mine, other, dests):
    tokens = local.shape[1]
    width = mine.shape[1]
    return pl.pallas_call(
        pack_kernel,
        out_shape=jax.ShapeDtypeStruct((dests, BLOCK, width), BF16),
        in_specs=[pl.BlockSpec(memory_space=pltpu.SMEM)]
        + [pl.BlockSpec(memory_space=pltpu.VMEM)] * 3,
        out_specs=pl.BlockSpec(memory_space=pltpu.VMEM),
        scratch_shapes=[pltpu.VMEM((dests * BLOCK, tokens), BF16)],
        compiler_params=pltpu.CompilerParams(vmem_limit_bytes=48 << 20),
    )(info, local, mine, other)


def count_kernel(info_ref, assign_ref, out_ref):
    dp, slabs, _ = assign_ref.shape
    targets = iota((128, SEQ), 0) + info_ref[0]
    columns = []
    for f in range(slabs):
        acc = jnp.zeros((128, SEQ), F32)
        for d in range(dp):
            acc = acc + jnp.where(assign_ref[d, f : f + 1, :] == targets, 1.0, 0.0)
        columns.append(jnp.sum(acc, axis=1, keepdims=True))
    out = jnp.zeros(out_ref.shape, F32)
    lane = iota(out_ref.shape, 1)
    for f in range(slabs):
        out = jnp.where(lane == f, columns[f], out)
    out_ref[...] = out


def counted(info, assign):
    return pl.pallas_call(
        count_kernel,
        out_shape=jax.ShapeDtypeStruct((128, 128), F32),
        in_specs=[pl.BlockSpec(memory_space=pltpu.SMEM), pl.BlockSpec(memory_space=pltpu.VMEM)],
        out_specs=pl.BlockSpec(memory_space=pltpu.VMEM),
    )(info, assign)


def unpack_kernel(info_ref, counts_ref, got_ref, out_ref):
    slabs, _, width = got_ref.shape
    counts = counts_ref[...]
    present = jnp.where(counts > 0.5, 1.0, 0.0).astype(BF16)
    lower = jnp.where(iota((128, 128), 1) < iota((128, 128), 0), 1.0, 0.0).astype(BF16)
    rank = dot(lower, present).astype(jnp.int32) - info_ref[1] * SLOTS
    slot = iota((128, BLOCK), 1)
    parts = []
    for f in range(slabs):
        chosen = (slot == rank[:, f : f + 1]) & (slot < SLOTS) & (counts[:, f : f + 1] > 0.5)
        parts.append(jnp.where(chosen, 1.0, 0.0))
    hits = jnp.concatenate(parts, axis=1).astype(BF16)
    out_ref[...] = dot(hits, got_ref[...].reshape(slabs * BLOCK, width))


def unpacked_sums(info, counts, got):
    return pl.pallas_call(
        unpack_kernel,
        out_shape=jax.ShapeDtypeStruct((128, got.shape[2]), F32),
        in_specs=[pl.BlockSpec(memory_space=pltpu.SMEM)]
        + [pl.BlockSpec(memory_space=pltpu.VMEM)] * 2,
        out_specs=pl.BlockSpec(memory_space=pltpu.VMEM),
    )(info, counts, got)


def exchanged(blocks, axis):
    return lax.all_to_all(blocks, axis, 0, 0, tiled=True)


def gathered(shard, axis):
    devices = lax.axis_size(axis)
    return exchanged(jnp.broadcast_to(shard[None], (devices,) + shard.shape), axis)


def swapped(shard, axis):
    return lax.ppermute(shard, axis, [(0, 1), (1, 0)])


def shards(token_ids, embed_table, w_qkv, w_out, ln_gain, ln_bias, centroids_t, assignments):
    core = lax.axis_index("core")
    dp_rank = lax.axis_index(DP)
    fs_rank = lax.axis_index(FS)
    fs_size = lax.axis_size(FS)
    dp_size = lax.axis_size(DP)
    x_size = lax.axis_size("x")
    vocab, width = embed_table.shape
    zero = jnp.int32(0)
    ids = token_ids.reshape(fs_size, SEQ)

    part = (w_qkv.shape[1] + w_out.shape[1]) // (2 * x_size)
    both = jnp.concatenate([w_qkv, w_out], axis=1)
    chosen = core * x_size + lax.axis_index("x")
    piece = lax.dynamic_slice_in_dim(both, chosen * part, part, 1)
    column = gathered(piece, FS).reshape(width, part)
    mine_w = gathered(column, "x")
    other_w = swapped(mine_w, "core")
    weights = jnp.where(
        core == 0,
        jnp.concatenate([mine_w, other_w], axis=0),
        jnp.concatenate([other_w, mine_w], axis=0),
    )

    rows = gathered(centroids_t, "zl").reshape(-1, centroids_t.shape[1])
    cent = gathered(rows, "y").reshape(width, -1)

    my_row = lax.dynamic_slice_in_dim(ids, fs_rank, 1, 0)
    vocab_arr = jnp.full((1,), vocab, jnp.int32)

    def info_of(first, turn):
        return jnp.stack([first, turn]).astype(jnp.int32)

    sent, most = listed_rows(info_of(fs_rank, zero), ids, embed_table)
    inputs = expanded(info_of(fs_rank, zero), my_row, vocab_arr, exchanged(sent, FS))

    def more_rows(state):
        turn, acc = state
        info = info_of(fs_rank, turn)
        again, _ = listed_rows(info, ids, embed_table)
        return turn + 1, acc + expanded(info, my_row, vocab_arr, exchanged(again, FS))

    most = most[0, 0]
    _, inputs = lax.while_loop(
        lambda state: state[0] * LIST < most, more_rows, (jnp.int32(1), inputs)
    )

    far = swapped(inputs, "zh")
    near = lax.axis_index("zh") == 0
    two = jnp.concatenate([jnp.where(near, inputs, far), jnp.where(near, far, inputs)], axis=0)
    slab = gathered(two, "x").reshape(-1, width)
    mine = encoded(slab, weights, ln_gain, ln_bias)
    other = swapped(mine, "core")

    by_dev = assignments.reshape(2, x_size, 2, fs_size, SEQ)
    of_slab = lax.dynamic_index_in_dim(by_dev, fs_rank, 3, keepdims=False)
    of_slab = jnp.transpose(of_slab, (2, 1, 0, 3))
    of_slab = jnp.where(core == 0, of_slab, of_slab[::-1])
    block = cent.shape[1]
    local = of_slab.reshape(2, -1) - dp_rank * block

    counts = counted(
        (dp_rank * block + fs_rank * (block // fs_size)).reshape(1).astype(jnp.int32),
        assignments.reshape(dp_size, fs_size, SEQ),
    )
    flat = local.reshape(1, -1)

    def one_turn(turn):
        info = info_of(zero, turn)
        got = exchanged(packed_sums(info, flat, mine, other, fs_size), FS)
        return unpacked_sums(info, counts, got), got

    sums, got = one_turn(zero)
    widest = jnp.max(got[:, SLOTS, 0:1].astype(F32)).astype(jnp.int32)
    _, sums = lax.while_loop(
        lambda state: state[0] * SLOTS < widest,
        lambda state: (state[0] + 1, state[1] + one_turn(state[0])[0]),
        (jnp.int32(1), sums),
    )

    stats = jnp.stack([scored(mine, local[0], cent), scored(other, local[1], cent)])
    stats = jnp.where(core == 0, stats, stats[::-1]).reshape(2, x_size, 2, 8, SEQ)
    stats = jnp.transpose(stats, (2, 1, 0, 3, 4)).reshape(dp_size, 8, SEQ)
    home = exchanged(stats, DP)
    lse = home[:, 0, :]
    peak = jnp.max(lse, axis=0)
    token_loss = (
        jnp.log(jnp.sum(jnp.exp(lse - peak[None, :]), axis=0)) + peak - jnp.sum(home[:, 1, :], axis=0)
    )

    total = jnp.sum(counts[:, 0:fs_size], axis=1, keepdims=True)
    previous = lax.dynamic_slice_in_dim(cent, fs_rank * 128, 128, 1).T.astype(F32)
    new_centroids = jnp.where(total > 0, sums / jnp.maximum(total, 1.0), previous)
    return token_loss, new_centroids


def solution(mesh):
    finer = Mesh(mesh.devices.reshape(2, 4, 2, 4, 4), ALL)
    placed = (P(DP), P(FS, None), P(FS, None), P(FS, None), P(), P(), P(FS, DP), P())
    return jax.shard_map(
        shards, mesh=finer, in_specs=placed, out_specs=(P(ALL), P(ALL, None)), check_vma=False
    )
```

time: 508 us -> 273 us (0.54)
  waiting for transfers between devices: 225 us -> 61.6 us
  blocking collectives: 158 us -> 73.9 us
  Pallas kernels: 0 us -> 76.1 us
  matrix products: 54.5 us -> 0 us
  starting transfers between devices: 10.2 us -> 38 us
  local copies, waits for them, and re-layouts: 23.6 us -> 9.88 us
  other arithmetic: 22.2 us -> 9.79 us
  between operations: 14 us -> 1.6 us
    all_gather x2 -> x0, waiting for transfers between devices: 136 us -> none  [the longest x1 69.7 us: in_one_piece(): filled, at, done = (lax.all_gather(both, axis, axis=dim, tiled=True), 0, [])]
    all_to_all x1 -> x3, blocking collectives: 158 us -> 73.9 us  [exchanged(): return lax.all_to_all(blocks, axis, 0, 0, tiled=True)]
    reduce_scatter x2 -> x0, waiting for transfers between devices: 78.4 us -> none  [scatter_axes(): nearer = lax.psum_scatter(shard, axes[0], scatter_dimension=dim, tiled=True)]
    pallas_call x0 -> x8, Pallas kernels: none -> 76.1 us  [the longest x1 38.7 us: encoded(): pl.pallas_call(encode_kernel, grid=(tokens // step,), out_shape=jax.Shape...]
    dot_general x12 -> x0, matrix products: 54 us -> none  [the longest x4 28.8 us: visit(): lax.dot_general(hits.astype(jnp.bfloat16), block_rows, (((0,), (0,)), (()...]
    all_to_all x1 -> x5, waiting for transfers between devices: 9.7 us -> 45.8 us  [exchanged(): return lax.all_to_all(blocks, axis, 0, 0, tiled=True)]
    all_to_all x1 -> x5, starting transfers between devices: 10.1 us -> 27.8 us  [exchanged(): return lax.all_to_all(blocks, axis, 0, 0, tiled=True)]
    ppermute x0 -> x3, waiting for transfers between devices: none -> 15.8 us  [swapped(): return lax.ppermute(shard, axis, [(0, 1), (1, 0)])]
  transfers between devices with their start and end apart: 5 -> 8, of which waited for: 5 -> 4; matrix products, arithmetic and copies ran while one was open for 5% -> 4% of each run, Pallas kernels for 0% -> 22%
where the time goes in v1:
time: 273 us; the launch traced here: 272 us
  Pallas kernels  76.1 us (28%)
  blocking collectives  73.9 us (27%)
  waiting for transfers between devices  61.6 us (23%)
  starting transfers between devices  38 us (14%)
  local copies, waits for them, and re-layouts  9.88 us (4%)
  other arithmetic  9.79 us (4%)
    all_to_all x3, blocking collectives, exchanged(): return lax.all_to_all(blocks, axis, 0, 0, tiled=True)  73.9 us
    all_to_all x5, waiting for transfers between devices, exchanged(): return lax.all_to_all(blocks, axis, 0, 0, tiled=True)  45.8 us
    pallas_call x1, Pallas kernels, encoded(): pl.pallas_call(encode_kernel, grid=(tokens // step,), out_shape=jax.Shape...  38.7 us
    all_to_all x5, starting transfers between devices, exchanged(): return lax.all_to_all(blocks, axis, 0, 0, tiled=True)  27.8 us
    ppermute x3, waiting for transfers between devices, swapped(): return lax.ppermute(shard, axis, [(0, 1), (1, 0)])  15.8 us
    pallas_call x2, Pallas kernels, scored(): pl.pallas_call(score_kernel, grid=(tokens // step,), out_shape=jax.ShapeD...  13.9 us
    pallas_call x1, Pallas kernels, packed_sums(): pl.pallas_call(pack_kernel, out_shape=jax.ShapeDtypeStruct((dests, BLOCK,...  10.7 us
    ppermute x3, starting transfers between devices, swapped(): return lax.ppermute(shard, axis, [(0, 1), (1, 0)])  10.2 us
  transfers between devices with their start and end apart: 8, of which 4 were waited for; matrix products, arithmetic and copies ran while one was open for 4% of the time, Pallas kernels for 22%

profile of v1, /device:TPU:1, one launch (start us, length us, event | category | flops | bytes accessed | tf_op | source)
XLA Modules:
  0.0 271.8 jit_solution(7339088114092588244)
XLA Ops:
  0.6 0.0 copy-start.11
  0.6 0.1 pad_add_fusion.2.info_ref
  0.7 5.5 %shard_map.95 = (bf16[16,24,768]{2,1,0:T(8,128)(2,1)}, s32[8,128]{1,0:T(8,128)S(1)}) custom-call(s32[2]{0:T(128)S(1)} %pad_add_fusion.2.info_ref, s32[16,128]{1,0:T(8,128)} %bitcast.49, bf16[1908,768]{1,0:T(8,128)(2,1)} %table_ref.1), custom_call_target="tpu_custom_call" | custom-call | tf_op jit(solution)/shard_map/pallas_call | solution.py:71
  6.3 9.2 %all-to-all-start.2 = ((bf16[16,24,768]{2,1,0:T(8,128)(2,1)}), bf16[16,24,768]{2,1,0:T(8,128)(2,1)S(1)}, u32[]{:S(2)}, u32[]{:S(2)}) async-start(bf16[16,24,768]{2,1,0:T(8,128)(2,1)} %get-tuple-element.81), calls=%async_computation.2 | async-start | bytes 1179648 | tf_op jit(solution)/shard_map/all_to_all | solution.py:307
  15.4 0.5 slice.23
  15.9 0.0 copy-done.11
  16.0 1.4 fusion
  17.4 15.2 %all-to-all-done.2.got_ref = bf16[16,24,768]{2,1,0:T(8,128)(2,1)S(1)} async-done(((bf16[16,24,768]{2,1,0:T(8,128)(2,1)}), bf16[16,24,768]{2,1,0:T(8,128)(2,1)S(1)}, u32[]{:S(2)}, u32[]{:S(2)}) %all-to-all-start.2) | async-done | bytes 589856 | tf_op jit(solution)/shard_map/all_to_all | solution.py:307
  32.6 0.0 copy-done.5
  32.6 0.8 copy-done.10
  33.4 2.3 shard_map.96
  35.6 0.0 copy-done.6
  35.6 0.6 while.20
  36.2 0.8 broadcast_in_dim.20
  37.0 20.9 %all_to_all.52 = bf16[16,48,384]{2,1,0:T(8,128)(2,1)S(1)} all-to-all(bf16[16,48,384]{2,1,0:T(8,128)(2,1)S(1)} %broadcast_in_dim.20), channel_id=1, replica_groups=mesh['zh'=2,'x'=4,'core'=2,'y'=4,'zl'=4] {'y','zl'}, dimensions={0} | all-to-all | bytes 1179648 | tf_op jit(solution)/shard_map/all_to_all | solution.py:307
  57.9 0.2 broadcast_in_dim.22
  58.1 0.0 copy-start.12
  58.2 30.9 %all_to_all.53 = bf16[4,768,384]{2,1,0:T(8,128)(2,1)} all-to-all(bf16[4,768,384]{2,1,0:T(8,128)(2,1)S(1)} %broadcast_in_dim.22), channel_id=1, replica_groups=mesh['zh'=2,'x'=4,'core'=2,'y'=4,'zl'=4] {'x'}, dimensions={0} | all-to-all | bytes 4718592 | tf_op jit(solution)/shard_map/all_to_all | solution.py:307
  89.0 0.0 copy-done.12
  89.1 1.0 broadcast_in_dim.46
  90.0 3.7 %all-to-all-start.6 = ((bf16[4,48,2048]{2,1,0:T(8,128)(2,1)}), bf16[4,48,2048]{2,1,0:T(8,128)(2,1)S(1)}, u32[]{:S(2)}, u32[]{:S(2)}) async-start(bf16[4,48,2048]{2,1,0:T(8,128)(2,1)} %broadcast_in_dim.46), calls=%async_computation.6 | async-start | bytes 1572864 | tf_op jit(solution)/shard_map/all_to_all | solution.py:307
  93.7 3.2 %collective-permute-start.1 = (bf16[4,768,384]{2,1,0:T(8,128)(2,1)}, bf16[4,768,384]{2,1,0:T(8,128)(2,1)}, u32[]{:S(2)}, u32[]{:S(2)}) collective-permute-start(bf16[4,768,384]{2,1,0:T(8,128)(2,1)} %all_to_all.53), channel_id=1, source_target_pairs={{0,16},{16,0},{1,17},{17,1},{2,18},{18,2},{3,19},{19,3},{4,20},{20... | collective-permute-start | bytes 7077896 | tf_op jit(solution)/shard_map/ppermute | solution.py:316
  96.9 0.0 copy-done.8
  96.9 4.2 %collective-permute-start = (bf16[128,768]{1,0:T(8,128)(2,1)S(1)}, bf16[128,768]{1,0:T(8,128)(2,1)S(1)}, u32[]{:S(2)}, u32[]{:S(2)}) collective-permute-start(bf16[128,768]{1,0:T(8,128)(2,1)S(1)} %copy-done.8), channel_id=1, source_target_pairs={{0,128},{128,0},{1,129},{129,1},{2,130},{130,2},{3,131},{131,3},{4... | collective-permute-start | bytes 589832 | tf_op jit(solution)/shard_map/ppermute | solution.py:316
  101.1 15.8 %collective-permute-done = bf16[128,768]{1,0:T(8,128)(2,1)S(1)} collective-permute-done((bf16[128,768]{1,0:T(8,128)(2,1)S(1)}, bf16[128,768]{1,0:T(8,128)(2,1)S(1)}, u32[]{:S(2)}, u32[]{:S(2)}) %collective-permute-start) | collective-permute-done | bytes 196640 | tf_op jit(solution)/shard_map/ppermute | solution.py:316
  117.0 4.3 %all-to-all-done.6 = bf16[4,48,2048]{2,1,0:T(8,128)(2,1)S(1)} async-done(((bf16[4,48,2048]{2,1,0:T(8,128)(2,1)}), bf16[4,48,2048]{2,1,0:T(8,128)(2,1)S(1)}, u32[]{:S(2)}, u32[]{:S(2)}) %all-to-all-start.6) | async-done | bytes 786464 | tf_op jit(solution)/shard_map/all_to_all | solution.py:307
  121.3 0.1 broadcast_in_dim.19
  121.4 22.1 %all_to_all.54 = bf16[4,256,768]{2,1,0:T(8,128)(2,1)} all-to-all(bf16[4,256,768]{2,1,0:T(8,128)(2,1)S(1)} %broadcast_in_dim.19), channel_id=1, replica_groups=mesh['zh'=2,'x'=4,'core'=2,'y'=4,'zl'=4] {'x'}, dimensions={0} | all-to-all | bytes 3145728 | tf_op jit(solution)/shard_map/all_to_all | solution.py:307
  143.5 2.0 broadcast_in_dim.48
  145.6 4.0 %all-to-all-start.7 = ((bf16[4,192,2048]{2,1,0:T(8,128)(2,1)}), bf16[4,192,2048]{2,1,0:T(8,128)(2,1)S(1)}, u32[]{:S(2)}, u32[]{:S(2)}) async-start(bf16[4,192,2048]{2,1,0:T(8,128)(2,1)} %broadcast_in_dim.48), calls=%async_computation.7 | async-start | bytes 6291456 | tf_op jit(solution)/shard_map/all_to_all | solution.py:307
  149.6 0.0 copy-done.13
  149.6 0.0 copy-done.14
  149.6 0.0 copy-start
  149.7 0.0 collective-permute-done.1
  149.7 4.6 %maximum_select_fusion.w_ref = bf16[8,768,384]{2,1,0:T(8,128)(2,1)S(1)} fusion(bf16[4,768,384]{2,1,0:T(8,128)(2,1)} %collective-permute-done.1, bf16[4,768,384]{2,1,0:T(8,128)(2,1)} %all_to_all.53, pred[]{:T(512)S(6)} %eq.8), kind=kLoop, calls=%fused_computation.2 | loop fusion | flops 7077888 | bytes 9437185 | tf_op jit(solution)/shard_map/jit(_where)/select_n | solution.py:337
  154.2 0.0 copy-done
  154.3 38.7 %shard_map.97.x_ref.mine_ref = bf16[1024,768]{1,0:T(8,128)(2,1)} custom-call(bf16[1024,768]{1,0:T(8,128)(2,1)S(1)} %bitcast.40, bf16[8,768,384]{2,1,0:T(8,128)(2,1)S(1)} %maximum_select_fusion.w_ref, f32[1,768]{1,0:T(1,128)S(1)} %reshape.71.gain_ref, f32[1,768]{1,0:T(1,128)S(1)} %reshape.72.bias_ref), custom_call_target="tpu_custom_call" | custom-call | tf_op jit(solution)/shard_map/pallas_call | solution.py:166
  193.0 2.8 %collective-permute-start.2 = (bf16[1024,768]{1,0:T(8,128)(2,1)}, bf16[1024,768]{1,0:T(8,128)(2,1)}, u32[]{:S(2)}, u32[]{:S(2)}) collective-permute-start(bf16[1024,768]{1,0:T(8,128)(2,1)} %shard_map.97.x_ref.mine_ref), channel_id=1, source_target_pairs={{0,16},{16,0},{1,17},{17,1},{2,18},{18,2},{3,19},{19,3},{4,20},{20... | collective-permute-start | bytes 4718600 | tf_op jit(solution)/shard_map/ppermute | solution.py:316
  195.8 0.8 constant_dynamic-slice_fusion
  196.7 0.0 all-to-all-done.7
  196.7 7.0 %shard_map.98 = f32[8,8,128]{2,1,0:T(8,128)S(1)} custom-call(bf16[1024,768]{1,0:T(8,128)(2,1)} %shard_map.97.x_ref.mine_ref, s32[8,1,128]{2,1,0:T(1,128)S(1)} %bitcast.44, bf16[768,2048]{1,0:T(8,128)(2,1)S(1)} %bitcast.37), custom_call_target="tpu_custom_call" | custom-call | tf_op jit(solution)/shard_map/pallas_call | solution.py:201
  203.7 0.0 collective-permute-done.2.x_ref.other_ref
  203.7 6.9 %shard_map.99 = f32[8,8,128]{2,1,0:T(8,128)S(1)} custom-call(bf16[1024,768]{1,0:T(8,128)(2,1)} %collective-permute-done.2.x_ref.other_ref, s32[8,1,128]{2,1,0:T(1,128)S(1)} %bitcast.43, bf16[768,2048]{1,0:T(8,128)(2,1)S(1)} %bitcast.38), custom_call_target="tpu_custom_call" | custom-call | tf_op jit(solution)/shard_map/pallas_call | solution.py:201
  210.7 0.6 copy.17
  211.3 6.5 %all-to-all-start.8 = ((f32[16,8,128]{2,1,0:T(8,128)}), f32[16,8,128]{2,1,0:T(8,128)S(1)}, u32[]{:S(2)}, u32[]{:S(2)}) async-start(f32[16,8,128]{2,1,0:T(8,128)} %bitcast.20), calls=%async_computation.8 | async-start | bytes 131072 | tf_op jit(solution)/shard_map/all_to_all | solution.py:307
  217.8 0.0 copy-start.4
  217.8 10.7 %shard_map.101 = bf16[16,48,768]{2,1,0:T(8,128)(2,1)S(1)} custom-call(s32[2]{0:T(128)S(1)} %broadcast_1_info_ref.2.info_ref, s32[1,2048]{1,0:T(1,128)S(1)} %bitcast.47, bf16[1024,768]{1,0:T(8,128)(2,1)} %shard_map.97.x_ref.mine_ref, bf16[1024,768]{1,0:T(8,128)(2,1)} %collective-permute-done.2.x_ref.other_ref), custom_call_target="tpu_custom_call" | custom-call | tf_op jit(solution)/shard_map/pallas_call | solution.py:245
  228.5 0.0 copy-start.1
  228.6 1.0 copy-done.1
  229.6 0.0 all-to-all-done.8
  229.6 0.0 copy-done.4
  229.6 4.5 %all-to-all-start.9 = ((bf16[16,48,768]{2,1,0:T(8,128)(2,1)}), bf16[16,48,768]{2,1,0:T(8,128)(2,1)}, u32[]{:S(2)}, u32[]{:S(2)}) async-start(bf16[16,48,768]{2,1,0:T(8,128)(2,1)} %copy-done.1), calls=%async_computation.9 | async-start | bytes 2359296 | tf_op jit(solution)/shard_map/all_to_all | solution.py:307
  234.0 2.6 shard_map.100.counts_ref
  236.7 0.1 slice_reduce_fusion
  236.8 0.5 broadcast_maximum_fusion
  237.3 0.5 add_subtract_fusion
  237.9 26.3 %all-to-all-done.9.got_ref = bf16[16,48,768]{2,1,0:T(8,128)(2,1)} async-done(((bf16[16,48,768]{2,1,0:T(8,128)(2,1)}), bf16[16,48,768]{2,1,0:T(8,128)(2,1)}, u32[]{:S(2)}, u32[]{:S(2)}) %all-to-all-start.9) | async-done | bytes 1179680 | tf_op jit(solution)/shard_map/all_to_all | solution.py:307
  264.2 1.4 slice_reduce_fusion.1
  266.2 0.0 copy-done.9
  266.2 2.4 shard_map.102
  268.6 0.3 while.21
  268.9 0.9 copy.19
  269.8 1.1 bitcast_select_fusion
  270.9 0.9 copy.20
  (24 shorter events, 0.2 us)
Async XLA Ops:
  0.6 15.3 %copy-start.11 = (s32[2048]{0:T(1024)S(1)}, s32[2048]{0:T(1024)}, u32[]{:S(2)}) copy-start(s32[2048]{0:T(1024)} %param.12) | copy-start | bytes 24580
  0.7 31.8 %copy-start.5 = (s32[2]{0:T(128)}, s32[2]{0:T(128)S(1)}, u32[]{:S(2)}) copy-start(s32[2]{0:T(128)S(1)} %pad_add_fusion.2.info_ref) | copy-start | bytes 28
  0.7 34.9 %copy-start.6 = (bf16[1908,768]{1,0:T(8,128)(2,1)S(1)}, bf16[1908,768]{1,0:T(8,128)(2,1)}, u32[]{:S(2)}) copy-start(bf16[1908,768]{1,0:T(8,128)(2,1)} %table_ref.1) | copy-start | bytes 8792068
  6.3 26.3 %all-to-all-start.2 = ((bf16[16,24,768]{2,1,0:T(8,128)(2,1)}), bf16[16,24,768]{2,1,0:T(8,128)(2,1)S(1)}, u32[]{:S(2)}, u32[]{:S(2)}) async-start(bf16[16,24,768]{2,1,0:T(8,128)(2,1)} %get-tuple-element.81), calls=%async_computation.2 | async-start | bytes 1179648 | tf_op jit(solution)/shard_map/all_to_all | solution.py:307
  32.6 0.8 copy-start.10
  58.1 30.9 %copy-start.12 = (bf16[48,2048]{1,0:T(8,128)(2,1)S(1)}, bf16[48,2048]{1,0:T(8,128)(2,1)}, u32[]{:S(2)}) copy-start(bf16[48,2048]{1,0:T(8,128)(2,1)} %param.18) | copy-start | bytes 589828
  89.0 7.8 %copy-start.8 = (bf16[128,768]{1,0:T(8,128)(2,1)S(1)}, bf16[128,768]{1,0:T(8,128)(2,1)}, u32[]{:S(2)}) copy-start(bf16[128,768]{1,0:T(8,128)(2,1)} %get-tuple-element.83) | copy-start | bytes 589828
  90.0 31.3 %all-to-all-start.6 = ((bf16[4,48,2048]{2,1,0:T(8,128)(2,1)}), bf16[4,48,2048]{2,1,0:T(8,128)(2,1)S(1)}, u32[]{:S(2)}, u32[]{:S(2)}) async-start(bf16[4,48,2048]{2,1,0:T(8,128)(2,1)} %broadcast_in_dim.46), calls=%async_computation.6 | async-start | bytes 1572864 | tf_op jit(solution)/shard_map/all_to_all | solution.py:307
  93.7 56.0 %collective-permute-start.1 = (bf16[4,768,384]{2,1,0:T(8,128)(2,1)}, bf16[4,768,384]{2,1,0:T(8,128)(2,1)}, u32[]{:S(2)}, u32[]{:S(2)}) collective-permute-start(bf16[4,768,384]{2,1,0:T(8,128)(2,1)} %all_to_all.53), channel_id=1, source_target_pairs={{0,16},{16,0},{1,17},{17,1},{2,18},{18,2},{3,19},{19,3},{4,20},{20... | collective-permute-start | bytes 7077896 | tf_op jit(solution)/shard_map/ppermute | solution.py:316
  96.9 20.0 %collective-permute-start = (bf16[128,768]{1,0:T(8,128)(2,1)S(1)}, bf16[128,768]{1,0:T(8,128)(2,1)S(1)}, u32[]{:S(2)}, u32[]{:S(2)}) collective-permute-start(bf16[128,768]{1,0:T(8,128)(2,1)S(1)} %copy-done.8), channel_id=1, source_target_pairs={{0,128},{128,0},{1,129},{129,1},{2,130},{130,2},{3,131},{131,3},{4... | collective-permute-start | bytes 589832 | tf_op jit(solution)/shard_map/ppermute | solution.py:316
  145.6 4.0 %copy-start.13 = (f32[768]{0:T(1024)S(1)}, f32[768]{0:T(1024)}, u32[]{:S(2)}) copy-start(f32[768]{0:T(1024)} %param.16) | copy-start | bytes 9220
  145.6 4.1 %copy-start.14 = (f32[768]{0:T(1024)S(1)}, f32[768]{0:T(1024)}, u32[]{:S(2)}) copy-start(f32[768]{0:T(1024)} %param.17) | copy-start | bytes 9220
  145.6 51.1 %all-to-all-start.7 = ((bf16[4,192,2048]{2,1,0:T(8,128)(2,1)}), bf16[4,192,2048]{2,1,0:T(8,128)(2,1)S(1)}, u32[]{:S(2)}, u32[]{:S(2)}) async-start(bf16[4,192,2048]{2,1,0:T(8,128)(2,1)} %broadcast_in_dim.48), calls=%async_computation.7 | async-start | bytes 6291456 | tf_op jit(solution)/shard_map/all_to_all | solution.py:307
  149.6 4.6 %copy-start = (bf16[4,256,768]{2,1,0:T(8,128)(2,1)S(1)}, bf16[4,256,768]{2,1,0:T(8,128)(2,1)}, u32[]{:S(2)}) copy-start(bf16[4,256,768]{2,1,0:T(8,128)(2,1)} %all_to_all.54) | copy-start | bytes 4718596
  193.0 10.7 %collective-permute-start.2 = (bf16[1024,768]{1,0:T(8,128)(2,1)}, bf16[1024,768]{1,0:T(8,128)(2,1)}, u32[]{:S(2)}, u32[]{:S(2)}) collective-permute-start(bf16[1024,768]{1,0:T(8,128)(2,1)} %shard_map.97.x_ref.mine_ref), channel_id=1, source_target_pairs={{0,16},{16,0},{1,17},{17,1},{2,18},{18,2},{3,19},{19,3},{4,20},{20... | collective-permute-start | bytes 4718600 | tf_op jit(solution)/shard_map/ppermute | solution.py:316
  211.3 18.3 %all-to-all-start.8 = ((f32[16,8,128]{2,1,0:T(8,128)}), f32[16,8,128]{2,1,0:T(8,128)S(1)}, u32[]{:S(2)}, u32[]{:S(2)}) async-start(f32[16,8,128]{2,1,0:T(8,128)} %bitcast.20), calls=%async_computation.8 | async-start | bytes 131072 | tf_op jit(solution)/shard_map/all_to_all | solution.py:307
  217.8 11.7 %copy-start.4 = (s32[2]{0:T(128)}, s32[2]{0:T(128)S(1)}, u32[]{:S(2)}) copy-start(s32[2]{0:T(128)S(1)} %broadcast_1_info_ref.2.info_ref) | copy-start | bytes 28
  228.5 1.0 copy-start.1
  229.6 34.6 %all-to-all-start.9 = ((bf16[16,48,768]{2,1,0:T(8,128)(2,1)}), bf16[16,48,768]{2,1,0:T(8,128)(2,1)}, u32[]{:S(2)}, u32[]{:S(2)}) async-start(bf16[16,48,768]{2,1,0:T(8,128)(2,1)} %copy-done.1), calls=%async_computation.9 | async-start | bytes 2359296 | tf_op jit(solution)/shard_map/all_to_all | solution.py:307
  236.6 29.6 %copy-start.9 = (f32[128,128]{1,0:T(8,128)}, f32[128,128]{1,0:T(8,128)S(1)}, u32[]{:S(2)}) copy-start(f32[128,128]{1,0:T(8,128)S(1)} %shard_map.100.counts_ref) | copy-start | bytes 196612

commit v2 on v1

v2 whole, which is shorter than its diff:
```python
import jax
import jax.numpy as jnp
from jax import lax
from jax.experimental import pallas as pl
from jax.experimental.pallas import tpu as pltpu
from jax.sharding import Mesh
from jax.sharding import PartitionSpec as P

HEADS = 12
HEAD = 64
SEQ = 128
DP = ("zh", "x", "core")
FS = ("y", "zl")
ALL = DP + FS
LIST = 16
SLOTS = 39
BLOCK = SLOTS + 1
ROOM = 48
F32 = jnp.float32
BF16 = jnp.bfloat16


def iota(shape, dim):
    return lax.broadcasted_iota(jnp.int32, shape, dim)


def dot(a, b, dims=((1,), (0,))):
    return lax.dot_general(a, b, (dims, ((), ())), preferred_element_type=F32)


def lists_kernel(info_ref, ids_ref, table_ref, rows_ref, count_ref, found_ref):
    vocab = table_ref.shape[0]
    passages = ids_ref.shape[0]
    base = info_ref[0] * vocab
    first_slot = info_ref[1] * LIST
    earlier = iota((SEQ, SEQ), 0) < iota((SEQ, SEQ), 1)
    later = iota((SEQ, SEQ), 0) > iota((SEQ, SEQ), 1)
    owners = iota((passages, SEQ), 0) * vocab

    def passage(p, most):
        row = ids_ref[pl.ds(p, 1), :]
        across = jnp.broadcast_to(row, (SEQ, SEQ))
        down = across.T
        same = across == down
        new_row = jnp.max(jnp.where(same & earlier, 1.0, 0.0), axis=0, keepdims=True) < 0.5
        new_down = jnp.max(jnp.where(same & later, 1.0, 0.0), axis=1, keepdims=True) < 0.5
        mine_down = (down >= base) & (down < base + vocab)
        before = jnp.where(new_down & mine_down & (down < across), 1.0, 0.0)
        slot = jnp.sum(before, axis=0, keepdims=True).astype(jnp.int32) - first_slot
        mine = (row >= base) & (row < base + vocab)
        chosen = (iota((LIST, SEQ), 0) == slot) & mine
        found = jnp.max(jnp.where(chosen, row - base, -1).astype(F32), axis=1, keepdims=True)
        found_ref[pl.ds(pl.multiple_of(p * LIST, LIST), LIST), :] = jnp.broadcast_to(found, (LIST, 128))
        held = (row >= owners) & (row < owners + vocab) & new_row
        return jnp.maximum(most, jnp.sum(jnp.where(held, 1.0, 0.0), axis=1, keepdims=True))

    most = lax.fori_loop(0, passages, passage, jnp.zeros((passages, 1), F32), unroll=4)
    wanted = found_ref[:, 0:1].astype(jnp.int32)
    whole = vocab // 16 * 16
    hits = jnp.where(wanted == iota((wanted.shape[0], whole), 1), 1.0, 0.0).astype(BF16)
    rows = dot(hits, table_ref[0:whole, :])
    if whole < vocab:
        tail = table_ref[whole:vocab, :].astype(F32)
        for k in range(vocab - whole):
            rows = rows + jnp.where(wanted == whole + k, tail[k : k + 1, :], 0.0)
    rows_ref[...] = rows.astype(BF16).reshape(rows_ref.shape)
    count_ref[...] = jnp.broadcast_to(jnp.max(most, axis=0, keepdims=True), count_ref.shape).astype(
        jnp.int32
    )


def listed_rows(info, ids, table):
    passages = ids.shape[0]
    return pl.pallas_call(
        lists_kernel,
        out_shape=(
            jax.ShapeDtypeStruct((passages, LIST, table.shape[1]), BF16),
            jax.ShapeDtypeStruct((8, 128), jnp.int32),
        ),
        in_specs=[
            pl.BlockSpec(memory_space=pltpu.SMEM),
            pl.BlockSpec(memory_space=pltpu.VMEM),
            pl.BlockSpec(memory_space=pltpu.VMEM),
        ],
        out_specs=(pl.BlockSpec(memory_space=pltpu.VMEM), pl.BlockSpec(memory_space=pltpu.VMEM)),
        scratch_shapes=[pltpu.VMEM((passages * LIST, 128), F32)],
        compiler_params=pltpu.CompilerParams(vmem_limit_bytes=40 << 20),
    )(info, ids, table)


def expand_kernel(info_ref, row_ref, vocab_ref, got_ref, out_ref):
    owners, _, width = got_ref.shape
    vocab = vocab_ref[0]
    first_slot = info_ref[1] * LIST
    row = row_ref[...]
    across = jnp.broadcast_to(row, (SEQ, SEQ))
    down = across.T

    def owner_of(ids):
        owner = jnp.zeros(ids.shape, jnp.int32)
        for k in range(1, owners):
            owner = owner + jnp.where(ids >= k * vocab, 1, 0)
        return owner

    owner_across = jnp.broadcast_to(owner_of(row), (SEQ, SEQ))
    owner_down = owner_across.T
    earlier = iota((SEQ, SEQ), 0) < iota((SEQ, SEQ), 1)
    new_row = jnp.max(jnp.where((across == down) & earlier, 1.0, 0.0), axis=0, keepdims=True) < 0.5
    before = jnp.where(new_row & (owner_across == owner_down) & (across < down), 1.0, 0.0)
    slot = jnp.sum(before, axis=1, keepdims=True).astype(jnp.int32) - first_slot
    place = owner_down[:, 0:1] * LIST + slot
    place = jnp.where((slot >= 0) & (slot < LIST), place, -1)
    hits = jnp.where(place == iota((SEQ, owners * LIST), 1), 1.0, 0.0).astype(BF16)
    out_ref[...] = dot(hits, got_ref[...].reshape(owners * LIST, width)).astype(BF16)


def expanded(info, row, vocab, got):
    return pl.pallas_call(
        expand_kernel,
        out_shape=jax.ShapeDtypeStruct((SEQ, got.shape[2]), BF16),
        in_specs=[
            pl.BlockSpec(memory_space=pltpu.SMEM),
            pl.BlockSpec(memory_space=pltpu.VMEM),
            pl.BlockSpec(memory_space=pltpu.SMEM),
            pl.BlockSpec(memory_space=pltpu.VMEM),
        ],
        out_specs=pl.BlockSpec(memory_space=pltpu.VMEM),
    )(info, row, vocab, got)


def put(sources, targets, sems):
    copies = [
        pltpu.make_async_copy(src, dst, sems.at[k])
        for k, (src, dst) in enumerate(zip(sources, targets, strict=True))
    ]
    for c in copies:
        c.start()
    for c in copies:
        c.wait()


def encode_kernel(info_ref, *refs):
    x_size = 4
    x_parts, w_parts = refs[0:x_size], refs[x_size : 3 * x_size]
    gain_ref, bias_ref, out_ref = refs[3 * x_size : 3 * x_size + 3]
    x_ref, w_ref, packed_ref, scores_ref, probs_ref, context_ref, sems = refs[3 * x_size + 3 :]
    core, at_x = info_ref[0], info_ref[1]
    places = [
        half * x_size + lax.rem(at_x - k + x_size, x_size)
        for half in (core, 1 - core)
        for k in range(x_size)
    ]
    put(
        x_parts + w_parts,
        [x_ref.at[k] for k in range(x_size)] + [w_ref.at[p] for p in places],
        sems,
    )
    part = w_ref.shape[2]
    tokens, width = x_ref.shape[1:]
    left = iota((SEQ, 2 * HEAD), 1) < HEAD
    zero = jnp.zeros((SEQ, 2 * HEAD), BF16)
    pairs = HEADS // 2
    passages = tokens // SEQ

    def stacked(values):
        return jnp.concatenate([jnp.where(left, values, zero), jnp.where(left, zero, values)], axis=0)

    def step(i, _):
        x = x_ref[i]
        for j in range(6):
            packed_ref[:, j * part : (j + 1) * part] = dot(x, w_ref[j]).astype(BF16)
        for b in range(passages):
            rows = slice(b * SEQ, (b + 1) * SEQ)
            for pair in range(pairs):
                at = pair * 2 * HEAD
                q = packed_ref[rows, at : at + 2 * HEAD] * jnp.asarray(HEAD**-0.5, BF16)
                k = packed_ref[rows, width + at : width + at + 2 * HEAD]
                scores_ref[b * pairs + pair] = dot(q, stacked(k), ((1,), (1,)))
        for n in range(passages * pairs):
            for h in range(2):
                s = scores_ref[n, :, h * SEQ : (h + 1) * SEQ]
                e = jnp.exp(s - jnp.max(s, axis=1, keepdims=True))
                probs = e * (1.0 / jnp.sum(e, axis=1, keepdims=True))
                probs_ref[n, :, h * SEQ : (h + 1) * SEQ] = probs.astype(BF16)
        for b in range(passages):
            rows = slice(b * SEQ, (b + 1) * SEQ)
            for pair in range(pairs):
                at = pair * 2 * HEAD
                v = packed_ref[rows, 2 * width + at : 2 * width + at + 2 * HEAD]
                context_ref[rows, at : at + 2 * HEAD] = dot(
                    probs_ref[b * pairs + pair], stacked(v)
                ).astype(BF16)
        context = context_ref[...]
        half = width // 2
        mixed = [
            dot(context, w_ref[6 + k]) + x[:, k * half : (k + 1) * half].astype(F32) for k in range(2)
        ]
        mean = sum(jnp.sum(m, axis=1, keepdims=True) for m in mixed) * (1.0 / width)
        center = [m - mean for m in mixed]
        spread = sum(jnp.sum(c * c, axis=1, keepdims=True) for c in center) * (1.0 / width)
        scale = lax.rsqrt(spread + 1e-05)
        for k in range(2):
            cols = slice(k * half, (k + 1) * half)
            out_ref[pl.ds(i * tokens, tokens), cols] = (
                center[k] * scale * gain_ref[:, cols] + bias_ref[:, cols]
            ).astype(BF16)
        return 0

    lax.fori_loop(0, x_size, step, 0)


def encoded(info, x_parts, w_parts, gain, bias):
    tokens, width = x_parts[0].shape
    part = w_parts[0].shape[1]
    count = len(x_parts) + len(w_parts)
    pairs = tokens // SEQ * HEADS // 2
    return pl.pallas_call(
        encode_kernel,
        out_shape=jax.ShapeDtypeStruct((len(x_parts) * tokens, width), BF16),
        in_specs=[pl.BlockSpec(memory_space=pltpu.SMEM)]
        + [pl.BlockSpec(memory_space=pl.ANY)] * count
        + [pl.BlockSpec(memory_space=pltpu.VMEM)] * 2,
        out_specs=pl.BlockSpec(memory_space=pltpu.VMEM),
        scratch_shapes=[
            pltpu.VMEM((len(x_parts), tokens, width), BF16),
            pltpu.VMEM((len(w_parts), width, part), BF16),
            pltpu.VMEM((tokens, 3 * width), BF16),
            pltpu.VMEM((pairs, SEQ, 2 * SEQ), F32),
            pltpu.VMEM((pairs, SEQ, 2 * SEQ), BF16),
            pltpu.VMEM((tokens, width), BF16),
            pltpu.SemaphoreType.DMA((count,)),
        ],
        compiler_params=pltpu.CompilerParams(vmem_limit_bytes=40 << 20),
    )(info, *x_parts, *w_parts, gain.reshape(1, width), bias.reshape(1, width))


def score_kernel(info_ref, mine_ref, other_ref, local_ref, *refs):
    own, (back_ref, low_ref, high_ref, ahead_ref) = refs[0:4], refs[4:8]
    out_ref, old_ref, cent_ref, sems = refs[8:]
    step = pl.program_id(0)
    shard = own[0].shape[0]

    @pl.when(step == 0)
    def _():
        at_y, at_zl = info_ref[0], info_ref[1]
        targets = []
        for back in range(4):
            for k in range(4):
                place = 4 * lax.rem(at_y - back + 4, 4) + lax.rem(at_zl - k + 4, 4)
                targets.append(cent_ref.at[pl.ds(pl.multiple_of(place * shard, shard), shard), :])
        far = [low_ref] * 2 + [high_ref] * 2
        spots = [(back_ref, k) for k in range(4)]
        spots += [(ref, k % 2) for k, ref in enumerate(far)]
        spots += [(ahead_ref, k) for k in range(4)]
        put(list(own) + [ref.at[pl.ds(k * shard, shard), :] for ref, k in spots], targets, sems)

    rows = mine_ref.shape[0]
    block = cent_ref.shape[1]
    half = pl.num_programs(0) // 2
    x = jnp.where(step < half, mine_ref[...], other_ref[...])
    s = dot(x, cent_ref[...])
    peak = jnp.max(s, axis=1, keepdims=True)
    mass = jnp.sum(jnp.exp(s - peak), axis=1, keepdims=True)
    local = jnp.concatenate(
        [jnp.broadcast_to(local_ref[b], (SEQ, SEQ)).T[:, 0:1] for b in range(rows // SEQ)], axis=0
    )
    picked = jnp.sum(jnp.where(local == iota((rows, block), 1), s, 0.0), axis=1, keepdims=True)
    both = jnp.where(iota((rows, 128), 1) == 0, peak + jnp.log(mass), picked)
    for b in range(rows // SEQ):
        out_ref[b] = both[b * SEQ : (b + 1) * SEQ, :].T[0:8, :]

    @pl.when(step == pl.num_programs(0) - 1)
    def _():
        per = old_ref.shape[0]
        old = cent_ref[:, pl.ds(pl.multiple_of(info_ref[2] * per, per), per)]
        old_ref[...] = old.astype(F32).T


def scored(info, mine, other, local, parts):
    tokens, width = mine.shape
    block = parts[0].shape[1]
    step = 2 * SEQ
    per = step // SEQ
    half = tokens // step
    return pl.pallas_call(
        score_kernel,
        grid=(2 * half,),
        out_shape=(
            jax.ShapeDtypeStruct((2 * tokens // SEQ, 8, SEQ), F32),
            jax.ShapeDtypeStruct((SEQ, width), F32),
        ),
        in_specs=[
            pl.BlockSpec(memory_space=pltpu.SMEM),
            pl.BlockSpec((step, width), lambda i: (jnp.minimum(i, half - 1), 0)),
            pl.BlockSpec((step, width), lambda i: (jnp.maximum(i - half, 0), 0)),
            pl.BlockSpec((per, 1, SEQ), lambda i: (i, 0, 0)),
        ]
        + [pl.BlockSpec(memory_space=pl.ANY)] * len(parts),
        out_specs=(
            pl.BlockSpec((per, 8, SEQ), lambda i: (i, 0, 0)),
            pl.BlockSpec((SEQ, width), lambda i: (0, 0)),
        ),
        scratch_shapes=[
            pltpu.VMEM((width, block), BF16),
            pltpu.SemaphoreType.DMA((16,)),
        ],
        compiler_params=pltpu.CompilerParams(vmem_limit_bytes=40 << 20),
    )(info, mine, other, local.reshape(2 * tokens // SEQ, 1, SEQ), *parts)


def pack_kernel(info_ref, local_ref, mine_ref, other_ref, out_ref, hits_ref):
    dests, _, width = out_ref.shape
    per = 128
    tokens = local_ref.shape[1]
    first_slot = info_ref[1] * SLOTS
    local = local_ref[...]
    upper = iota((per, per), 0) < iota((per, per), 1)
    diagonal = iota((per, per), 0) == iota((per, per), 1)

    def group(g, most):
        match = jnp.where(local - g * per == iota((per, tokens), 0), 1.0, 0.0)
        hits = match.astype(BF16)
        present = jnp.broadcast_to(jnp.max(match, axis=1, keepdims=True), (per, per))
        rank = jnp.sum(jnp.where(upper, present, 0.0), axis=0, keepdims=True).astype(jnp.int32)
        here = jnp.sum(jnp.where(diagonal, present, 0.0), axis=0, keepdims=True)
        slot = iota((ROOM, per), 0)
        chosen = (slot < SLOTS) & (slot == rank - first_slot) & (here > 0.5)
        packing = jnp.where(chosen, 1.0, 0.0).astype(BF16)
        hits_ref[pl.ds(pl.multiple_of(g * ROOM, ROOM), ROOM), :] = dot(packing, hits).astype(BF16)
        return jnp.maximum(most, jnp.sum(here, axis=1, keepdims=True))

    most = lax.fori_loop(0, dests, group, jnp.zeros((1, 1), F32), unroll=4)
    half = tokens // 2
    sums = dot(hits_ref[:, 0:half], mine_ref[...]) + dot(hits_ref[:, half:], other_ref[...])
    sums = sums.reshape(dests, ROOM, width)[:, 0:BLOCK, :]
    last = iota((dests, BLOCK, width), 1) == SLOTS
    out_ref[...] = jnp.where(last, most.reshape(1, 1, 1), sums).astype(BF16)


def packed_sums(info, local, mine, other, dests):
    tokens = local.shape[1]
    width = mine.shape[1]
    return pl.pallas_call(
        pack_kernel,
        out_shape=jax.ShapeDtypeStruct((dests, BLOCK, width), BF16),
        in_specs=[pl.BlockSpec(memory_space=pltpu.SMEM)]
        + [pl.BlockSpec(memory_space=pltpu.VMEM)] * 3,
        out_specs=pl.BlockSpec(memory_space=pltpu.VMEM),
        scratch_shapes=[pltpu.VMEM((dests * ROOM, tokens), BF16)],
        compiler_params=pltpu.CompilerParams(vmem_limit_bytes=48 << 20),
    )(info, local, mine, other)


def count_kernel(info_ref, assign_ref, out_ref):
    dp, slabs, _ = assign_ref.shape
    targets = iota((128, SEQ), 0) + info_ref[0]
    lane = iota(out_ref.shape, 1)

    def slab(f, out):
        acc = jnp.zeros((128, SEQ), F32)
        for d in range(dp):
            acc = acc + jnp.where(assign_ref[d, pl.ds(f, 1), :] == targets, 1.0, 0.0)
        return jnp.where(lane == f, jnp.sum(acc, axis=1, keepdims=True), out)

    out_ref[...] = lax.fori_loop(0, slabs, slab, jnp.zeros(out_ref.shape, F32))


def counted(info, assign):
    return pl.pallas_call(
        count_kernel,
        out_shape=jax.ShapeDtypeStruct((128, 128), F32),
        in_specs=[pl.BlockSpec(memory_space=pltpu.SMEM), pl.BlockSpec(memory_space=pltpu.VMEM)],
        out_specs=pl.BlockSpec(memory_space=pltpu.VMEM),
    )(info, assign)


def unpack_kernel(info_ref, counts_ref, got_ref, out_ref):
    slabs, _, width = got_ref.shape
    counts = counts_ref[...]
    present = jnp.where(counts > 0.5, 1.0, 0.0).astype(BF16)
    lower = jnp.where(iota((128, 128), 1) < iota((128, 128), 0), 1.0, 0.0).astype(BF16)
    rank = dot(lower, present).astype(jnp.int32) - info_ref[1] * SLOTS
    slot = iota((128, BLOCK), 1)
    parts = []
    for f in range(slabs):
        chosen = (slot == rank[:, f : f + 1]) & (slot < SLOTS) & (counts[:, f : f + 1] > 0.5)
        parts.append(jnp.where(chosen, 1.0, 0.0))
    hits = jnp.concatenate(parts, axis=1).astype(BF16)
    out_ref[...] = dot(hits, got_ref[...].reshape(slabs * BLOCK, width))


def unpacked_sums(info, counts, got):
    return pl.pallas_call(
        unpack_kernel,
        out_shape=jax.ShapeDtypeStruct((128, got.shape[2]), F32),
        in_specs=[pl.BlockSpec(memory_space=pltpu.SMEM)]
        + [pl.BlockSpec(memory_space=pltpu.VMEM)] * 2,
        out_specs=pl.BlockSpec(memory_space=pltpu.VMEM),
    )(info, counts, got)


def exchanged(blocks, axis):
    return lax.all_to_all(blocks, axis, 0, 0, tiled=True)


def gathered(shard, axis):
    devices = lax.axis_size(axis)
    return exchanged(jnp.broadcast_to(shard[None], (devices,) + shard.shape), axis)


def swapped(shard, axis):
    return lax.ppermute(shard, axis, [(0, 1), (1, 0)])


def turned(shard, axis, by):
    devices = lax.axis_size(axis)
    return lax.ppermute(shard, axis, [(i, (i + by) % devices) for i in range(devices)])


def backwards(values, here):
    for dim, at in enumerate(here):
        size = values.shape[dim]
        values = jnp.take(values, (at - jnp.arange(size)) % size, axis=dim)
    return values


def shards(token_ids, embed_table, w_qkv, w_out, ln_gain, ln_bias, centroids_t, assignments):
    core = lax.axis_index("core")
    dp_rank = lax.axis_index(DP)
    fs_rank = lax.axis_index(FS)
    fs_size = lax.axis_size(FS)
    dp_size = lax.axis_size(DP)
    x_size = lax.axis_size("x")
    vocab, width = embed_table.shape
    zero = jnp.int32(0)
    ids = token_ids.reshape(fs_size, SEQ)

    at_x = lax.axis_index("x")

    rows = [centroids_t] + [turned(centroids_t, "zl", k) for k in range(1, 4)]

    part = (w_qkv.shape[1] + w_out.shape[1]) // (2 * x_size)
    both = jnp.concatenate([w_qkv, w_out], axis=1)
    piece = lax.dynamic_slice_in_dim(both, (core * x_size + at_x) * part, part, 1)
    column = gathered(piece, FS).reshape(width, part)

    def info_of(*values):
        return jnp.stack(values).astype(jnp.int32)

    my_row = lax.dynamic_slice_in_dim(ids, fs_rank, 1, 0)
    vocab_arr = jnp.full((1,), vocab, jnp.int32)
    sent, most = listed_rows(info_of(fs_rank, zero), ids, embed_table)
    sent, column, *rows = lax.optimization_barrier((sent, column, *rows))
    mine_w = [column] + [turned(column, "x", k) for k in range(1, x_size)]
    got = exchanged(sent, FS)
    inputs = expanded(info_of(fs_rank, zero), my_row, vocab_arr, got)

    def more_rows(state):
        turn, acc = state
        info = info_of(fs_rank, turn)
        again, _ = listed_rows(info, ids, embed_table)
        return turn + 1, acc + expanded(info, my_row, vocab_arr, exchanged(again, FS))

    most = most[0, 0]
    _, inputs = lax.while_loop(
        lambda state: state[0] * LIST < most, more_rows, (jnp.int32(1), inputs)
    )

    two = jnp.concatenate([inputs, swapped(inputs, "zh")], axis=0)
    other_w = [swapped(w, "core") for w in mine_w]

    near = jnp.concatenate(rows, axis=0)
    back = turned(near, "y", 1)
    ahead = turned(near, "y", 3)
    two, back, ahead = lax.optimization_barrier((two, back, ahead))
    pieces = [two] + [turned(two, "x", k) for k in range(1, x_size)]
    half = near.shape[0] // 2
    far_low = turned(back[:half], "y", 1)
    far_high = turned(ahead[half:], "y", 3)
    two, far_low, far_high = lax.optimization_barrier((two, far_low, far_high))
    pieces[0] = two

    mine = encoded(info_of(core, at_x), pieces, mine_w + other_w, ln_gain, ln_bias)
    other = swapped(mine, "core")

    by_dev = assignments.reshape(2, x_size, 2, fs_size, SEQ)
    of_slab = lax.dynamic_index_in_dim(by_dev, fs_rank, 3, keepdims=False)
    of_slab = jnp.transpose(of_slab, (2, 1, 0, 3))
    here = (core, at_x, lax.axis_index("zh"))
    of_slab = backwards(of_slab, here)
    block = centroids_t.shape[1]
    local = of_slab.reshape(1, -1) - dp_rank * block

    counts = counted(
        info_of(dp_rank * block + fs_rank * (block // fs_size)),
        assignments.reshape(dp_size, fs_size, SEQ),
    )

    def one_turn(turn):
        info = info_of(zero, turn)
        got = exchanged(packed_sums(info, local, mine, other, fs_size), FS)
        return unpacked_sums(info, counts, got)

    packed = packed_sums(info_of(zero, zero), local, mine, other, fs_size)
    packed, mine, other = lax.optimization_barrier((packed, mine, other))
    got = exchanged(packed, FS)
    stats, previous = scored(
        info_of(lax.axis_index("y"), lax.axis_index("zl"), fs_rank),
        mine,
        other,
        local,
        rows + [back, far_low, far_high, ahead],
    )
    stats, got = lax.optimization_barrier((stats, got))
    stats = backwards(stats.reshape(2, x_size, 2, 8, SEQ), here)
    stats = jnp.transpose(stats, (2, 1, 0, 3, 4)).reshape(dp_size, 8, SEQ)
    sums = unpacked_sums(info_of(zero, zero), counts, got)
    widest = jnp.max(got[:, SLOTS, 0:1].astype(F32)).astype(jnp.int32)
    _, sums = lax.while_loop(
        lambda state: state[0] * SLOTS < widest,
        lambda state: (state[0] + 1, state[1] + one_turn(state[0])),
        (jnp.int32(1), sums),
    )

    home = exchanged(stats, DP)
    lse = home[:, 0, :]
    peak = jnp.max(lse, axis=0)
    token_loss = (
        jnp.log(jnp.sum(jnp.exp(lse - peak[None, :]), axis=0)) + peak - jnp.sum(home[:, 1, :], axis=0)
    )

    total = jnp.sum(counts[:, 0:fs_size], axis=1, keepdims=True)
    new_centroids = jnp.where(total > 0, sums / jnp.maximum(total, 1.0), previous)
    return token_loss, new_centroids


def solution(mesh):
    finer = Mesh(mesh.devices.reshape(2, 4, 2, 4, 4), ALL)
    placed = (P(DP), P(FS, None), P(FS, None), P(FS, None), P(), P(), P(FS, DP), P())
    return jax.shard_map(
        shards, mesh=finer, in_specs=placed, out_specs=(P(ALL), P(ALL, None)), check_vma=False
    )
```

time: 273 us -> 204 us (0.75)
  blocking collectives: 73.9 us -> 0 us
  starting transfers between devices: 38 us -> 67.6 us
  Pallas kernels: 76.1 us -> 58.9 us
  waiting for transfers between devices: 61.6 us -> 57.8 us
  other arithmetic: 9.79 us -> 6.22 us
    all_to_all x3 -> x0, blocking collectives: 73.9 us -> none  [exchanged(): return lax.all_to_all(blocks, axis, 0, 0, tiled=True)]
    ppermute x0 -> x13, waiting for transfers between devices: none -> 40.6 us  [turned(): lax.ppermute(shard, axis, [(i, (i + by) % devices) for i in range(devices)])]
    all_to_all x5 -> x4, waiting for transfers between devices: 45.8 us -> 15.9 us  [exchanged(): return lax.all_to_all(blocks, axis, 0, 0, tiled=True)]
    ppermute x0 -> x13, starting transfers between devices: none -> 23.8 us  [turned(): lax.ppermute(shard, axis, [(i, (i + by) % devices) for i in range(devices)])]
    pallas_call x3 -> x2, Pallas kernels: 52.6 us -> 34.9 us  [the longest x1 18.3 us: scored(): pl.pallas_call(score_kernel, grid=(2 * half,), out_shape=(jax.ShapeDtypeS...]
    ppermute x3 -> x6, waiting for transfers between devices: 15.8 us -> 1.3 us  [swapped(): return lax.ppermute(shard, axis, [(0, 1), (1, 0)])]
    all_to_all x5 -> x4, starting transfers between devices: 27.8 us -> 32.1 us  [exchanged(): return lax.all_to_all(blocks, axis, 0, 0, tiled=True)]
    select_n x3 -> x7, other arithmetic: 4.63 us -> 1.02 us  [backwards(): values = jnp.take(values, (at - jnp.arange(size)) % size, axis=dim)]
  transfers between devices with their start and end apart: 8 -> 23, of which waited for: 4 -> 11; matrix products, arithmetic and copies ran while one was open for 4% -> 4% of each run, Pallas kernels for 22% -> 14%
where the time goes in v2:
time: 204 us; the launch traced here: 203 us
  starting transfers between devices  67.6 us (33%)
  Pallas kernels  58.9 us (29%)
  waiting for transfers between devices  57.8 us (28%)
  local copies, waits for them, and re-layouts  10.8 us (5%)
  other arithmetic  6.22 us (3%)
    ppermute x13, waiting for transfers between devices, turned(): lax.ppermute(shard, axis, [(i, (i + by) % devices) for i in range(devices)])  40.6 us
    all_to_all x4, starting transfers between devices, exchanged(): return lax.all_to_all(blocks, axis, 0, 0, tiled=True)  32.1 us
    ppermute x13, starting transfers between devices, turned(): lax.ppermute(shard, axis, [(i, (i + by) % devices) for i in range(devices)])  23.8 us
    pallas_call x1, Pallas kernels, scored(): pl.pallas_call(score_kernel, grid=(2 * half,), out_shape=(jax.ShapeDtypeS...  18.3 us
    pallas_call x1, Pallas kernels, encoded(): pl.pallas_call(encode_kernel, out_shape=jax.ShapeDtypeStruct((len(x_parts...  16.6 us
    all_to_all x4, waiting for transfers between devices, exchanged(): return lax.all_to_all(blocks, axis, 0, 0, tiled=True)  15.9 us
    ppermute x6, starting transfers between devices, swapped(): return lax.ppermute(shard, axis, [(0, 1), (1, 0)])  11.8 us
    pallas_call x1, Pallas kernels, packed_sums(): pl.pallas_call(pack_kernel, out_shape=jax.ShapeDtypeStruct((dests, BLOCK,...  10.5 us
  transfers between devices with their start and end apart: 23, of which 11 were waited for; matrix products, arithmetic and copies ran while one was open for 4% of the time, Pallas kernels for 14%

profile of v2, /device:TPU:1, one launch (start us, length us, event | category | flops | bytes accessed | tf_op | source)
XLA Modules:
  0.0 203.5 jit_solution(55434395671792146)
XLA Ops:
  0.7 0.9 fusion
  1.5 0.9 broadcast_in_dim.83
  2.4 9.2 %all-to-all-start.2 = ((bf16[16,48,384]{2,1,0:T(8,128)(2,1)}), bf16[16,48,384]{2,1,0:T(8,128)(2,1)S(1)}, u32[]{:S(2)}, u32[]{:S(2)}) async-start(bf16[16,48,384]{2,1,0:T(8,128)(2,1)} %broadcast_in_dim.83), calls=%async_computation.2 | async-start | bytes 1179648 | tf_op jit(solution)/shard_map/all_to_all | solution.py:403
  11.6 1.4 collective-permute-start
  13.0 2.1 %collective-permute-start.1 = (bf16[48,2048]{1,0:T(8,128)(2,1)S(1)}, bf16[48,2048]{1,0:T(8,128)(2,1)S(1)}, u32[]{:S(2)}, u32[]{:S(2)}) collective-permute-start(bf16[48,2048]{1,0:T(8,128)(2,1)S(1)} %copy-done), channel_id=1, source_target_pairs={{0,2},{1,3},{2,0},{3,1},{4,6},{5,7},{6,4},{7,5},{8,10},{9,11},{10,... | collective-permute-start | bytes 589832 | tf_op jit(solution)/shard_map/ppermute | solution.py:417
  15.1 1.2 collective-permute-start.2
  16.4 5.2 %shard_map.95 = (bf16[16,16,768]{2,1,0:T(8,128)(2,1)}, s32[8,128]{1,0:T(8,128)S(1)}) custom-call(s32[2]{0:T(128)S(1)} %pad_add_fusion.4.info_ref, s32[16,128]{1,0:T(8,128)S(1)} %bitcast.55, bf16[1908,768]{1,0:T(8,128)(2,1)} %table_ref.1), custom_call_target="tpu_custom_call" | custom-call | tf_op jit(solution)/shard_map/pallas_call | solution.py:74
  21.6 6.9 %collective-permute-done.refs_1_ = bf16[48,2048]{1,0:T(8,128)(2,1)S(1)} collective-permute-done((bf16[48,2048]{1,0:T(8,128)(2,1)S(1)}, bf16[48,2048]{1,0:T(8,128)(2,1)S(1)}, u32[]{:S(2)}, u32[]{:S(2)}) %collective-permute-start) | collective-permute-done | bytes 196640 | tf_op jit(solution)/shard_map/ppermute | solution.py:417
  28.5 11.0 %collective-permute-done.1.refs_2_ = bf16[48,2048]{1,0:T(8,128)(2,1)S(1)} collective-permute-done((bf16[48,2048]{1,0:T(8,128)(2,1)S(1)}, bf16[48,2048]{1,0:T(8,128)(2,1)S(1)}, u32[]{:S(2)}, u32[]{:S(2)}) %collective-permute-start.1) | collective-permute-done | bytes 196640 | tf_op jit(solution)/shard_map/ppermute | solution.py:417
  39.5 0.7 constant_dynamic-update-slice_fusion.3
  40.2 0.7 constant_dynamic-update-slice_fusion.2
  40.9 10.0 %all-to-all-start.3 = ((bf16[16,16,768]{2,1,0:T(8,128)(2,1)}), bf16[16,16,768]{2,1,0:T(8,128)(2,1)}, u32[]{:S(2)}, u32[]{:S(2)}) async-start(bf16[16,16,768]{2,1,0:T(8,128)(2,1)} %get-tuple-element.101), calls=%async_computation.3 | async-start | bytes 786432 | tf_op jit(solution)/shard_map/all_to_all | solution.py:403
  51.0 0.7 constant_dynamic-update-slice_fusion.1
  51.7 0.7 constant_dynamic-update-slice_fusion
  52.3 1.3 collective-permute-start.4
  53.7 1.2 collective-permute-start.11
  54.9 0.5 slice.21
  55.4 1.4 collective-permute-start.5
  56.7 2.5 %collective-permute-start.12 = (bf16[768,384]{1,0:T(8,128)(2,1)S(1)}, bf16[768,384]{1,0:T(8,128)(2,1)}, u32[]{:S(2)}, u32[]{:S(2)}) collective-permute-start(bf16[768,384]{1,0:T(8,128)(2,1)S(1)} %bitcast.48), channel_id=1, source_target_pairs={{0,64},{32,96},{64,0},{96,32},{1,65},{33,97},{65,1},{97,33},{2,66}... | collective-permute-start | bytes 1769480 | tf_op jit(solution)/shard_map/ppermute | solution.py:417
  59.2 4.7 %all-to-all-done.3.got_ref = bf16[16,16,768]{2,1,0:T(8,128)(2,1)} async-done(((bf16[16,16,768]{2,1,0:T(8,128)(2,1)}), bf16[16,16,768]{2,1,0:T(8,128)(2,1)}, u32[]{:S(2)}, u32[]{:S(2)}) %all-to-all-start.3) | async-done | bytes 393248 | tf_op jit(solution)/shard_map/all_to_all | solution.py:403
  63.9 2.1 %shard_map.96 = bf16[128,768]{1,0:T(8,128)(2,1)} custom-call(s32[2]{0:T(128)} %copy-done.10, s32[1,128]{1,0:T(1,128)S(1)} %constant_dynamic-slice_fusion.row_ref, s32[1]{0:T(128)} %constant.179.clone.1.vocab_ref, bf16[16,16,768]{2,1,0:T(8,128)(2,1)} %all-to-all-done.3.got_ref), custom_call_target="tpu_custom_call" | custom-call | tf_op jit(solution)/shard_map/pallas_call | solution.py:118
  66.1 0.6 while.20
  66.6 4.3 %collective-permute-start.3 = (bf16[128,768]{1,0:T(8,128)(2,1)}, bf16[128,768]{1,0:T(8,128)(2,1)S(1)}, u32[]{:S(2)}, u32[]{:S(2)}) collective-permute-start(bf16[128,768]{1,0:T(8,128)(2,1)} %get-tuple-element.103), channel_id=1, source_target_pairs={{0,128},{128,0},{1,129},{129,1},{2,130},{130,2},{3,131},{131,3},{4... | collective-permute-start | bytes 589832 | tf_op jit(solution)/shard_map/ppermute | solution.py:412
  70.9 2.5 %collective-permute-start.13 = (bf16[768,384]{1,0:T(8,128)(2,1)S(1)}, bf16[768,384]{1,0:T(8,128)(2,1)S(1)}, u32[]{:S(2)}, u32[]{:S(2)}) collective-permute-start(bf16[768,384]{1,0:T(8,128)(2,1)S(1)} %bitcast.49), channel_id=1, source_target_pairs={{0,96},{32,0},{64,32},{96,64},{1,97},{33,1},{65,33},{97,65},{2,98}... | collective-permute-start | bytes 1769480 | tf_op jit(solution)/shard_map/ppermute | solution.py:417
  73.5 2.9 %collective-permute-done.4.refs_4_ = bf16[192,2048]{1,0:T(8,128)(2,1)S(1)} collective-permute-done((bf16[192,2048]{1,0:T(8,128)(2,1)}, bf16[192,2048]{1,0:T(8,128)(2,1)S(1)}, u32[]{:S(2)}, u32[]{:S(2)}) %collective-permute-start.4) | collective-permute-done | bytes 786464 | tf_op jit(solution)/shard_map/ppermute | solution.py:417
  76.4 0.6 collective-permute-start.14
  77.0 0.8 collective-permute-done.3
  77.8 3.2 %collective-permute-start.15 = (bf16[768,384]{1,0:T(8,128)(2,1)S(1)}, bf16[768,384]{1,0:T(8,128)(2,1)S(1)}, u32[]{:S(2)}, u32[]{:S(2)}) collective-permute-start(bf16[768,384]{1,0:T(8,128)(2,1)S(1)} %collective-permute-done.11.refs_5_), channel_id=1, source_target_pairs={{0,16},{16,0},{1,17},{17,1},{2,18},{18,2},{3,19},{19,3},{4,20},{20... | collective-permute-start | bytes 1769480 | tf_op jit(solution)/shard_map/ppermute | solution.py:412
  81.1 1.0 pad_maximum_fusion.refs_0_
  82.1 0.3 collective-permute-start.6
  82.4 2.7 %collective-permute-start.7 = (bf16[96,2048]{1,0:T(8,128)(2,1)S(1)}, bf16[96,2048]{1,0:T(8,128)(2,1)S(1)}, u32[]{:S(2)}, u32[]{:S(2)}) collective-permute-start(bf16[96,2048]{1,0:T(8,128)(2,1)S(1)} %slice.23), channel_id=1, source_target_pairs={{0,12},{4,0},{8,4},{12,8},{1,13},{5,1},{9,5},{13,9},{2,14},{6,2},{... | collective-permute-start | bytes 1179656 | tf_op jit(solution)/shard_map/ppermute | solution.py:417
  85.1 1.9 collective-permute-start.16
  87.0 3.5 %collective-permute-start.10 = (bf16[256,768]{1,0:T(8,128)(2,1)S(1)}, bf16[256,768]{1,0:T(8,128)(2,1)S(1)}, u32[]{:S(2)}, u32[]{:S(2)}) collective-permute-start(bf16[256,768]{1,0:T(8,128)(2,1)S(1)} %pad_maximum_fusion.refs_0_), channel_id=1, source_target_pairs={{0,96},{32,0},{64,32},{96,64},{1,97},{33,1},{65,33},{97,65},{2,98}... | collective-permute-start | bytes 1179656 | tf_op jit(solution)/shard_map/ppermute | solution.py:417
  90.5 3.8 %collective-permute-done.6.refs_5_ = bf16[96,2048]{1,0:T(8,128)(2,1)S(1)} collective-permute-done((bf16[96,2048]{1,0:T(8,128)(2,1)S(1)}, bf16[96,2048]{1,0:T(8,128)(2,1)S(1)}, u32[]{:S(2)}, u32[]{:S(2)}) %collective-permute-start.6) | collective-permute-done | bytes 393248 | tf_op jit(solution)/shard_map/ppermute | solution.py:417
  94.3 0.7 copy-done.1
  95.0 1.2 collective-permute-start.8
  96.3 0.7 copy-done.3
  97.0 2.5 %collective-permute-start.9 = (bf16[256,768]{1,0:T(8,128)(2,1)S(1)}, bf16[256,768]{1,0:T(8,128)(2,1)S(1)}, u32[]{:S(2)}, u32[]{:S(2)}) collective-permute-start(bf16[256,768]{1,0:T(8,128)(2,1)S(1)} %pad_maximum_fusion.refs_0_), channel_id=1, source_target_pairs={{0,64},{32,96},{64,0},{96,32},{1,65},{33,97},{65,1},{97,33},{2,66}... | collective-permute-start | bytes 1179656 | tf_op jit(solution)/shard_map/ppermute | solution.py:417
  99.6 6.5 %collective-permute-done.8.refs_1_ = bf16[256,768]{1,0:T(8,128)(2,1)S(1)} collective-permute-done((bf16[256,768]{1,0:T(8,128)(2,1)S(1)}, bf16[256,768]{1,0:T(8,128)(2,1)S(1)}, u32[]{:S(2)}, u32[]{:S(2)}) %collective-permute-start.8) | collective-permute-done | bytes 393248 | tf_op jit(solution)/shard_map/ppermute | solution.py:417
  106.1 9.4 %collective-permute-done.9.refs_2_ = bf16[256,768]{1,0:T(8,128)(2,1)S(1)} collective-permute-done((bf16[256,768]{1,0:T(8,128)(2,1)S(1)}, bf16[256,768]{1,0:T(8,128)(2,1)S(1)}, u32[]{:S(2)}, u32[]{:S(2)}) %collective-permute-start.9) | collective-permute-done | bytes 393248 | tf_op jit(solution)/shard_map/ppermute | solution.py:417
  115.5 16.6 %shard_map.97.mine_ref = bf16[1024,768]{1,0:T(8,128)(2,1)} custom-call(s32[2]{0:T(128)S(1)} %pad_add_fusion.3.info_ref, bf16[256,768]{1,0:T(8,128)(2,1)S(1)} %pad_maximum_fusion.refs_0_, bf16[256,768]{1,0:T(8,128)(2,1)S(1)} %collective-permute-done.8.refs_1_, bf16[256,768]{1,0:T(8,128)(2,1)S(1)} %collective-permute-done.9.refs_2_, ...), custom_call_target="tpu_custom_call" | custom-call | tf_op jit(solution)/shard_map/pallas_call | solution.py:217
  132.2 1.8 collective-permute-start.18
  133.9 0.8 constant_dynamic-slice_fusion.1
  134.8 0.6 gather_fusion
  135.5 0.6 gather_fusion.1
  136.2 0.6 gather_fusion.2
  136.9 0.5 collective-permute-done.18.other_ref
  137.3 10.5 %shard_map.98 = bf16[16,40,768]{2,1,0:T(8,128)(2,1)} custom-call(s32[2]{0:T(128)S(1)} %broadcast.368.info_ref, s32[1,2048]{1,0:T(1,128)S(1)} %bitcast.53, bf16[1024,768]{1,0:T(8,128)(2,1)} %shard_map.97.mine_ref, bf16[1024,768]{1,0:T(8,128)(2,1)} %collective-permute-done.18.other_ref), custom_call_target="tpu_custom_call" | custom-call | tf_op jit(solution)/shard_map/pallas_call | solution.py:343
  147.8 4.7 %all-to-all-start.4 = ((bf16[16,40,768]{2,1,0:T(8,128)(2,1)}), bf16[16,40,768]{2,1,0:T(8,128)(2,1)}, u32[]{:S(2)}, u32[]{:S(2)}) async-start(bf16[16,40,768]{2,1,0:T(8,128)(2,1)} %shard_map.98), calls=%async_computation.4 | async-start | bytes 1966080 | tf_op jit(solution)/shard_map/all_to_all | solution.py:403
  152.6 3.9 %shard_map.100.counts_ref = f32[128,128]{1,0:T(8,128)S(1)} custom-call(s32[1]{0:T(128)} %bitcast.27.info_ref, s32[16,16,128]{2,1,0:T(8,128)} %bitcast.59), custom_call_target="tpu_custom_call" | custom-call | tf_op jit(solution)/shard_map/pallas_call | solution.py:369
  156.6 0.1 slice_reduce_fusion
  156.8 18.3 %shard_map.99 = (f32[16,8,128]{2,1,0:T(8,128)S(1)}, f32[128,768]{1,0:T(8,128)S(1)}) custom-call(s32[3]{0:T(128)S(1)} %pad_add_fusion.2.info_ref, bf16[1024,768]{1,0:T(8,128)(2,1)} %shard_map.97.mine_ref, bf16[1024,768]{1,0:T(8,128)(2,1)} %collective-permute-done.18.other_ref, s32[16,1,128]{2,1,0:T(1,128)S(1)} %fusion.2.local_ref, ...), custom_call_target="tpu_custom_call" | custom-call | tf_op jit(solution)/shard_map/pallas_call | solution.py:285
  175.1 0.7 copy-done.5
  175.8 2.3 %all-to-all-done.4.got_ref = bf16[16,40,768]{2,1,0:T(8,128)(2,1)} async-done(((bf16[16,40,768]{2,1,0:T(8,128)(2,1)}), bf16[16,40,768]{2,1,0:T(8,128)(2,1)}, u32[]{:S(2)}, u32[]{:S(2)}) %all-to-all-start.4) | async-done | bytes 983072 | tf_op jit(solution)/shard_map/all_to_all | solution.py:403
  178.2 2.3 %shard_map.101 = f32[128,768]{1,0:T(8,128)S(1)} custom-call(s32[2]{0:T(128)} %copy-done.9, f32[128,128]{1,0:T(8,128)S(1)} %shard_map.100.counts_ref, bf16[16,40,768]{2,1,0:T(8,128)(2,1)} %all-to-all-done.4.got_ref), custom_call_target="tpu_custom_call" | custom-call | tf_op jit(solution)/shard_map/pallas_call | solution.py:393
  180.5 1.4 slice_reduce_fusion.2
  182.5 0.6 gather_fusion.3
  183.1 0.5 gather_fusion.4
  183.8 0.5 gather_fusion.5
  184.3 0.7 broadcast_select_fusion
  185.0 8.1 %all-to-all-start.5 = ((f32[16,8,128]{2,1,0:T(8,128)}), f32[16,8,128]{2,1,0:T(8,128)S(1)}, u32[]{:S(2)}, u32[]{:S(2)}) async-start(f32[16,8,128]{2,1,0:T(8,128)} %bitcast.25), calls=%async_computation.5 | async-start | bytes 131072 | tf_op jit(solution)/shard_map/all_to_all | solution.py:403
  193.2 0.9 divide_select_fusion
  194.0 8.9 %all-to-all-done.5 = f32[16,8,128]{2,1,0:T(8,128)S(1)} async-done(((f32[16,8,128]{2,1,0:T(8,128)}), f32[16,8,128]{2,1,0:T(8,128)S(1)}, u32[]{:S(2)}, u32[]{:S(2)}) %all-to-all-start.5) | async-done | bytes 65568 | tf_op jit(solution)/shard_map/all_to_all | solution.py:403
  203.0 0.5 add_subtract_fusion
  (68 shorter events, 1.1 us)
Async XLA Ops:
  0.6 11.0 %copy-start = (bf16[48,2048]{1,0:T(8,128)(2,1)S(1)}, bf16[48,2048]{1,0:T(8,128)(2,1)}, u32[]{:S(2)}) copy-start(bf16[48,2048]{1,0:T(8,128)(2,1)} %refs_0_) | copy-start | bytes 589828
  0.6 15.7 %copy-start.12 = (s32[2048]{0:T(1024)S(1)}, s32[2048]{0:T(1024)}, u32[]{:S(2)}) copy-start(s32[2048]{0:T(1024)} %param.12) | copy-start | bytes 24580
  2.4 37.1 %all-to-all-start.2 = ((bf16[16,48,384]{2,1,0:T(8,128)(2,1)}), bf16[16,48,384]{2,1,0:T(8,128)(2,1)S(1)}, u32[]{:S(2)}, u32[]{:S(2)}) async-start(bf16[16,48,384]{2,1,0:T(8,128)(2,1)} %broadcast_in_dim.83), calls=%async_computation.2 | async-start | bytes 1179648 | tf_op jit(solution)/shard_map/all_to_all | solution.py:403
  11.6 16.9 %collective-permute-start = (bf16[48,2048]{1,0:T(8,128)(2,1)S(1)}, bf16[48,2048]{1,0:T(8,128)(2,1)S(1)}, u32[]{:S(2)}, u32[]{:S(2)}) collective-permute-start(bf16[48,2048]{1,0:T(8,128)(2,1)S(1)} %copy-done), channel_id=1, source_target_pairs={{0,1},{1,2},{2,3},{3,0},{4,5},{5,6},{6,7},{7,4},{8,9},{9,10},{10,1... | collective-permute-start | bytes 589832 | tf_op jit(solution)/shard_map/ppermute | solution.py:417
  13.0 26.5 %collective-permute-start.1 = (bf16[48,2048]{1,0:T(8,128)(2,1)S(1)}, bf16[48,2048]{1,0:T(8,128)(2,1)S(1)}, u32[]{:S(2)}, u32[]{:S(2)}) collective-permute-start(bf16[48,2048]{1,0:T(8,128)(2,1)S(1)} %copy-done), channel_id=1, source_target_pairs={{0,2},{1,3},{2,0},{3,1},{4,6},{5,7},{6,4},{7,5},{8,10},{9,11},{10,... | collective-permute-start | bytes 589832 | tf_op jit(solution)/shard_map/ppermute | solution.py:417
  15.1 24.4 %collective-permute-start.2 = (bf16[48,2048]{1,0:T(8,128)(2,1)S(1)}, bf16[48,2048]{1,0:T(8,128)(2,1)S(1)}, u32[]{:S(2)}, u32[]{:S(2)}) collective-permute-start(bf16[48,2048]{1,0:T(8,128)(2,1)S(1)} %copy-done), channel_id=1, source_target_pairs={{0,3},{1,0},{2,1},{3,2},{4,7},{5,4},{6,5},{7,6},{8,11},{9,8},{10,9... | collective-permute-start | bytes 589832 | tf_op jit(solution)/shard_map/ppermute | solution.py:417
  16.4 23.8 %copy-start.10 = (s32[2]{0:T(128)}, s32[2]{0:T(128)S(1)}, u32[]{:S(2)}) copy-start(s32[2]{0:T(128)S(1)} %pad_add_fusion.4.info_ref) | copy-start | bytes 28
  40.9 23.0 %all-to-all-start.3 = ((bf16[16,16,768]{2,1,0:T(8,128)(2,1)}), bf16[16,16,768]{2,1,0:T(8,128)(2,1)}, u32[]{:S(2)}, u32[]{:S(2)}) async-start(bf16[16,16,768]{2,1,0:T(8,128)(2,1)} %get-tuple-element.101), calls=%async_computation.3 | async-start | bytes 786432 | tf_op jit(solution)/shard_map/all_to_all | solution.py:403
  52.3 24.0 %collective-permute-start.4 = (bf16[192,2048]{1,0:T(8,128)(2,1)}, bf16[192,2048]{1,0:T(8,128)(2,1)S(1)}, u32[]{:S(2)}, u32[]{:S(2)}) collective-permute-start(bf16[192,2048]{1,0:T(8,128)(2,1)} %constant_dynamic-update-slice_fusion), channel_id=1, source_target_pairs={{0,4},{4,8},{8,12},{12,0},{1,5},{5,9},{9,13},{13,1},{2,6},{6,10},{... | collective-permute-start | bytes 2359304 | tf_op jit(solution)/shard_map/ppermute | solution.py:417
  53.7 17.3 %collective-permute-start.11 = (bf16[768,384]{1,0:T(8,128)(2,1)S(1)}, bf16[768,384]{1,0:T(8,128)(2,1)S(1)}, u32[]{:S(2)}, u32[]{:S(2)}) collective-permute-start(bf16[768,384]{1,0:T(8,128)(2,1)S(1)} %bitcast.47), channel_id=1, source_target_pairs={{0,32},{32,64},{64,96},{96,0},{1,33},{33,65},{65,97},{97,1},{2,34}... | collective-permute-start | bytes 1769480 | tf_op jit(solution)/shard_map/ppermute | solution.py:417
  55.4 26.7 %collective-permute-start.5 = (bf16[192,2048]{1,0:T(8,128)(2,1)}, bf16[192,2048]{1,0:T(8,128)(2,1)S(1)}, u32[]{:S(2)}, u32[]{:S(2)}) collective-permute-start(bf16[192,2048]{1,0:T(8,128)(2,1)} %constant_dynamic-update-slice_fusion), channel_id=1, source_target_pairs={{0,12},{4,0},{8,4},{12,8},{1,13},{5,1},{9,5},{13,9},{2,14},{6,2},{... | collective-permute-start | bytes 2359304 | tf_op jit(solution)/shard_map/ppermute | solution.py:417
  56.7 25.7 %collective-permute-start.12 = (bf16[768,384]{1,0:T(8,128)(2,1)S(1)}, bf16[768,384]{1,0:T(8,128)(2,1)}, u32[]{:S(2)}, u32[]{:S(2)}) collective-permute-start(bf16[768,384]{1,0:T(8,128)(2,1)S(1)} %bitcast.48), channel_id=1, source_target_pairs={{0,64},{32,96},{64,0},{96,32},{1,65},{33,97},{65,1},{97,33},{2,66}... | collective-permute-start | bytes 1769480 | tf_op jit(solution)/shard_map/ppermute | solution.py:417
  66.6 32.9 %copy-start.13 = (f32[768]{0:T(1024)S(1)}, f32[768]{0:T(1024)}, u32[]{:S(2)}) copy-start(f32[768]{0:T(1024)} %param.16) | copy-start | bytes 9220
  66.6 32.8 %copy-start.14 = (f32[768]{0:T(1024)S(1)}, f32[768]{0:T(1024)}, u32[]{:S(2)}) copy-start(f32[768]{0:T(1024)} %param.17) | copy-start | bytes 9220
  66.6 11.2 %collective-permute-start.3 = (bf16[128,768]{1,0:T(8,128)(2,1)}, bf16[128,768]{1,0:T(8,128)(2,1)S(1)}, u32[]{:S(2)}, u32[]{:S(2)}) collective-permute-start(bf16[128,768]{1,0:T(8,128)(2,1)} %get-tuple-element.103), channel_id=1, source_target_pairs={{0,128},{128,0},{1,129},{129,1},{2,130},{130,2},{3,131},{131,3},{4... | collective-permute-start | bytes 589832 | tf_op jit(solution)/shard_map/ppermute | solution.py:412
  70.9 14.2 %collective-permute-start.13 = (bf16[768,384]{1,0:T(8,128)(2,1)S(1)}, bf16[768,384]{1,0:T(8,128)(2,1)S(1)}, u32[]{:S(2)}, u32[]{:S(2)}) collective-permute-start(bf16[768,384]{1,0:T(8,128)(2,1)S(1)} %bitcast.49), channel_id=1, source_target_pairs={{0,96},{32,0},{64,32},{96,64},{1,97},{33,1},{65,33},{97,65},{2,98}... | collective-permute-start | bytes 1769480 | tf_op jit(solution)/shard_map/ppermute | solution.py:417
  76.4 10.6 %collective-permute-start.14 = (bf16[768,384]{1,0:T(8,128)(2,1)S(1)}, bf16[768,384]{1,0:T(8,128)(2,1)S(1)}, u32[]{:S(2)}, u32[]{:S(2)}) collective-permute-start(bf16[768,384]{1,0:T(8,128)(2,1)S(1)} %bitcast.50), channel_id=1, source_target_pairs={{0,16},{16,0},{1,17},{17,1},{2,18},{18,2},{3,19},{19,3},{4,20},{20... | collective-permute-start | bytes 1769480 | tf_op jit(solution)/shard_map/ppermute | solution.py:412
  77.8 9.2 %collective-permute-start.15 = (bf16[768,384]{1,0:T(8,128)(2,1)S(1)}, bf16[768,384]{1,0:T(8,128)(2,1)S(1)}, u32[]{:S(2)}, u32[]{:S(2)}) collective-permute-start(bf16[768,384]{1,0:T(8,128)(2,1)S(1)} %collective-permute-done.11.refs_5_), channel_id=1, source_target_pairs={{0,16},{16,0},{1,17},{17,1},{2,18},{18,2},{3,19},{19,3},{4,20},{20... | collective-permute-start | bytes 1769480 | tf_op jit(solution)/shard_map/ppermute | solution.py:412
  82.1 12.2 %collective-permute-start.6 = (bf16[96,2048]{1,0:T(8,128)(2,1)S(1)}, bf16[96,2048]{1,0:T(8,128)(2,1)S(1)}, u32[]{:S(2)}, u32[]{:S(2)}) collective-permute-start(bf16[96,2048]{1,0:T(8,128)(2,1)S(1)} %slice.22), channel_id=1, source_target_pairs={{0,4},{4,8},{8,12},{12,0},{1,5},{5,9},{9,13},{13,1},{2,6},{6,10},{... | collective-permute-start | bytes 1179656 | tf_op jit(solution)/shard_map/ppermute | solution.py:417
  82.4 13.9 %collective-permute-start.7 = (bf16[96,2048]{1,0:T(8,128)(2,1)S(1)}, bf16[96,2048]{1,0:T(8,128)(2,1)S(1)}, u32[]{:S(2)}, u32[]{:S(2)}) collective-permute-start(bf16[96,2048]{1,0:T(8,128)(2,1)S(1)} %slice.23), channel_id=1, source_target_pairs={{0,12},{4,0},{8,4},{12,8},{1,13},{5,1},{9,5},{13,9},{2,14},{6,2},{... | collective-permute-start | bytes 1179656 | tf_op jit(solution)/shard_map/ppermute | solution.py:417
  85.1 14.5 %collective-permute-start.16 = (bf16[768,384]{1,0:T(8,128)(2,1)}, bf16[768,384]{1,0:T(8,128)(2,1)S(1)}, u32[]{:S(2)}, u32[]{:S(2)}) collective-permute-start(bf16[768,384]{1,0:T(8,128)(2,1)} %collective-permute-done.12.refs_6_), channel_id=1, source_target_pairs={{0,16},{16,0},{1,17},{17,1},{2,18},{18,2},{3,19},{19,3},{4,20},{20... | collective-permute-start | bytes 1769480 | tf_op jit(solution)/shard_map/ppermute | solution.py:412
  87.0 12.6 %collective-permute-start.17 = (bf16[768,384]{1,0:T(8,128)(2,1)S(1)}, bf16[768,384]{1,0:T(8,128)(2,1)S(1)}, u32[]{:S(2)}, u32[]{:S(2)}) collective-permute-start(bf16[768,384]{1,0:T(8,128)(2,1)S(1)} %collective-permute-done.13.refs_7_), channel_id=1, source_target_pairs={{0,16},{16,0},{1,17},{17,1},{2,18},{18,2},{3,19},{19,3},{4,20},{20... | collective-permute-start | bytes 1769480 | tf_op jit(solution)/shard_map/ppermute | solution.py:412
  87.0 12.6 %collective-permute-start.10 = (bf16[256,768]{1,0:T(8,128)(2,1)S(1)}, bf16[256,768]{1,0:T(8,128)(2,1)S(1)}, u32[]{:S(2)}, u32[]{:S(2)}) collective-permute-start(bf16[256,768]{1,0:T(8,128)(2,1)S(1)} %pad_maximum_fusion.refs_0_), channel_id=1, source_target_pairs={{0,96},{32,0},{64,32},{96,64},{1,97},{33,1},{65,33},{97,65},{2,98}... | collective-permute-start | bytes 1179656 | tf_op jit(solution)/shard_map/ppermute | solution.py:417
  94.3 0.7 copy-start.1
  95.0 11.1 %collective-permute-start.8 = (bf16[256,768]{1,0:T(8,128)(2,1)S(1)}, bf16[256,768]{1,0:T(8,128)(2,1)S(1)}, u32[]{:S(2)}, u32[]{:S(2)}) collective-permute-start(bf16[256,768]{1,0:T(8,128)(2,1)S(1)} %pad_maximum_fusion.refs_0_), channel_id=1, source_target_pairs={{0,32},{32,64},{64,96},{96,0},{1,33},{33,65},{65,97},{97,1},{2,34}... | collective-permute-start | bytes 1179656 | tf_op jit(solution)/shard_map/ppermute | solution.py:417
  96.3 0.7 copy-start.3
  97.0 18.5 %collective-permute-start.9 = (bf16[256,768]{1,0:T(8,128)(2,1)S(1)}, bf16[256,768]{1,0:T(8,128)(2,1)S(1)}, u32[]{:S(2)}, u32[]{:S(2)}) collective-permute-start(bf16[256,768]{1,0:T(8,128)(2,1)S(1)} %pad_maximum_fusion.refs_0_), channel_id=1, source_target_pairs={{0,64},{32,96},{64,0},{96,32},{1,65},{33,97},{65,1},{97,33},{2,66}... | collective-permute-start | bytes 1179656 | tf_op jit(solution)/shard_map/ppermute | solution.py:417
  132.2 5.1 %collective-permute-start.18 = (bf16[1024,768]{1,0:T(8,128)(2,1)}, bf16[1024,768]{1,0:T(8,128)(2,1)}, u32[]{:S(2)}, u32[]{:S(2)}) collective-permute-start(bf16[1024,768]{1,0:T(8,128)(2,1)} %shard_map.97.mine_ref), channel_id=1, source_target_pairs={{0,16},{16,0},{1,17},{17,1},{2,18},{18,2},{3,19},{19,3},{4,20},{20... | collective-permute-start | bytes 4718600 | tf_op jit(solution)/shard_map/ppermute | solution.py:412
  137.3 10.5 %copy-start.9 = (s32[2]{0:T(128)}, s32[2]{0:T(128)S(1)}, u32[]{:S(2)}) copy-start(s32[2]{0:T(128)S(1)} %broadcast.368.info_ref) | copy-start | bytes 28
  147.8 9.0 %copy-start.2 = (bf16[96,2048]{1,0:T(8,128)(2,1)S(1)}, bf16[96,2048]{1,0:T(8,128)(2,1)}, u32[]{:S(2)}) copy-start(bf16[96,2048]{1,0:T(8,128)(2,1)} %copy-done.1) | copy-start | bytes 1179652
  147.8 9.0 %copy-start.4 = (bf16[96,2048]{1,0:T(8,128)(2,1)S(1)}, bf16[96,2048]{1,0:T(8,128)(2,1)}, u32[]{:S(2)}) copy-start(bf16[96,2048]{1,0:T(8,128)(2,1)} %copy-done.3) | copy-start | bytes 1179652
  147.8 30.3 %all-to-all-start.4 = ((bf16[16,40,768]{2,1,0:T(8,128)(2,1)}), bf16[16,40,768]{2,1,0:T(8,128)(2,1)}, u32[]{:S(2)}, u32[]{:S(2)}) async-start(bf16[16,40,768]{2,1,0:T(8,128)(2,1)} %shard_map.98), calls=%async_computation.4 | async-start | bytes 1966080 | tf_op jit(solution)/shard_map/all_to_all | solution.py:403
  175.1 0.7 copy-start.5
  185.0 8.2 %copy-start.6 = (f32[128,768]{1,0:T(8,128)S(1)}, f32[128,768]{1,0:T(8,128)}, u32[]{:S(2)}) copy-start(f32[128,768]{1,0:T(8,128)} %copy-done.5) | copy-start | bytes 1179652
  185.0 17.9 %all-to-all-start.5 = ((f32[16,8,128]{2,1,0:T(8,128)}), f32[16,8,128]{2,1,0:T(8,128)S(1)}, u32[]{:S(2)}, u32[]{:S(2)}) async-start(f32[16,8,128]{2,1,0:T(8,128)} %bitcast.25), calls=%async_computation.5 | async-start | bytes 131072 | tf_op jit(solution)/shard_map/all_to_all | solution.py:403

commit v3 on v2

--- a/solution.py
+++ b/solution.py
@@ -18,6 +18,9 @@
 ROOM = 48
 F32 = jnp.float32
 BF16 = jnp.bfloat16
+
+
+RING = ((0, 0, 2), (1, 0, 2), (2, 0, 1), (2, 1, 1), (3, 0, 2))
 
 
 def iota(shape, dim):
@@ -141,18 +144,19 @@
 
 def encode_kernel(info_ref, *refs):
     x_size = 4
-    x_parts, w_parts = refs[0:x_size], refs[x_size : 3 * x_size]
-    gain_ref, bias_ref, out_ref = refs[3 * x_size : 3 * x_size + 3]
-    x_ref, w_ref, packed_ref, scores_ref, probs_ref, context_ref, sems = refs[3 * x_size + 3 :]
+    x_parts, w_parts = refs[0 : 2 * x_size], refs[2 * x_size : 2 * x_size + 10]
+    gain_ref, bias_ref, out_ref = refs[2 * x_size + 10 : 2 * x_size + 13]
+    x_ref, w_ref, packed_ref, scores_ref, probs_ref, context_ref, sems = refs[2 * x_size + 13 :]
     core, at_x = info_ref[0], info_ref[1]
-    places = [
-        half * x_size + lax.rem(at_x - k + x_size, x_size)
-        for half in (core, 1 - core)
-        for k in range(x_size)
-    ]
+    depth = w_ref.shape[1]
+    places = []
+    for side in (core, 1 - core):
+        for back, first, count in RING:
+            place = side * x_size + lax.rem(at_x - back + x_size, x_size)
+            places.append(w_ref.at[place, pl.ds(first * (depth // 2), count * (depth // 2)), :])
     put(
         x_parts + w_parts,
-        [x_ref.at[k] for k in range(x_size)] + [w_ref.at[p] for p in places],
+        [x_ref.at[k, pl.ds(z * SEQ, SEQ), :] for z in range(2) for k in range(x_size)] + places,
         sems,
     )
     part = w_ref.shape[2]
@@ -210,20 +214,21 @@
 
 
 def encoded(info, x_parts, w_parts, gain, bias):
-    tokens, width = x_parts[0].shape
-    part = w_parts[0].shape[1]
+    tokens, width = 2 * SEQ, x_parts[0].shape[1]
+    chunks = len(x_parts) // 2
+    depth, part = w_parts[0].shape
     count = len(x_parts) + len(w_parts)
     pairs = tokens // SEQ * HEADS // 2
     return pl.pallas_call(
         encode_kernel,
-        out_shape=jax.ShapeDtypeStruct((len(x_parts) * tokens, width), BF16),
+        out_shape=jax.ShapeDtypeStruct((chunks * tokens, width), BF16),
         in_specs=[pl.BlockSpec(memory_space=pltpu.SMEM)]
         + [pl.BlockSpec(memory_space=pl.ANY)] * count
         + [pl.BlockSpec(memory_space=pltpu.VMEM)] * 2,
         out_specs=pl.BlockSpec(memory_space=pltpu.VMEM),
         scratch_shapes=[
-            pltpu.VMEM((len(x_parts), tokens, width), BF16),
-            pltpu.VMEM((len(w_parts), width, part), BF16),
+            pltpu.VMEM((chunks, tokens, width), BF16),
+            pltpu.VMEM((chunks * 2, depth, part), BF16),
             pltpu.VMEM((tokens, 3 * width), BF16),
             pltpu.VMEM((pairs, SEQ, 2 * SEQ), F32),
             pltpu.VMEM((pairs, SEQ, 2 * SEQ), BF16),
@@ -235,24 +240,22 @@
 
 
 def score_kernel(info_ref, mine_ref, other_ref, local_ref, *refs):
-    own, (back_ref, low_ref, high_ref, ahead_ref) = refs[0:4], refs[4:8]
-    out_ref, old_ref, cent_ref, sems = refs[8:]
+    parts = refs[0:5]
+    out_ref, old_ref, cent_ref, sems = refs[5:]
+    quarters = 4
     step = pl.program_id(0)
-    shard = own[0].shape[0]
 
     @pl.when(step == 0)
     def _():
-        at_y, at_zl = info_ref[0], info_ref[1]
-        targets = []
-        for back in range(4):
-            for k in range(4):
-                place = 4 * lax.rem(at_y - back + 4, 4) + lax.rem(at_zl - k + 4, 4)
+        shard = parts[0].shape[0] // quarters
+        sources, targets = [], []
+        for ref, (back, first, count) in zip(parts, RING, strict=True):
+            owner = lax.rem(info_ref[0] - back + 4, 4) * quarters
+            for k in range(2 * count):
+                place = owner + lax.rem(info_ref[2] - 2 * first - k + quarters, quarters)
+                sources.append(ref.at[pl.ds(k * shard, shard), :])
                 targets.append(cent_ref.at[pl.ds(pl.multiple_of(place * shard, shard), shard), :])
-        far = [low_ref] * 2 + [high_ref] * 2
-        spots = [(back_ref, k) for k in range(4)]
-        spots += [(ref, k % 2) for k, ref in enumerate(far)]
-        spots += [(ahead_ref, k) for k in range(4)]
-        put(list(own) + [ref.at[pl.ds(k * shard, shard), :] for ref, k in spots], targets, sems)
+        put(sources, targets, sems)
 
     rows = mine_ref.shape[0]
     block = cent_ref.shape[1]
@@ -272,7 +275,7 @@
     @pl.when(step == pl.num_programs(0) - 1)
     def _():
         per = old_ref.shape[0]
-        old = cent_ref[:, pl.ds(pl.multiple_of(info_ref[2] * per, per), per)]
+        old = cent_ref[:, pl.ds(pl.multiple_of(info_ref[1] * per, per), per)]
         old_ref[...] = old.astype(F32).T
 
 
@@ -308,10 +311,10 @@
     )(info, mine, other, local.reshape(2 * tokens // SEQ, 1, SEQ), *parts)
 
 
-def pack_kernel(info_ref, local_ref, mine_ref, other_ref, out_ref, hits_ref):
-    dests, _, width = out_ref.shape
+def choose_kernel(info_ref, local_ref, out_ref, most_ref):
+    tokens = local_ref.shape[1]
     per = 128
-    tokens = local_ref.shape[1]
+    dests = out_ref.shape[0] // ROOM
     first_slot = info_ref[1] * SLOTS
     local = local_ref[...]
     upper = iota((per, per), 0) < iota((per, per), 1)
@@ -326,29 +329,45 @@
         slot = iota((ROOM, per), 0)
         chosen = (slot < SLOTS) & (slot == rank - first_slot) & (here > 0.5)
         packing = jnp.where(chosen, 1.0, 0.0).astype(BF16)
-        hits_ref[pl.ds(pl.multiple_of(g * ROOM, ROOM), ROOM), :] = dot(packing, hits).astype(BF16)
+        out_ref[pl.ds(pl.multiple_of(g * ROOM, ROOM), ROOM), :] = dot(packing, hits).astype(BF16)
         return jnp.maximum(most, jnp.sum(here, axis=1, keepdims=True))
 
     most = lax.fori_loop(0, dests, group, jnp.zeros((1, 1), F32), unroll=4)
-    half = tokens // 2
+    most_ref[...] = jnp.broadcast_to(most, most_ref.shape)
+
+
+def choices(info, local, dests):
+    return pl.pallas_call(
+        choose_kernel,
+        out_shape=(
+            jax.ShapeDtypeStruct((dests * ROOM, local.shape[1]), BF16),
+            jax.ShapeDtypeStruct((8, 128), F32),
+        ),
+        in_specs=[pl.BlockSpec(memory_space=pltpu.SMEM), pl.BlockSpec(memory_space=pltpu.VMEM)],
+        out_specs=(pl.BlockSpec(memory_space=pltpu.VMEM), pl.BlockSpec(memory_space=pltpu.VMEM)),
+        compiler_params=pltpu.CompilerParams(vmem_limit_bytes=40 << 20),
+    )(info, local)
+
+
+def pack_kernel(hits_ref, most_ref, mine_ref, other_ref, out_ref):
+    dests, _, width = out_ref.shape
+    half = mine_ref.shape[0]
     sums = dot(hits_ref[:, 0:half], mine_ref[...]) + dot(hits_ref[:, half:], other_ref[...])
     sums = sums.reshape(dests, ROOM, width)[:, 0:BLOCK, :]
     last = iota((dests, BLOCK, width), 1) == SLOTS
-    out_ref[...] = jnp.where(last, most.reshape(1, 1, 1), sums).astype(BF16)
-
-
-def packed_sums(info, local, mine, other, dests):
-    tokens = local.shape[1]
+    out_ref[...] = jnp.where(last, most_ref[0:1, 0:1].reshape(1, 1, 1), sums).astype(BF16)
+
+
+def packed_sums(chosen, mine, other):
+    hits, most = chosen
     width = mine.shape[1]
     return pl.pallas_call(
         pack_kernel,
-        out_shape=jax.ShapeDtypeStruct((dests, BLOCK, width), BF16),
-        in_specs=[pl.BlockSpec(memory_space=pltpu.SMEM)]
-        + [pl.BlockSpec(memory_space=pltpu.VMEM)] * 3,
+        out_shape=jax.ShapeDtypeStruct((hits.shape[0] // ROOM, BLOCK, width), BF16),
+        in_specs=[pl.BlockSpec(memory_space=pltpu.VMEM)] * 4,
         out_specs=pl.BlockSpec(memory_space=pltpu.VMEM),
-        scratch_shapes=[pltpu.VMEM((dests * ROOM, tokens), BF16)],
-        compiler_params=pltpu.CompilerParams(vmem_limit_bytes=48 << 20),
-    )(info, local, mine, other)
+        compiler_params=pltpu.CompilerParams(vmem_limit_bytes=40 << 20),
+    )(hits, most, mine, other)
 
 
 def count_kernel(info_ref, assign_ref, out_ref):
@@ -417,6 +436,15 @@
     return lax.ppermute(shard, axis, [(i, (i + by) % devices) for i in range(devices)])
 
 
+def neighbours(block, axis):
+    return turned(block, axis, 1), turned(block, axis, lax.axis_size(axis) - 1)
+
+
+def far_halves(back, ahead, axis):
+    half = back.shape[0] // 2
+    return turned(back[:half], axis, 1), turned(ahead[half:], axis, lax.axis_size(axis) - 1)
+
+
 def backwards(values, here):
     for dim, at in enumerate(here):
         size = values.shape[dim]
@@ -437,51 +465,8 @@
 
     at_x = lax.axis_index("x")
 
-    rows = [centroids_t] + [turned(centroids_t, "zl", k) for k in range(1, 4)]
-
-    part = (w_qkv.shape[1] + w_out.shape[1]) // (2 * x_size)
-    both = jnp.concatenate([w_qkv, w_out], axis=1)
-    piece = lax.dynamic_slice_in_dim(both, (core * x_size + at_x) * part, part, 1)
-    column = gathered(piece, FS).reshape(width, part)
-
     def info_of(*values):
         return jnp.stack(values).astype(jnp.int32)
-
-    my_row = lax.dynamic_slice_in_dim(ids, fs_rank, 1, 0)
-    vocab_arr = jnp.full((1,), vocab, jnp.int32)
-    sent, most = listed_rows(info_of(fs_rank, zero), ids, embed_table)
-    sent, column, *rows = lax.optimization_barrier((sent, column, *rows))
-    mine_w = [column] + [turned(column, "x", k) for k in range(1, x_size)]
-    got = exchanged(sent, FS)
-    inputs = expanded(info_of(fs_rank, zero), my_row, vocab_arr, got)
-
-    def more_rows(state):
-        turn, acc = state
-        info = info_of(fs_rank, turn)
-        again, _ = listed_rows(info, ids, embed_table)
-        return turn + 1, acc + expanded(info, my_row, vocab_arr, exchanged(again, FS))
-
-    most = most[0, 0]
-    _, inputs = lax.while_loop(
-        lambda state: state[0] * LIST < most, more_rows, (jnp.int32(1), inputs)
-    )
-
-    two = jnp.concatenate([inputs, swapped(inputs, "zh")], axis=0)
-    other_w = [swapped(w, "core") for w in mine_w]
-
-    near = jnp.concatenate(rows, axis=0)
-    back = turned(near, "y", 1)
-    ahead = turned(near, "y", 3)
-    two, back, ahead = lax.optimization_barrier((two, back, ahead))
-    pieces = [two] + [turned(two, "x", k) for k in range(1, x_size)]
-    half = near.shape[0] // 2
-    far_low = turned(back[:half], "y", 1)
-    far_high = turned(ahead[half:], "y", 3)
-    two, far_low, far_high = lax.optimization_barrier((two, far_low, far_high))
-    pieces[0] = two
-
-    mine = encoded(info_of(core, at_x), pieces, mine_w + other_w, ln_gain, ln_bias)
-    other = swapped(mine, "core")
 
     by_dev = assignments.reshape(2, x_size, 2, fs_size, SEQ)
     of_slab = lax.dynamic_index_in_dim(by_dev, fs_rank, 3, keepdims=False)
@@ -490,26 +475,73 @@
     of_slab = backwards(of_slab, here)
     block = centroids_t.shape[1]
     local = of_slab.reshape(1, -1) - dp_rank * block
-
+    chosen = choices(info_of(zero, zero), local, fs_size)
     counts = counted(
         info_of(dp_rank * block + fs_rank * (block // fs_size)),
         assignments.reshape(dp_size, fs_size, SEQ),
     )
 
+    part = (w_qkv.shape[1] + w_out.shape[1]) // (2 * x_size)
+    both = jnp.concatenate([w_qkv, w_out], axis=1)
+    piece = lax.dynamic_slice_in_dim(both, (core * x_size + at_x) * part, part, 1)
+    column = gathered(piece, FS).reshape(width, part)
+
+    my_row = lax.dynamic_slice_in_dim(ids, fs_rank, 1, 0)
+    vocab_arr = jnp.full((1,), vocab, jnp.int32)
+    sent, most = listed_rows(info_of(fs_rank, zero), ids, embed_table)
+    sent, column = lax.optimization_barrier((sent, column))
+    w_back, w_ahead = neighbours(column, "x")
+
+    sent, start = lax.optimization_barrier((sent, centroids_t))
+    rows = [start] + [turned(start, "zl", k) for k in range(1, 4)]
+
+    got = exchanged(sent, FS)
+    got, chosen = lax.optimization_barrier((got, chosen))
+    inputs = expanded(info_of(fs_rank, zero), my_row, vocab_arr, got)
+
+    def more_rows(state):
+        turn, acc = state
+        info = info_of(fs_rank, turn)
+        again, _ = listed_rows(info, ids, embed_table)
+        return turn + 1, acc + expanded(info, my_row, vocab_arr, exchanged(again, FS))
+
+    most = most[0, 0]
+    _, inputs = lax.while_loop(
+        lambda state: state[0] * LIST < most, more_rows, (jnp.int32(1), inputs)
+    )
+
+    inputs, w_back, w_ahead, *rows = lax.optimization_barrier((inputs, w_back, w_ahead, *rows))
+    far = swapped(inputs, "zh")
+    pieces = [inputs] + [turned(inputs, "x", k) for k in range(1, x_size)]
+    mine_w = [column, w_back, *far_halves(w_back, w_ahead, "x"), w_ahead]
+    other_w = [swapped(w, "core") for w in mine_w]
+
+    near = jnp.concatenate(rows, axis=0)
+    back, ahead = neighbours(near, "y")
+    far, counts = lax.optimization_barrier((far, counts))
+    pieces += [far] + [turned(far, "x", k) for k in range(1, x_size)]
+    pieces[0], back, ahead = lax.optimization_barrier((inputs, back, ahead))
+    far_low, far_high = far_halves(back, ahead, "y")
+
+    mine = encoded(info_of(core, at_x), pieces, mine_w + other_w, ln_gain, ln_bias)
+    mine, far_low, far_high = lax.optimization_barrier((mine, far_low, far_high))
+    other = swapped(mine, "core")
+
     def one_turn(turn):
         info = info_of(zero, turn)
-        got = exchanged(packed_sums(info, local, mine, other, fs_size), FS)
+        got = exchanged(packed_sums(choices(info, local, fs_size), mine, other), FS)
         return unpacked_sums(info, counts, got)
 
-    packed = packed_sums(info_of(zero, zero), local, mine, other, fs_size)
+    packed = packed_sums(chosen, mine, other)
     packed, mine, other = lax.optimization_barrier((packed, mine, other))
     got = exchanged(packed, FS)
+
     stats, previous = scored(
-        info_of(lax.axis_index("y"), lax.axis_index("zl"), fs_rank),
+        info_of(lax.axis_index("y"), fs_rank, lax.axis_index("zl")),
         mine,
         other,
         local,
-        rows + [back, far_low, far_high, ahead],
+        [near, back, far_low, far_high, ahead],
     )
     stats, got = lax.optimization_barrier((stats, got))
     stats = backwards(stats.reshape(2, x_size, 2, 8, SEQ), here)

time: 204 us -> 203 us (level)
  local copies, waits for them, and re-layouts: 10.8 us -> 28.8 us
  waiting for transfers between devices: 57.8 us -> 43.3 us
  Pallas kernels: 58.9 us -> 55.9 us
  starting transfers between devices: 67.6 us -> 64.9 us
    ppermute x13 -> x17, waiting for transfers between devices: 40.6 us -> 8.55 us  [turned(): lax.ppermute(shard, axis, [(i, (i + by) % devices) for i in range(devices)])]
    all_to_all x4, waiting for transfers between devices: 15.9 us -> 29.2 us  [exchanged(): return lax.all_to_all(blocks, axis, 0, 0, tiled=True)]
    unnamed x27 -> x61, local copies, waits for them, and re-layouts: 4.35 us -> 13.5 us
    ppermute x6 -> x7, starting transfers between devices: 11.8 us -> 17.9 us  [swapped(): return lax.ppermute(shard, axis, [(0, 1), (1, 0)])]
    slice x2 -> x4, local copies, waits for them, and re-layouts: 0.05 us -> 5.44 us  [the longest x2 2.72 us: far_halves(): back[:half]]
    ppermute x13 -> x17, starting transfers between devices: 23.8 us -> 19.3 us  [turned(): lax.ppermute(shard, axis, [(i, (i + by) % devices) for i in range(devices)])]
    ppermute x6 -> x7, waiting for transfers between devices: 1.3 us -> 5.6 us  [swapped(): return lax.ppermute(shard, axis, [(0, 1), (1, 0)])]
    all_to_all x4, starting transfers between devices: 32.1 us -> 27.8 us  [exchanged(): return lax.all_to_all(blocks, axis, 0, 0, tiled=True)]
  transfers between devices with their start and end apart: 23 -> 28, of which waited for: 11 -> 11; matrix products, arithmetic and copies ran while one was open for 4% -> 9% of each run, Pallas kernels for 14% -> 25%
where the time goes in v3:
time: 203 us; the launch traced here: 202 us
  starting transfers between devices  64.9 us (32%)
  Pallas kernels  55.9 us (28%)
  waiting for transfers between devices  43.3 us (21%)
  local copies, waits for them, and re-layouts  28.8 us (14%)
  other arithmetic  6.05 us (3%)
    all_to_all x4, waiting for transfers between devices, exchanged(): return lax.all_to_all(blocks, axis, 0, 0, tiled=True)  29.2 us
    all_to_all x4, starting transfers between devices, exchanged(): return lax.all_to_all(blocks, axis, 0, 0, tiled=True)  27.8 us
    ppermute x17, starting transfers between devices, turned(): lax.ppermute(shard, axis, [(i, (i + by) % devices) for i in range(devices)])  19.3 us
    ppermute x7, starting transfers between devices, swapped(): return lax.ppermute(shard, axis, [(0, 1), (1, 0)])  17.9 us
    pallas_call x1, Pallas kernels, encoded(): pl.pallas_call(encode_kernel, out_shape=jax.ShapeDtypeStruct((chunks * to...  16.5 us
    pallas_call x1, Pallas kernels, scored(): pl.pallas_call(score_kernel, grid=(2 * half,), out_shape=(jax.ShapeDtypeS...  15.8 us
    unnamed x61, local copies, waits for them, and re-layouts  13.5 us
    ppermute x17, waiting for transfers between devices, turned(): lax.ppermute(shard, axis, [(i, (i + by) % devices) for i in range(devices)])  8.55 us
  transfers between devices with their start and end apart: 28, of which 11 were waited for; matrix products, arithmetic and copies ran while one was open for 9% of the time, Pallas kernels for 25%

profile of v3, /device:TPU:1, one launch (start us, length us, event | category | flops | bytes accessed | tf_op | source)
XLA Modules:
  0.0 201.6 jit_solution(3001760279900224110)
XLA Ops:
  0.6 0.8 fusion
  1.4 0.9 broadcast_in_dim.79
  2.3 9.2 %all-to-all-start.2 = ((bf16[16,48,384]{2,1,0:T(8,128)(2,1)}), bf16[16,48,384]{2,1,0:T(8,128)(2,1)}, u32[]{:S(2)}, u32[]{:S(2)}) async-start(bf16[16,48,384]{2,1,0:T(8,128)(2,1)} %broadcast_in_dim.79), calls=%async_computation.2 | async-start | bytes 1179648 | tf_op jit(solution)/shard_map/all_to_all | solution.py:422
  11.6 0.9 constant_dynamic-slice_fusion.1
  13.9 5.3 %shard_map.95 = (bf16[16,16,768]{2,1,0:T(8,128)(2,1)}, s32[8,128]{1,0:T(8,128)S(1)}) custom-call(s32[2]{0:T(128)S(1)} %pad_add_fusion.3.info_ref, s32[16,128]{1,0:T(8,128)} %bitcast.50, bf16[1908,768]{1,0:T(8,128)(2,1)} %table_ref.1), custom_call_target="tpu_custom_call" | custom-call | tf_op jit(solution)/shard_map/pallas_call | solution.py:77
  19.1 9.6 %all-to-all-done.2 = bf16[16,48,384]{2,1,0:T(8,128)(2,1)} async-done(((bf16[16,48,384]{2,1,0:T(8,128)(2,1)}), bf16[16,48,384]{2,1,0:T(8,128)(2,1)}, u32[]{:S(2)}, u32[]{:S(2)}) %all-to-all-start.2) | async-done | bytes 589856 | tf_op jit(solution)/shard_map/all_to_all | solution.py:422
  28.7 4.0 %all-to-all-start.3 = ((bf16[16,16,768]{2,1,0:T(8,128)(2,1)}), bf16[16,16,768]{2,1,0:T(8,128)(2,1)S(1)}, u32[]{:S(2)}, u32[]{:S(2)}) async-start(bf16[16,16,768]{2,1,0:T(8,128)(2,1)} %get-tuple-element.116), calls=%async_computation.3 | async-start | bytes 786432 | tf_op jit(solution)/shard_map/all_to_all | solution.py:422
  32.7 1.3 collective-permute-start
  34.0 1.5 collective-permute-start.1
  36.2 1.4 collective-permute-start.2
  37.6 2.1 %collective-permute-start.3 = (bf16[48,2048]{1,0:T(8,128)(2,1)}, bf16[48,2048]{1,0:T(8,128)(2,1)}, u32[]{:S(2)}, u32[]{:S(2)}) collective-permute-start(bf16[48,2048]{1,0:T(8,128)(2,1)} %param.18), channel_id=1, source_target_pairs={{0,2},{1,3},{2,0},{3,1},{4,6},{5,7},{6,4},{7,5},{8,10},{9,11},{10,... | collective-permute-start | bytes 589832 | tf_op jit(solution)/shard_map/ppermute | solution.py:436
  39.7 1.2 collective-permute-start.4
  42.1 5.7 %shard_map.96 = (bf16[768,2048]{1,0:T(8,128)(2,1)S(1)}, f32[8,128]{1,0:T(8,128)S(1)}) custom-call(s32[2]{0:T(128)S(1)} %broadcast.368.info_ref, s32[1,2048]{1,0:T(1,128)} %bitcast.48), custom_call_target="tpu_custom_call" | custom-call | tf_op jit(solution)/shard_map/pallas_call | solution.py:340
  47.9 0.7 constant_dynamic-slice_fusion.row_ref
  48.6 3.8 %all-to-all-done.3.got_ref = bf16[16,16,768]{2,1,0:T(8,128)(2,1)S(1)} async-done(((bf16[16,16,768]{2,1,0:T(8,128)(2,1)}), bf16[16,16,768]{2,1,0:T(8,128)(2,1)S(1)}, u32[]{:S(2)}, u32[]{:S(2)}) %all-to-all-start.3) | async-done | bytes 393248 | tf_op jit(solution)/shard_map/all_to_all | solution.py:422
  52.3 0.7 copy-done.18
  53.1 2.1 %shard_map.97 = bf16[128,768]{1,0:T(8,128)(2,1)} custom-call(s32[2]{0:T(128)} %copy-done.12, s32[1,128]{1,0:T(1,128)S(1)} %constant_dynamic-slice_fusion.row_ref, s32[1]{0:T(128)} %constant.181.clone.1.vocab_ref, bf16[16,16,768]{2,1,0:T(8,128)(2,1)} %copy-done.18), custom_call_target="tpu_custom_call" | custom-call | tf_op jit(solution)/shard_map/pallas_call | solution.py:121
  55.2 4.5 %collective-permute-start.16 = (bf16[768,384]{1,0:T(8,128)(2,1)}, bf16[768,384]{1,0:T(8,128)(2,1)}, u32[]{:S(2)}, u32[]{:S(2)}) collective-permute-start(bf16[768,384]{1,0:T(8,128)(2,1)} %bitcast.7.refs_8_), channel_id=1, source_target_pairs={{0,16},{16,0},{1,17},{17,1},{2,18},{18,2},{3,19},{19,3},{4,20},{20... | collective-permute-start | bytes 1769480 | tf_op jit(solution)/shard_map/ppermute | solution.py:431
  60.4 1.6 constant_dynamic-update-slice_fusion.3
  62.0 1.6 constant_dynamic-update-slice_fusion.2
  63.6 1.6 constant_dynamic-update-slice_fusion.1
  65.2 1.6 constant_dynamic-update-slice_fusion.refs_0_
  66.9 2.7 %collective-permute-start.6 = (bf16[192,2048]{1,0:T(8,128)(2,1)}, bf16[192,2048]{1,0:T(8,128)(2,1)}, u32[]{:S(2)}, u32[]{:S(2)}) collective-permute-start(bf16[192,2048]{1,0:T(8,128)(2,1)} %constant_dynamic-update-slice_fusion.refs_0_), channel_id=1, source_target_pairs={{0,12},{4,0},{8,4},{12,8},{1,13},{5,1},{9,5},{13,9},{2,14},{6,2},{... | collective-permute-start | bytes 2359304 | tf_op jit(solution)/shard_map/ppermute | solution.py:436
  69.6 1.2 collective-permute-start.7
  70.8 2.5 %collective-permute-start.8 = (bf16[128,768]{1,0:T(8,128)(2,1)}, bf16[128,768]{1,0:T(8,128)(2,1)S(1)}, u32[]{:S(2)}, u32[]{:S(2)}) collective-permute-start(bf16[128,768]{1,0:T(8,128)(2,1)} %get-tuple-element.131.refs_0_), channel_id=1, source_target_pairs={{0,64},{32,96},{64,0},{96,32},{1,65},{33,97},{65,1},{97,33},{2,66}... | collective-permute-start | bytes 589832 | tf_op jit(solution)/shard_map/ppermute | solution.py:436
  73.2 4.2 %collective-permute-start.10 = (bf16[128,768]{1,0:T(8,128)(2,1)}, bf16[128,768]{1,0:T(8,128)(2,1)}, u32[]{:S(2)}, u32[]{:S(2)}) collective-permute-start(bf16[128,768]{1,0:T(8,128)(2,1)} %get-tuple-element.131.refs_0_), channel_id=1, source_target_pairs={{0,128},{128,0},{1,129},{129,1},{2,130},{130,2},{3,131},{131,3},{4... | collective-permute-start | bytes 589832 | tf_op jit(solution)/shard_map/ppermute | solution.py:431
  78.1 1.2 collective-permute-start.9
  79.3 1.7 slice.28
  81.0 1.7 slice.29
  82.7 0.7 copy-done.6
  83.7 1.2 collective-permute-done.10.refs_4_
  84.9 1.1 collective-permute-start.15
  86.1 4.5 %shard_map.98.counts_ref = f32[128,128]{1,0:T(8,128)} custom-call(s32[1]{0:T(128)} %bitcast.20.info_ref, s32[16,16,128]{2,1,0:T(8,128)} %bitcast.54), custom_call_target="tpu_custom_call" | custom-call | tf_op jit(solution)/shard_map/pallas_call | solution.py:388
  91.1 3.2 %collective-permute-start.17 = (bf16[768,384]{1,0:T(8,128)(2,1)}, bf16[768,384]{1,0:T(8,128)(2,1)S(1)}, u32[]{:S(2)}, u32[]{:S(2)}) collective-permute-start(bf16[768,384]{1,0:T(8,128)(2,1)} %collective-permute-done.refs_9_), channel_id=1, source_target_pairs={{0,16},{16,0},{1,17},{17,1},{2,18},{18,2},{3,19},{19,3},{4,20},{20... | collective-permute-start | bytes 1769480 | tf_op jit(solution)/shard_map/ppermute | solution.py:431
  94.6 1.9 collective-permute-done.11.refs_5_
  96.5 4.0 %collective-permute-start.20 = (bf16[768,384]{1,0:T(8,128)(2,1)}, bf16[768,384]{1,0:T(8,128)(2,1)S(1)}, u32[]{:S(2)}, u32[]{:S(2)}) collective-permute-start(bf16[768,384]{1,0:T(8,128)(2,1)} %collective-permute-done.1.refs_12_), channel_id=1, source_target_pairs={{0,16},{16,0},{1,17},{17,1},{2,18},{18,2},{3,19},{19,3},{4,20},{20... | collective-permute-start | bytes 1769480 | tf_op jit(solution)/shard_map/ppermute | solution.py:431
  100.5 1.1 collective-permute-start.13
  101.6 1.0 slice.30
  102.6 1.0 slice.31
  103.6 5.1 %collective-permute-done.12.refs_6_ = bf16[128,768]{1,0:T(8,128)(2,1)S(1)} collective-permute-done((bf16[128,768]{1,0:T(8,128)(2,1)}, bf16[128,768]{1,0:T(8,128)(2,1)S(1)}, u32[]{:S(2)}, u32[]{:S(2)}) %collective-permute-start.12) | collective-permute-done | bytes 196640 | tf_op jit(solution)/shard_map/ppermute | solution.py:436
  108.7 1.2 collective-permute-done.13.refs_7_
  110.0 1.4 collective-permute-start.22
  111.4 1.3 collective-permute-start.19
  112.9 1.3 collective-permute-done.19.refs_16_
  114.2 1.0 copy-done.3
  115.2 0.9 copy-done.5
  116.1 0.9 copy-done.7
  117.0 16.5 %shard_map.99.mine_ref = bf16[1024,768]{1,0:T(8,128)(2,1)S(1)} custom-call(s32[2]{0:T(128)S(1)} %pad_add_fusion.4.info_ref, bf16[128,768]{1,0:T(8,128)(2,1)} %get-tuple-element.131.refs_0_, bf16[128,768]{1,0:T(8,128)(2,1)S(1)} %copy-done.5, bf16[128,768]{1,0:T(8,128)(2,1)S(1)} %copy-done.7, bf16[128,768]{1,0:T(8,128)(2,1)} %collective-permute-done.9.refs_3_, ...), custom_call_target="tpu_custom_call" | custom-call | tf_op jit(solution)/shard_map/pallas_call | solution.py:222
  133.6 0.8 copy-done
  134.8 3.0 %collective-permute-done.23.other_ref = bf16[1024,768]{1,0:T(8,128)(2,1)S(1)} collective-permute-done((bf16[1024,768]{1,0:T(8,128)(2,1)S(1)}, bf16[1024,768]{1,0:T(8,128)(2,1)S(1)}, u32[]{:S(2)}, u32[]{:S(2)}) %collective-permute-start.23) | collective-permute-done | bytes 1572896 | tf_op jit(solution)/shard_map/ppermute | solution.py:431
  137.9 1.1 copy-done.15
  139.0 3.6 %shard_map.100 = bf16[16,40,768]{2,1,0:T(8,128)(2,1)} custom-call(bf16[768,2048]{1,0:T(8,128)(2,1)S(1)} %get-tuple-element.119.hits_ref, f32[8,128]{1,0:T(8,128)S(1)} %get-tuple-element.120.most_ref, bf16[1024,768]{1,0:T(8,128)(2,1)S(1)} %shard_map.99.mine_ref, bf16[1024,768]{1,0:T(8,128)(2,1)S(1)} %collective-permute-done.23.other_ref), custom_call_target="tpu_custom_call" | custom-call | tf_op jit(solution)/shard_map/pallas_call | solution.py:364
  142.6 5.1 %all-to-all-start.4 = ((bf16[16,40,768]{2,1,0:T(8,128)(2,1)}), bf16[16,40,768]{2,1,0:T(8,128)(2,1)}, u32[]{:S(2)}, u32[]{:S(2)}) async-start(bf16[16,40,768]{2,1,0:T(8,128)(2,1)} %shard_map.100), calls=%async_computation.4 | async-start | bytes 1966080 | tf_op jit(solution)/shard_map/all_to_all | solution.py:422
  148.0 0.9 slice_reduce_fusion
  149.0 1.0 copy-done.1
  150.0 15.8 %shard_map.101 = (f32[16,8,128]{2,1,0:T(8,128)S(1)}, f32[128,768]{1,0:T(8,128)S(1)}) custom-call(s32[3]{0:T(128)S(1)} %pad_add_fusion.2.info_ref, bf16[1024,768]{1,0:T(8,128)(2,1)} %copy-done.13, bf16[1024,768]{1,0:T(8,128)(2,1)} %copy-done.15, s32[16,1,128]{2,1,0:T(1,128)S(1)} %fusion.2.local_ref, ...), custom_call_target="tpu_custom_call" | custom-call | tf_op jit(solution)/shard_map/pallas_call | solution.py:288
  166.5 6.9 %all-to-all-done.4.got_ref = bf16[16,40,768]{2,1,0:T(8,128)(2,1)} async-done(((bf16[16,40,768]{2,1,0:T(8,128)(2,1)}), bf16[16,40,768]{2,1,0:T(8,128)(2,1)}, u32[]{:S(2)}, u32[]{:S(2)}) %all-to-all-start.4) | async-done | bytes 983072 | tf_op jit(solution)/shard_map/all_to_all | solution.py:422
  173.4 2.3 %shard_map.102 = f32[128,768]{1,0:T(8,128)S(1)} custom-call(s32[2]{0:T(128)} %copy-done.11, f32[128,128]{1,0:T(8,128)S(1)} %copy-done.17, bf16[16,40,768]{2,1,0:T(8,128)(2,1)} %all-to-all-done.4.got_ref), custom_call_target="tpu_custom_call" | custom-call | tf_op jit(solution)/shard_map/pallas_call | solution.py:412
  175.7 1.4 slice_reduce_fusion.2
  177.1 1.5 gather_fusion.3
  180.1 0.7 broadcast_select_fusion
  181.8 9.5 %all-to-all-start.5 = ((f32[16,8,128]{2,1,0:T(8,128)}), f32[16,8,128]{2,1,0:T(8,128)S(1)}, u32[]{:S(2)}, u32[]{:S(2)}) async-start(f32[16,8,128]{2,1,0:T(8,128)} %bitcast.27), calls=%async_computation.5 | async-start | bytes 131072 | tf_op jit(solution)/shard_map/all_to_all | solution.py:422
  191.3 0.9 divide_select_fusion
  192.2 8.9 %all-to-all-done.5 = f32[16,8,128]{2,1,0:T(8,128)S(1)} async-done(((f32[16,8,128]{2,1,0:T(8,128)}), f32[16,8,128]{2,1,0:T(8,128)S(1)}, u32[]{:S(2)}, u32[]{:S(2)}) %all-to-all-start.5) | async-done | bytes 65568 | tf_op jit(solution)/shard_map/all_to_all | solution.py:422
  (114 shorter events, 9.5 us)
Async XLA Ops:
  2.3 26.4 %all-to-all-start.2 = ((bf16[16,48,384]{2,1,0:T(8,128)(2,1)}), bf16[16,48,384]{2,1,0:T(8,128)(2,1)}, u32[]{:S(2)}, u32[]{:S(2)}) async-start(bf16[16,48,384]{2,1,0:T(8,128)(2,1)} %broadcast_in_dim.79), calls=%async_computation.2 | async-start | bytes 1179648 | tf_op jit(solution)/shard_map/all_to_all | solution.py:422
  12.5 1.4 copy-start.22
  13.1 0.8 copy-start.27
  13.1 29.0 %copy-start.25 = (pred[2]{0:T(512)(128)(4,1)}, pred[2]{0:T(512)(128)(4,1)S(1)}, u32[]{:S(2)}) copy-start(pred[2]{0:T(512)(128)(4,1)S(1)} %get-tuple-element.181) | copy-start | bytes 10
  13.2 0.7 copy-start.23
  13.8 38.5 %copy-start.12 = (s32[2]{0:T(128)}, s32[2]{0:T(128)S(1)}, u32[]{:S(2)}) copy-start(s32[2]{0:T(128)S(1)} %pad_add_fusion.3.info_ref) | copy-start | bytes 28
  28.7 23.6 %all-to-all-start.3 = ((bf16[16,16,768]{2,1,0:T(8,128)(2,1)}), bf16[16,16,768]{2,1,0:T(8,128)(2,1)S(1)}, u32[]{:S(2)}, u32[]{:S(2)}) async-start(bf16[16,16,768]{2,1,0:T(8,128)(2,1)} %get-tuple-element.116), calls=%async_computation.3 | async-start | bytes 786432 | tf_op jit(solution)/shard_map/all_to_all | solution.py:422
  32.7 2.8 %copy-start.31 = (pred[4]{0:T(512)(128)(4,1)}, pred[4]{0:T(512)(128)(4,1)S(1)}, u32[]{:S(2)}) copy-start(pred[4]{0:T(512)(128)(4,1)S(1)} %compare_and_fusion.1) | copy-start | bytes 16
  32.7 27.0 %collective-permute-start = (bf16[768,384]{1,0:T(8,128)(2,1)}, bf16[768,384]{1,0:T(8,128)(2,1)}, u32[]{:S(2)}, u32[]{:S(2)}) collective-permute-start(bf16[768,384]{1,0:T(8,128)(2,1)} %bitcast.7.refs_8_), channel_id=1, source_target_pairs={{0,32},{32,64},{64,96},{96,0},{1,33},{33,65},{65,97},{97,1},{2,34}... | collective-permute-start | bytes 1769480 | tf_op jit(solution)/shard_map/ppermute | solution.py:436
  34.0 25.7 %collective-permute-start.1 = (bf16[768,384]{1,0:T(8,128)(2,1)}, bf16[768,384]{1,0:T(8,128)(2,1)}, u32[]{:S(2)}, u32[]{:S(2)}) collective-permute-start(bf16[768,384]{1,0:T(8,128)(2,1)} %bitcast.7.refs_8_), channel_id=1, source_target_pairs={{0,96},{32,0},{64,32},{96,64},{1,97},{33,1},{65,33},{97,65},{2,98}... | collective-permute-start | bytes 1769480 | tf_op jit(solution)/shard_map/ppermute | solution.py:436
  35.6 6.5 %copy-start.24 = (s32[1024]{0:T(1024)}, s32[1024]{0:T(1024)S(1)}, u32[]{:S(2)}) copy-start(s32[1024]{0:T(1024)S(1)} %pad_clamp_fusion) | copy-start | bytes 12292
  36.2 5.9 %copy-start.20 = (s32[2,2,4,128]{3,2,1,0:T(4,128)}, s32[2,2,4,128]{3,2,1,0:T(4,128)S(1)}, u32[]{:S(2)}) copy-start(s32[2,2,4,128]{3,2,1,0:T(4,128)S(1)} %gather_fusion.2) | copy-start | bytes 24580
  36.2 19.0 %collective-permute-start.2 = (bf16[48,2048]{1,0:T(8,128)(2,1)}, bf16[48,2048]{1,0:T(8,128)(2,1)}, u32[]{:S(2)}, u32[]{:S(2)}) collective-permute-start(bf16[48,2048]{1,0:T(8,128)(2,1)} %param.18), channel_id=1, source_target_pairs={{0,1},{1,2},{2,3},{3,0},{4,5},{5,6},{6,7},{7,4},{8,9},{9,10},{10,1... | collective-permute-start | bytes 589832 | tf_op jit(solution)/shard_map/ppermute | solution.py:436
  37.6 22.1 %collective-permute-start.3 = (bf16[48,2048]{1,0:T(8,128)(2,1)}, bf16[48,2048]{1,0:T(8,128)(2,1)}, u32[]{:S(2)}, u32[]{:S(2)}) collective-permute-start(bf16[48,2048]{1,0:T(8,128)(2,1)} %param.18), channel_id=1, source_target_pairs={{0,2},{1,3},{2,0},{3,1},{4,6},{5,7},{6,4},{7,5},{8,10},{9,11},{10,... | collective-permute-start | bytes 589832 | tf_op jit(solution)/shard_map/ppermute | solution.py:436
  39.7 20.0 %collective-permute-start.4 = (bf16[48,2048]{1,0:T(8,128)(2,1)}, bf16[48,2048]{1,0:T(8,128)(2,1)}, u32[]{:S(2)}, u32[]{:S(2)}) collective-permute-start(bf16[48,2048]{1,0:T(8,128)(2,1)} %param.18), channel_id=1, source_target_pairs={{0,3},{1,0},{2,1},{3,2},{4,7},{5,4},{6,5},{7,6},{8,11},{9,8},{10,9... | collective-permute-start | bytes 589832 | tf_op jit(solution)/shard_map/ppermute | solution.py:436
  42.1 17.6 %copy-start.11 = (s32[2]{0:T(128)}, s32[2]{0:T(128)S(1)}, u32[]{:S(2)}) copy-start(s32[2]{0:T(128)S(1)} %broadcast.368.info_ref) | copy-start | bytes 28
  52.3 0.7 copy-start.18
  55.2 18.0 %collective-permute-start.16 = (bf16[768,384]{1,0:T(8,128)(2,1)}, bf16[768,384]{1,0:T(8,128)(2,1)}, u32[]{:S(2)}, u32[]{:S(2)}) collective-permute-start(bf16[768,384]{1,0:T(8,128)(2,1)} %bitcast.7.refs_8_), channel_id=1, source_target_pairs={{0,16},{16,0},{1,17},{17,1},{2,18},{18,2},{3,19},{19,3},{4,20},{20... | collective-permute-start | bytes 1769480 | tf_op jit(solution)/shard_map/ppermute | solution.py:431
  60.4 52.4 %copy-start.29 = (f32[768]{0:T(1024)S(1)}, f32[768]{0:T(1024)}, u32[]{:S(2)}) copy-start(f32[768]{0:T(1024)} %param.16) | copy-start | bytes 9220
  60.4 52.4 %copy-start.30 = (f32[768]{0:T(1024)S(1)}, f32[768]{0:T(1024)}, u32[]{:S(2)}) copy-start(f32[768]{0:T(1024)} %param.17) | copy-start | bytes 9220
  66.9 33.6 %collective-permute-start.5 = (bf16[192,2048]{1,0:T(8,128)(2,1)}, bf16[192,2048]{1,0:T(8,128)(2,1)}, u32[]{:S(2)}, u32[]{:S(2)}) collective-permute-start(bf16[192,2048]{1,0:T(8,128)(2,1)} %constant_dynamic-update-slice_fusion.refs_0_), channel_id=1, source_target_pairs={{0,4},{4,8},{8,12},{12,0},{1,5},{5,9},{9,13},{13,1},{2,6},{6,10},{... | collective-permute-start | bytes 2359304 | tf_op jit(solution)/shard_map/ppermute | solution.py:436
  66.9 33.6 %collective-permute-start.6 = (bf16[192,2048]{1,0:T(8,128)(2,1)}, bf16[192,2048]{1,0:T(8,128)(2,1)}, u32[]{:S(2)}, u32[]{:S(2)}) collective-permute-start(bf16[192,2048]{1,0:T(8,128)(2,1)} %constant_dynamic-update-slice_fusion.refs_0_), channel_id=1, source_target_pairs={{0,12},{4,0},{8,4},{12,8},{1,13},{5,1},{9,5},{13,9},{2,14},{6,2},{... | collective-permute-start | bytes 2359304 | tf_op jit(solution)/shard_map/ppermute | solution.py:436
  69.6 7.9 %collective-permute-start.7 = (bf16[128,768]{1,0:T(8,128)(2,1)}, bf16[128,768]{1,0:T(8,128)(2,1)S(1)}, u32[]{:S(2)}, u32[]{:S(2)}) collective-permute-start(bf16[128,768]{1,0:T(8,128)(2,1)} %get-tuple-element.131.refs_0_), channel_id=1, source_target_pairs={{0,32},{32,64},{64,96},{96,0},{1,33},{33,65},{65,97},{97,1},{2,34}... | collective-permute-start | bytes 589832 | tf_op jit(solution)/shard_map/ppermute | solution.py:436
  70.8 11.9 %collective-permute-start.8 = (bf16[128,768]{1,0:T(8,128)(2,1)}, bf16[128,768]{1,0:T(8,128)(2,1)S(1)}, u32[]{:S(2)}, u32[]{:S(2)}) collective-permute-start(bf16[128,768]{1,0:T(8,128)(2,1)} %get-tuple-element.131.refs_0_), channel_id=1, source_target_pairs={{0,64},{32,96},{64,0},{96,32},{1,65},{33,97},{65,1},{97,33},{2,66}... | collective-permute-start | bytes 589832 | tf_op jit(solution)/shard_map/ppermute | solution.py:436
  73.2 11.7 %collective-permute-start.10 = (bf16[128,768]{1,0:T(8,128)(2,1)}, bf16[128,768]{1,0:T(8,128)(2,1)}, u32[]{:S(2)}, u32[]{:S(2)}) collective-permute-start(bf16[128,768]{1,0:T(8,128)(2,1)} %get-tuple-element.131.refs_0_), channel_id=1, source_target_pairs={{0,128},{128,0},{1,129},{129,1},{2,130},{130,2},{3,131},{131,3},{4... | collective-permute-start | bytes 589832 | tf_op jit(solution)/shard_map/ppermute | solution.py:431
  77.5 0.7 copy-start.4
  78.1 12.4 %collective-permute-start.9 = (bf16[128,768]{1,0:T(8,128)(2,1)}, bf16[128,768]{1,0:T(8,128)(2,1)}, u32[]{:S(2)}, u32[]{:S(2)}) collective-permute-start(bf16[128,768]{1,0:T(8,128)(2,1)} %get-tuple-element.131.refs_0_), channel_id=1, source_target_pairs={{0,96},{32,0},{64,32},{96,64},{1,97},{33,1},{65,33},{97,65},{2,98}... | collective-permute-start | bytes 589832 | tf_op jit(solution)/shard_map/ppermute | solution.py:436
  82.7 0.7 copy-start.6
  83.4 7.7 %collective-permute-start.14 = (bf16[384,384]{1,0:T(8,128)(2,1)}, bf16[384,384]{1,0:T(8,128)(2,1)}, u32[]{:S(2)}, u32[]{:S(2)}) collective-permute-start(bf16[384,384]{1,0:T(8,128)(2,1)} %slice.28), channel_id=1, source_target_pairs={{0,32},{32,64},{64,96},{96,0},{1,33},{33,65},{65,97},{97,1},{2,34}... | collective-permute-start | bytes 884744 | tf_op jit(solution)/shard_map/ppermute | solution.py:436
  84.9 9.4 %collective-permute-start.15 = (bf16[384,384]{1,0:T(8,128)(2,1)}, bf16[384,384]{1,0:T(8,128)(2,1)S(1)}, u32[]{:S(2)}, u32[]{:S(2)}) collective-permute-start(bf16[384,384]{1,0:T(8,128)(2,1)} %slice.29), channel_id=1, source_target_pairs={{0,96},{32,0},{64,32},{96,64},{1,97},{33,1},{65,33},{97,65},{2,98}... | collective-permute-start | bytes 884744 | tf_op jit(solution)/shard_map/ppermute | solution.py:436
  90.6 5.9 %collective-permute-start.11 = (bf16[128,768]{1,0:T(8,128)(2,1)}, bf16[128,768]{1,0:T(8,128)(2,1)S(1)}, u32[]{:S(2)}, u32[]{:S(2)}) collective-permute-start(bf16[128,768]{1,0:T(8,128)(2,1)} %collective-permute-done.10.refs_4_), channel_id=1, source_target_pairs={{0,32},{32,64},{64,96},{96,0},{1,33},{33,65},{65,97},{97,1},{2,34}... | collective-permute-start | bytes 589832 | tf_op jit(solution)/shard_map/ppermute | solution.py:436
  91.1 23.1 %collective-permute-start.17 = (bf16[768,384]{1,0:T(8,128)(2,1)}, bf16[768,384]{1,0:T(8,128)(2,1)S(1)}, u32[]{:S(2)}, u32[]{:S(2)}) collective-permute-start(bf16[768,384]{1,0:T(8,128)(2,1)} %collective-permute-done.refs_9_), channel_id=1, source_target_pairs={{0,16},{16,0},{1,17},{17,1},{2,18},{18,2},{3,19},{19,3},{4,20},{20... | collective-permute-start | bytes 1769480 | tf_op jit(solution)/shard_map/ppermute | solution.py:431
  94.3 9.3 %copy-start.2 = (bf16[384,384]{1,0:T(8,128)(2,1)}, bf16[384,384]{1,0:T(8,128)(2,1)S(1)}, u32[]{:S(2)}) copy-start(bf16[384,384]{1,0:T(8,128)(2,1)S(1)} %collective-permute-done.15.refs_11_) | copy-start | bytes 884740
  94.3 17.1 %collective-permute-start.18 = (bf16[384,384]{1,0:T(8,128)(2,1)}, bf16[384,384]{1,0:T(8,128)(2,1)S(1)}, u32[]{:S(2)}, u32[]{:S(2)}) collective-permute-start(bf16[384,384]{1,0:T(8,128)(2,1)} %collective-permute-done.14.refs_10_), channel_id=1, source_target_pairs={{0,16},{16,0},{1,17},{17,1},{2,18},{18,2},{3,19},{19,3},{4,20},{20... | collective-permute-start | bytes 884744 | tf_op jit(solution)/shard_map/ppermute | solution.py:431
  96.5 17.7 %collective-permute-start.20 = (bf16[768,384]{1,0:T(8,128)(2,1)}, bf16[768,384]{1,0:T(8,128)(2,1)S(1)}, u32[]{:S(2)}, u32[]{:S(2)}) collective-permute-start(bf16[768,384]{1,0:T(8,128)(2,1)} %collective-permute-done.1.refs_12_), channel_id=1, source_target_pairs={{0,16},{16,0},{1,17},{17,1},{2,18},{18,2},{3,19},{19,3},{4,20},{20... | collective-permute-start | bytes 1769480 | tf_op jit(solution)/shard_map/ppermute | solution.py:431
  100.5 8.2 %collective-permute-start.12 = (bf16[128,768]{1,0:T(8,128)(2,1)}, bf16[128,768]{1,0:T(8,128)(2,1)S(1)}, u32[]{:S(2)}, u32[]{:S(2)}) collective-permute-start(bf16[128,768]{1,0:T(8,128)(2,1)} %collective-permute-done.10.refs_4_), channel_id=1, source_target_pairs={{0,64},{32,96},{64,0},{96,32},{1,65},{33,97},{65,1},{97,33},{2,66}... | collective-permute-start | bytes 589832 | tf_op jit(solution)/shard_map/ppermute | solution.py:436
  100.5 9.5 %collective-permute-start.13 = (bf16[128,768]{1,0:T(8,128)(2,1)}, bf16[128,768]{1,0:T(8,128)(2,1)S(1)}, u32[]{:S(2)}, u32[]{:S(2)}) collective-permute-start(bf16[128,768]{1,0:T(8,128)(2,1)} %collective-permute-done.10.refs_4_), channel_id=1, source_target_pairs={{0,96},{32,0},{64,32},{96,64},{1,97},{33,1},{65,33},{97,65},{2,98}... | collective-permute-start | bytes 589832 | tf_op jit(solution)/shard_map/ppermute | solution.py:436
  108.7 24.9 %collective-permute-start.21 = (bf16[96,2048]{1,0:T(8,128)(2,1)S(1)}, bf16[96,2048]{1,0:T(8,128)(2,1)S(1)}, u32[]{:S(2)}, u32[]{:S(2)}) collective-permute-start(bf16[96,2048]{1,0:T(8,128)(2,1)S(1)} %slice.30), channel_id=1, source_target_pairs={{0,4},{4,8},{8,12},{12,0},{1,5},{5,9},{9,13},{13,1},{2,6},{6,10},{... | collective-permute-start | bytes 1179656 | tf_op jit(solution)/shard_map/ppermute | solution.py:436
  110.0 23.6 %collective-permute-start.22 = (bf16[96,2048]{1,0:T(8,128)(2,1)S(1)}, bf16[96,2048]{1,0:T(8,128)(2,1)S(1)}, u32[]{:S(2)}, u32[]{:S(2)}) collective-permute-start(bf16[96,2048]{1,0:T(8,128)(2,1)S(1)} %slice.31), channel_id=1, source_target_pairs={{0,12},{4,0},{8,4},{12,8},{1,13},{5,1},{9,5},{13,9},{2,14},{6,2},{... | collective-permute-start | bytes 1179656 | tf_op jit(solution)/shard_map/ppermute | solution.py:436
  111.4 2.8 %collective-permute-start.19 = (bf16[384,384]{1,0:T(8,128)(2,1)}, bf16[384,384]{1,0:T(8,128)(2,1)S(1)}, u32[]{:S(2)}, u32[]{:S(2)}) collective-permute-start(bf16[384,384]{1,0:T(8,128)(2,1)} %copy-done.2), channel_id=1, source_target_pairs={{0,16},{16,0},{1,17},{17,1},{2,18},{18,2},{3,19},{19,3},{4,20},{20... | collective-permute-start | bytes 884744 | tf_op jit(solution)/shard_map/ppermute | solution.py:431
  114.2 1.0 copy-start.3
  115.2 0.9 copy-start.5
  116.1 0.9 copy-start.7
  133.6 4.3 %copy-start.13 = (bf16[1024,768]{1,0:T(8,128)(2,1)}, bf16[1024,768]{1,0:T(8,128)(2,1)S(1)}, u32[]{:S(2)}) copy-start(bf16[1024,768]{1,0:T(8,128)(2,1)S(1)} %shard_map.99.mine_ref) | copy-start | bytes 4718596
  133.6 14.1 %copy-start.21 = (s32[2,2,4,128]{3,2,1,0:T(4,128)S(1)}, s32[2,2,4,128]{3,2,1,0:T(4,128)}, u32[]{:S(2)}) copy-start(s32[2,2,4,128]{3,2,1,0:T(4,128)} %copy-done.20) | copy-start | bytes 24580
  133.6 14.1 %copy-start.26 = (pred[2]{0:T(512)(128)(4,1)S(1)}, pred[2]{0:T(512)(128)(4,1)}, u32[]{:S(2)}) copy-start(pred[2]{0:T(512)(128)(4,1)} %copy-done.25) | copy-start | bytes 10
  133.6 0.8 copy-start
  134.4 3.4 %collective-permute-start.23 = (bf16[1024,768]{1,0:T(8,128)(2,1)S(1)}, bf16[1024,768]{1,0:T(8,128)(2,1)S(1)}, u32[]{:S(2)}, u32[]{:S(2)}) collective-permute-start(bf16[1024,768]{1,0:T(8,128)(2,1)S(1)} %shard_map.99.mine_ref), channel_id=1, source_target_pairs={{0,16},{16,0},{1,17},{17,1},{2,18},{18,2},{3,19},{19,3},{4,20},{20... | collective-permute-start | bytes 4718600 | tf_op jit(solution)/shard_map/ppermute | solution.py:431
  137.9 1.1 copy-start.15
  142.6 30.8 %all-to-all-start.4 = ((bf16[16,40,768]{2,1,0:T(8,128)(2,1)}), bf16[16,40,768]{2,1,0:T(8,128)(2,1)}, u32[]{:S(2)}, u32[]{:S(2)}) async-start(bf16[16,40,768]{2,1,0:T(8,128)(2,1)} %shard_map.100), calls=%async_computation.4 | async-start | bytes 1966080 | tf_op jit(solution)/shard_map/all_to_all | solution.py:422
  149.0 1.0 copy-start.1
  150.0 23.4 %copy-start.17 = (f32[128,128]{1,0:T(8,128)S(1)}, f32[128,128]{1,0:T(8,128)}, u32[]{:S(2)}) copy-start(f32[128,128]{1,0:T(8,128)} %shard_map.98.counts_ref) | copy-start | bytes 196612
  150.0 28.6 %copy-start.28 = (pred[2]{0:T(512)(128)(4,1)S(1)}, pred[2]{0:T(512)(128)(4,1)}, u32[]{:S(2)}) copy-start(pred[2]{0:T(512)(128)(4,1)} %copy-done.27) | copy-start | bytes 10
  150.0 29.4 %copy-start.32 = (pred[4]{0:T(512)(128)(4,1)S(1)}, pred[4]{0:T(512)(128)(4,1)}, u32[]{:S(2)}) copy-start(pred[4]{0:T(512)(128)(4,1)} %copy-done.31) | copy-start | bytes 16
  150.0 31.5 %copy-start.19 = (s32[2,4,2,128]{3,2,1,0:T(2,128)S(1)}, s32[2,4,2,128]{3,2,1,0:T(2,128)}, u32[]{:S(2)}) copy-start(s32[2,4,2,128]{3,2,1,0:T(2,128)} %copy.18) | copy-start | bytes 24580
  165.8 0.6 copy-start.8
  181.8 19.3 %all-to-all-start.5 = ((f32[16,8,128]{2,1,0:T(8,128)}), f32[16,8,128]{2,1,0:T(8,128)S(1)}, u32[]{:S(2)}, u32[]{:S(2)}) async-start(f32[16,8,128]{2,1,0:T(8,128)} %bitcast.27), calls=%async_computation.5 | async-start | bytes 131072 | tf_op jit(solution)/shard_map/all_to_all | solution.py:422

commit v4 on v3

--- a/solution.py
+++ b/solution.py
@@ -66,34 +66,58 @@
         tail = table_ref[whole:vocab, :].astype(F32)
         for k in range(vocab - whole):
             rows = rows + jnp.where(wanted == whole + k, tail[k : k + 1, :], 0.0)
-    rows_ref[...] = rows.astype(BF16).reshape(rows_ref.shape)
+    rows = rows.astype(BF16)
+    half = rows_ref.shape[2]
+    for side in range(2):
+        rows_ref[:, side * LIST : (side + 1) * LIST, :] = rows[:, side * half : (side + 1) * half].reshape(
+            passages, LIST, half
+        )
     count_ref[...] = jnp.broadcast_to(jnp.max(most, axis=0, keepdims=True), count_ref.shape).astype(
         jnp.int32
     )
 
 
-def listed_rows(info, ids, table):
+def lists_with_weights_kernel(info_ref, ids_ref, table_ref, qkv_ref, wout_ref, rows_ref, count_ref, found_ref):
+    part = rows_ref.shape[2]
+    column = info_ref[2] * part
+    within = qkv_ref.shape[1]
+
+    def spread(piece):
+        for p in range(rows_ref.shape[0]):
+            rows_ref[p, 2 * LIST :, :] = piece
+
+    @pl.when(column < within)
+    def _():
+        spread(qkv_ref[:, pl.ds(pl.multiple_of(column, part), part)])
+
+    @pl.when(column >= within)
+    def _():
+        spread(wout_ref[:, pl.ds(pl.multiple_of(column - within, part), part)])
+
+    lists_kernel(info_ref, ids_ref, table_ref, rows_ref, count_ref, found_ref)
+
+
+def listed_rows(info, ids, table, weights=()):
     passages = ids.shape[0]
-    return pl.pallas_call(
-        lists_kernel,
+    half = table.shape[1] // 2
+    rows = 2 * LIST + (weights[0].shape[0] if weights else 0)
+    return pl.pallas_call(
+        lists_with_weights_kernel if weights else lists_kernel,
         out_shape=(
-            jax.ShapeDtypeStruct((passages, LIST, table.shape[1]), BF16),
+            jax.ShapeDtypeStruct((passages, rows, half), BF16),
             jax.ShapeDtypeStruct((8, 128), jnp.int32),
         ),
-        in_specs=[
-            pl.BlockSpec(memory_space=pltpu.SMEM),
-            pl.BlockSpec(memory_space=pltpu.VMEM),
-            pl.BlockSpec(memory_space=pltpu.VMEM),
-        ],
+        in_specs=[pl.BlockSpec(memory_space=pltpu.SMEM)]
+        + [pl.BlockSpec(memory_space=pltpu.VMEM)] * (2 + len(weights)),
         out_specs=(pl.BlockSpec(memory_space=pltpu.VMEM), pl.BlockSpec(memory_space=pltpu.VMEM)),
         scratch_shapes=[pltpu.VMEM((passages * LIST, 128), F32)],
         compiler_params=pltpu.CompilerParams(vmem_limit_bytes=40 << 20),
-    )(info, ids, table)
-
-
-def expand_kernel(info_ref, row_ref, vocab_ref, got_ref, out_ref):
-    owners, _, width = got_ref.shape
-    vocab = vocab_ref[0]
+    )(info, ids, table, *weights)
+
+
+def expand_kernel(info_ref, row_ref, got_ref, out_ref):
+    owners, _, half = got_ref.shape
+    vocab = info_ref[2]
     first_slot = info_ref[1] * LIST
     row = row_ref[...]
     across = jnp.broadcast_to(row, (SEQ, SEQ))
@@ -114,21 +138,26 @@
     place = owner_down[:, 0:1] * LIST + slot
     place = jnp.where((slot >= 0) & (slot < LIST), place, -1)
     hits = jnp.where(place == iota((SEQ, owners * LIST), 1), 1.0, 0.0).astype(BF16)
-    out_ref[...] = dot(hits, got_ref[...].reshape(owners * LIST, width)).astype(BF16)
-
-
-def expanded(info, row, vocab, got):
+    top = out_ref.shape[0] - 2 * SEQ
+    if top:
+        out_ref[0:top, :] = got_ref[:, 2 * LIST :, :].reshape(top, half)
+    for side in range(2):
+        rows = got_ref[:, side * LIST : (side + 1) * LIST, :].reshape(owners * LIST, half)
+        out_ref[top + side * SEQ : top + (side + 1) * SEQ, :] = dot(hits, rows).astype(BF16)
+
+
+def expanded(info, row, got):
+    owners, rows, half = got.shape
     return pl.pallas_call(
         expand_kernel,
-        out_shape=jax.ShapeDtypeStruct((SEQ, got.shape[2]), BF16),
+        out_shape=jax.ShapeDtypeStruct((owners * (rows - 2 * LIST) + 2 * SEQ, half), BF16),
         in_specs=[
             pl.BlockSpec(memory_space=pltpu.SMEM),
             pl.BlockSpec(memory_space=pltpu.VMEM),
-            pl.BlockSpec(memory_space=pltpu.SMEM),
             pl.BlockSpec(memory_space=pltpu.VMEM),
         ],
         out_specs=pl.BlockSpec(memory_space=pltpu.VMEM),
-    )(info, row, vocab, got)
+    )(info, row, got)
 
 
 def put(sources, targets, sems):
@@ -143,23 +172,34 @@
 
 
 def encode_kernel(info_ref, *refs):
-    x_size = 4
-    x_parts, w_parts = refs[0 : 2 * x_size], refs[2 * x_size : 2 * x_size + 10]
-    gain_ref, bias_ref, out_ref = refs[2 * x_size + 10 : 2 * x_size + 13]
-    x_ref, w_ref, packed_ref, scores_ref, probs_ref, context_ref, sems = refs[2 * x_size + 13 :]
+    rings, fars = refs[0:10], refs[10:14]
+    gain_ref, bias_ref, out_ref = refs[14:17]
+    x_ref, w_ref, packed_ref, scores_ref, probs_ref, context_ref, sems = refs[17:]
+    x_size = len(fars)
     core, at_x = info_ref[0], info_ref[1]
-    depth = w_ref.shape[1]
-    places = []
-    for side in (core, 1 - core):
-        for back, first, count in RING:
-            place = side * x_size + lax.rem(at_x - back + x_size, x_size)
-            places.append(w_ref.at[place, pl.ds(first * (depth // 2), count * (depth // 2)), :])
-    put(
-        x_parts + w_parts,
-        [x_ref.at[k, pl.ds(z * SEQ, SEQ), :] for z in range(2) for k in range(x_size)] + places,
-        sems,
-    )
-    part = w_ref.shape[2]
+    depth, part = w_ref.shape[1:]
+    joined = (depth + 2 * SEQ) // 2
+    sources, targets = [], []
+
+    def tokens_to(chunk, passage, ref, row):
+        for side in range(2):
+            sources.append(ref.at[pl.ds(row + side * SEQ, SEQ), :])
+            targets.append(x_ref.at[chunk, pl.ds(passage * SEQ, SEQ), pl.ds(side * part, part)])
+
+    for ref, (core_at, (back, first, count)) in zip(
+        rings, [(c, r) for c in (core, 1 - core) for r in RING], strict=True
+    ):
+        place = core_at * x_size + lax.rem(at_x - back + x_size, x_size)
+        start = first * joined
+        rows = min(count * joined, depth - start)
+        sources.append(ref.at[pl.ds(0, rows), :])
+        targets.append(w_ref.at[place, pl.ds(start, rows), :])
+    for ref, (back, first, count) in zip(rings[0:5], RING, strict=True):
+        if (first + count) * joined > depth:
+            tokens_to(back, 0, ref, depth - first * joined)
+    for back, ref in enumerate(fars):
+        tokens_to(back, 1, ref, 0)
+    put(sources, targets, sems)
     tokens, width = x_ref.shape[1:]
     left = iota((SEQ, 2 * HEAD), 1) < HEAD
     zero = jnp.zeros((SEQ, 2 * HEAD), BF16)
@@ -213,49 +253,44 @@
     lax.fori_loop(0, x_size, step, 0)
 
 
-def encoded(info, x_parts, w_parts, gain, bias):
-    tokens, width = 2 * SEQ, x_parts[0].shape[1]
-    chunks = len(x_parts) // 2
-    depth, part = w_parts[0].shape
-    count = len(x_parts) + len(w_parts)
+def encoded(info, rings, fars, gain, bias):
+    part = fars[0].shape[1]
+    tokens, width, chunks = 2 * SEQ, 2 * part, len(fars)
     pairs = tokens // SEQ * HEADS // 2
     return pl.pallas_call(
         encode_kernel,
         out_shape=jax.ShapeDtypeStruct((chunks * tokens, width), BF16),
         in_specs=[pl.BlockSpec(memory_space=pltpu.SMEM)]
-        + [pl.BlockSpec(memory_space=pl.ANY)] * count
+        + [pl.BlockSpec(memory_space=pl.ANY)] * (len(rings) + chunks)
         + [pl.BlockSpec(memory_space=pltpu.VMEM)] * 2,
         out_specs=pl.BlockSpec(memory_space=pltpu.VMEM),
         scratch_shapes=[
             pltpu.VMEM((chunks, tokens, width), BF16),
-            pltpu.VMEM((chunks * 2, depth, part), BF16),
+            pltpu.VMEM((chunks * 2, width, part), BF16),
             pltpu.VMEM((tokens, 3 * width), BF16),
             pltpu.VMEM((pairs, SEQ, 2 * SEQ), F32),
             pltpu.VMEM((pairs, SEQ, 2 * SEQ), BF16),
             pltpu.VMEM((tokens, width), BF16),
-            pltpu.SemaphoreType.DMA((count,)),
+            pltpu.SemaphoreType.DMA((len(rings) + 4 * chunks,)),
         ],
         compiler_params=pltpu.CompilerParams(vmem_limit_bytes=40 << 20),
-    )(info, *x_parts, *w_parts, gain.reshape(1, width), bias.reshape(1, width))
+    )(info, *rings, *fars, gain.reshape(1, width), bias.reshape(1, width))
 
 
 def score_kernel(info_ref, mine_ref, other_ref, local_ref, *refs):
     parts = refs[0:5]
     out_ref, old_ref, cent_ref, sems = refs[5:]
-    quarters = 4
     step = pl.program_id(0)
 
     @pl.when(step == 0)
     def _():
-        shard = parts[0].shape[0] // quarters
-        sources, targets = [], []
-        for ref, (back, first, count) in zip(parts, RING, strict=True):
-            owner = lax.rem(info_ref[0] - back + 4, 4) * quarters
-            for k in range(2 * count):
-                place = owner + lax.rem(info_ref[2] - 2 * first - k + quarters, quarters)
-                sources.append(ref.at[pl.ds(k * shard, shard), :])
-                targets.append(cent_ref.at[pl.ds(pl.multiple_of(place * shard, shard), shard), :])
-        put(sources, targets, sems)
+        rows_of = parts[0].shape[0]
+        targets = []
+        for back, first, count in RING:
+            start = lax.rem(info_ref[0] - back + 4, 4) * rows_of + first * (rows_of // 2)
+            start = pl.multiple_of(start, rows_of // 2)
+            targets.append(cent_ref.at[pl.ds(start, count * (rows_of // 2)), :])
+        put(parts, targets, sems)
 
     rows = mine_ref.shape[0]
     block = cent_ref.shape[1]
@@ -305,7 +340,7 @@
         ),
         scratch_shapes=[
             pltpu.VMEM((width, block), BF16),
-            pltpu.SemaphoreType.DMA((16,)),
+            pltpu.SemaphoreType.DMA((len(parts),)),
         ],
         compiler_params=pltpu.CompilerParams(vmem_limit_bytes=40 << 20),
     )(info, mine, other, local.reshape(2 * tokens // SEQ, 1, SEQ), *parts)
@@ -481,49 +516,35 @@
         assignments.reshape(dp_size, fs_size, SEQ),
     )
 
-    part = (w_qkv.shape[1] + w_out.shape[1]) // (2 * x_size)
-    both = jnp.concatenate([w_qkv, w_out], axis=1)
-    piece = lax.dynamic_slice_in_dim(both, (core * x_size + at_x) * part, part, 1)
-    column = gathered(piece, FS).reshape(width, part)
-
     my_row = lax.dynamic_slice_in_dim(ids, fs_rank, 1, 0)
-    vocab_arr = jnp.full((1,), vocab, jnp.int32)
-    sent, most = listed_rows(info_of(fs_rank, zero), ids, embed_table)
-    sent, column = lax.optimization_barrier((sent, column))
-    w_back, w_ahead = neighbours(column, "x")
-
-    sent, start = lax.optimization_barrier((sent, centroids_t))
-    rows = [start] + [turned(start, "zl", k) for k in range(1, 4)]
-
+    my_column = core * x_size + at_x
+    sent, most = listed_rows(info_of(fs_rank, zero, my_column), ids, embed_table, (w_qkv, w_out))
     got = exchanged(sent, FS)
-    got, chosen = lax.optimization_barrier((got, chosen))
-    inputs = expanded(info_of(fs_rank, zero), my_row, vocab_arr, got)
+    got, chosen, counts, my_row = lax.optimization_barrier((got, chosen, counts, my_row))
+    ring = expanded(info_of(fs_rank, zero, vocab), my_row, got)
 
     def more_rows(state):
         turn, acc = state
-        info = info_of(fs_rank, turn)
-        again, _ = listed_rows(info, ids, embed_table)
-        return turn + 1, acc + expanded(info, my_row, vocab_arr, exchanged(again, FS))
+        again, _ = listed_rows(info_of(fs_rank, turn, my_column), ids, embed_table)
+        extra = expanded(info_of(fs_rank, turn, vocab), my_row, exchanged(again, FS))
+        return turn + 1, acc.at[width:, :].add(extra)
 
     most = most[0, 0]
-    _, inputs = lax.while_loop(
-        lambda state: state[0] * LIST < most, more_rows, (jnp.int32(1), inputs)
-    )
-
-    inputs, w_back, w_ahead, *rows = lax.optimization_barrier((inputs, w_back, w_ahead, *rows))
-    far = swapped(inputs, "zh")
-    pieces = [inputs] + [turned(inputs, "x", k) for k in range(1, x_size)]
-    mine_w = [column, w_back, *far_halves(w_back, w_ahead, "x"), w_ahead]
-    other_w = [swapped(w, "core") for w in mine_w]
-
-    near = jnp.concatenate(rows, axis=0)
+    _, ring = lax.while_loop(lambda state: state[0] * LIST < most, more_rows, (jnp.int32(1), ring))
+
+    far = swapped(ring[width:], "zh")
+    back, ahead = neighbours(ring, "x")
+    rings = [ring, back, *far_halves(back, ahead, "x"), ahead]
+    fars = [far] + [turned(far, "x", k) for k in range(1, x_size)]
+    rings += [swapped(piece, "core") for piece in rings]
+
+    shard, _ = lax.optimization_barrier((centroids_t, ring))
+    near = gathered(shard, "zl").reshape(-1, block)
+    fars[0], near = lax.optimization_barrier((fars[0], near))
     back, ahead = neighbours(near, "y")
-    far, counts = lax.optimization_barrier((far, counts))
-    pieces += [far] + [turned(far, "x", k) for k in range(1, x_size)]
-    pieces[0], back, ahead = lax.optimization_barrier((inputs, back, ahead))
     far_low, far_high = far_halves(back, ahead, "y")
 
-    mine = encoded(info_of(core, at_x), pieces, mine_w + other_w, ln_gain, ln_bias)
+    mine = encoded(info_of(core, at_x), rings, fars, ln_gain, ln_bias)
     mine, far_low, far_high = lax.optimization_barrier((mine, far_low, far_high))
     other = swapped(mine, "core")
 
@@ -537,15 +558,15 @@
     got = exchanged(packed, FS)
 
     stats, previous = scored(
-        info_of(lax.axis_index("y"), fs_rank, lax.axis_index("zl")),
+        info_of(lax.axis_index("y"), fs_rank),
         mine,
         other,
         local,
         [near, back, far_low, far_high, ahead],
     )
-    stats, got = lax.optimization_barrier((stats, got))
     stats = backwards(stats.reshape(2, x_size, 2, 8, SEQ), here)
     stats = jnp.transpose(stats, (2, 1, 0, 3, 4)).reshape(dp_size, 8, SEQ)
+    stats, got = lax.optimization_barrier((stats, got))
     sums = unpacked_sums(info_of(zero, zero), counts, got)
     widest = jnp.max(got[:, SLOTS, 0:1].astype(F32)).astype(jnp.int32)
     _, sums = lax.while_loop(

time: 203 us -> 197 us (0.970)
  waiting for transfers between devices: 43.3 us -> 59.2 us
  local copies, waits for them, and re-layouts: 28.8 us -> 17 us
  starting transfers between devices: 64.9 us -> 53.9 us
    ppermute x7, waiting for transfers between devices: 5.6 us -> 20.1 us  [swapped(): return lax.ppermute(shard, axis, [(0, 1), (1, 0)])]
    ppermute x17 -> x11, starting transfers between devices: 19.3 us -> 12.8 us  [turned(): lax.ppermute(shard, axis, [(i, (i + by) % devices) for i in range(devices)])]
    unnamed x61 -> x56, local copies, waits for them, and re-layouts: 13.5 us -> 7.09 us
    ppermute x17 -> x11, waiting for transfers between devices: 8.55 us -> 13.1 us  [turned(): lax.ppermute(shard, axis, [(i, (i + by) % devices) for i in range(devices)])]
    all_to_all x4, waiting for transfers between devices: 29.2 us -> 26 us  [exchanged(): return lax.all_to_all(blocks, axis, 0, 0, tiled=True)]
    slice x2, local copies, waits for them, and re-layouts: 2.72 us -> 0.07 us  [far_halves(): back[:half]]
    all_to_all x4, starting transfers between devices: 27.8 us -> 25.5 us  [exchanged(): return lax.all_to_all(blocks, axis, 0, 0, tiled=True)]
    ppermute x7, starting transfers between devices: 17.9 us -> 15.6 us  [swapped(): return lax.ppermute(shard, axis, [(0, 1), (1, 0)])]
  transfers between devices with their start and end apart: 28 -> 22, of which waited for: 11 -> 9; matrix products, arithmetic and copies ran while one was open for 9% -> 7% of each run, Pallas kernels for 25% -> 21%
where the time goes in v4:
time: 197 us
  waiting for transfers between devices  59.2 us (30%)
  Pallas kernels  57.2 us (29%)
  starting transfers between devices  53.9 us (27%)
  local copies, waits for them, and re-layouts  17 us (9%)
  other arithmetic  6.72 us (3%)
    all_to_all x4, waiting for transfers between devices, exchanged(): return lax.all_to_all(blocks, axis, 0, 0, tiled=True)  26 us
    all_to_all x4, starting transfers between devices, exchanged(): return lax.all_to_all(blocks, axis, 0, 0, tiled=True)  25.5 us
    ppermute x7, waiting for transfers between devices, swapped(): return lax.ppermute(shard, axis, [(0, 1), (1, 0)])  20.1 us
    pallas_call x1, Pallas kernels, encoded(): pl.pallas_call(encode_kernel, out_shape=jax.ShapeDtypeStruct((chunks * to...  17.2 us
    ppermute x7, starting transfers between devices, swapped(): return lax.ppermute(shard, axis, [(0, 1), (1, 0)])  15.6 us
    pallas_call x1, Pallas kernels, scored(): pl.pallas_call(score_kernel, grid=(2 * half,), out_shape=(jax.ShapeDtypeS...  14 us
    ppermute x11, waiting for transfers between devices, turned(): lax.ppermute(shard, axis, [(i, (i + by) % devices) for i in range(devices)])  13.1 us
    ppermute x11, starting transfers between devices, turned(): lax.ppermute(shard, axis, [(i, (i + by) % devices) for i in range(devices)])  12.8 us
  transfers between devices with their start and end apart: 22, of which 9 were waited for; matrix products, arithmetic and copies ran while one was open for 7% of the time, Pallas kernels for 21%

profile of v4, /device:TPU:1, one launch (start us, length us, event | category | flops | bytes accessed | tf_op | source)
XLA Modules:
  0.0 196.6 jit_solution(3578100885014918997)
XLA Ops:
  0.7 0.9 copy-done.4
  1.7 0.9 copy-done.7
  2.6 5.7 %shard_map.95 = (bf16[16,80,384]{2,1,0:T(8,128)(2,1)}, s32[8,128]{1,0:T(8,128)S(1)}) custom-call(s32[3]{0:T(128)S(1)} %pad_add_fusion.5.info_ref, s32[16,128]{1,0:T(8,128)} %bitcast.56, bf16[1908,768]{1,0:T(8,128)(2,1)} %table_ref.1, bf16[48,2304]{1,0:T(8,128)(2,1)S(1)} %copy-done.4, bf16[48,768]{1,0:T(8,128)(2,1)S(1)} %copy-done.7), custom_call_target="tpu_custom_call" | custom-call | tf_op jit(solution)/shard_map/pallas_call | solution.py:104
  8.3 9.2 %all-to-all-start.2 = ((bf16[16,80,384]{2,1,0:T(8,128)(2,1)}), bf16[16,80,384]{2,1,0:T(8,128)(2,1)}, u32[]{:S(2)}, u32[]{:S(2)}) async-start(bf16[16,80,384]{2,1,0:T(8,128)(2,1)} %get-tuple-element.179), calls=%async_computation.2 | async-start | bytes 1966080 | tf_op jit(solution)/shard_map/all_to_all | solution.py:457
  17.5 0.9 constant_dynamic-slice_fusion.1
  18.4 0.6 gather_fusion
  19.0 0.6 copy-done.26
  19.7 0.6 gather_fusion.1
  20.4 0.4 copy-done.29
  20.8 0.6 gather_fusion.2
  21.5 0.6 slice.51
  22.1 5.6 %shard_map.96 = (bf16[768,2048]{1,0:T(8,128)(2,1)S(1)}, f32[8,128]{1,0:T(8,128)S(1)}) custom-call(s32[2]{0:T(128)S(1)} %broadcast.392.info_ref, s32[1,2048]{1,0:T(1,128)S(1)} %bitcast.54), custom_call_target="tpu_custom_call" | custom-call | tf_op jit(solution)/shard_map/pallas_call | solution.py:375
  27.7 1.6 copy-done
  29.3 4.5 %shard_map.97.counts_ref = f32[128,128]{1,0:T(8,128)} custom-call(s32[1]{0:T(128)} %bitcast.17.info_ref, s32[16,16,128]{2,1,0:T(8,128)} %bitcast.60), custom_call_target="tpu_custom_call" | custom-call | tf_op jit(solution)/shard_map/pallas_call | solution.py:423
  33.8 0.6 pad_add_fusion.8.info_ref
  34.4 8.8 %all-to-all-done.2.got_ref = bf16[16,80,384]{2,1,0:T(8,128)(2,1)} async-done(((bf16[16,80,384]{2,1,0:T(8,128)(2,1)}), bf16[16,80,384]{2,1,0:T(8,128)(2,1)}, u32[]{:S(2)}, u32[]{:S(2)}) %all-to-all-start.2) | async-done | bytes 983072 | tf_op jit(solution)/shard_map/all_to_all | solution.py:457
  43.2 2.6 %shard_map.98 = bf16[1024,384]{1,0:T(8,128)(2,1)} custom-call(s32[3]{0:T(128)} %pad_add_fusion.8.info_ref, s32[1,128]{1,0:T(1,128)S(1)} %constant_dynamic-slice_fusion.row_ref, bf16[16,80,384]{2,1,0:T(8,128)(2,1)} %all-to-all-done.2.got_ref), custom_call_target="tpu_custom_call" | custom-call | tf_op jit(solution)/shard_map/pallas_call | solution.py:151
  45.8 0.7 while.23
  46.5 0.1 copy-done.17
  46.7 1.0 broadcast_in_dim.83
  47.6 3.5 %all-to-all-start.3 = ((bf16[4,48,2048]{2,1,0:T(8,128)(2,1)}), bf16[4,48,2048]{2,1,0:T(8,128)(2,1)S(1)}, u32[]{:S(2)}, u32[]{:S(2)}) async-start(bf16[4,48,2048]{2,1,0:T(8,128)(2,1)} %broadcast_in_dim.83), calls=%async_computation.3 | async-start | bytes 1572864 | tf_op jit(solution)/shard_map/all_to_all | solution.py:457
  51.1 1.3 collective-permute-start
  52.4 1.5 collective-permute-start.2
  53.9 1.0 slice.54
  54.9 4.3 %collective-permute-start.9 = (bf16[256,384]{1,0:T(8,128)(2,1)S(1)}, bf16[256,384]{1,0:T(8,128)(2,1)S(1)}, u32[]{:S(2)}, u32[]{:S(2)}) collective-permute-start(bf16[256,384]{1,0:T(8,128)(2,1)S(1)} %slice.54), channel_id=1, source_target_pairs={{0,128},{128,0},{1,129},{129,1},{2,130},{130,2},{3,131},{131,3},{4... | collective-permute-start | bytes 589832 | tf_op jit(solution)/shard_map/ppermute | solution.py:466
  59.2 16.7 %collective-permute-done.9.refs_10_ = bf16[256,384]{1,0:T(8,128)(2,1)S(1)} collective-permute-done((bf16[256,384]{1,0:T(8,128)(2,1)S(1)}, bf16[256,384]{1,0:T(8,128)(2,1)S(1)}, u32[]{:S(2)}, u32[]{:S(2)}) %collective-permute-start.9) | collective-permute-done | bytes 196640 | tf_op jit(solution)/shard_map/ppermute | solution.py:466
  75.9 3.2 %all-to-all-done.3 = bf16[4,48,2048]{2,1,0:T(8,128)(2,1)S(1)} async-done(((bf16[4,48,2048]{2,1,0:T(8,128)(2,1)}), bf16[4,48,2048]{2,1,0:T(8,128)(2,1)S(1)}, u32[]{:S(2)}, u32[]{:S(2)}) %all-to-all-start.3) | async-done | bytes 786464 | tf_op jit(solution)/shard_map/all_to_all | solution.py:457
  79.1 1.2 collective-permute-start.10
  80.4 2.4 %collective-permute-start.11 = (bf16[256,384]{1,0:T(8,128)(2,1)S(1)}, bf16[256,384]{1,0:T(8,128)(2,1)S(1)}, u32[]{:S(2)}, u32[]{:S(2)}) collective-permute-start(bf16[256,384]{1,0:T(8,128)(2,1)S(1)} %collective-permute-done.9.refs_10_), channel_id=1, source_target_pairs={{0,64},{32,96},{64,0},{96,32},{1,65},{33,97},{65,1},{97,33},{2,66}... | collective-permute-start | bytes 589832 | tf_op jit(solution)/shard_map/ppermute | solution.py:471
  82.8 1.1 collective-permute-start.12
  84.0 1.3 collective-permute-done.10.refs_11_
  85.3 5.2 %collective-permute-done.11.refs_12_ = bf16[256,384]{1,0:T(8,128)(2,1)S(1)} collective-permute-done((bf16[256,384]{1,0:T(8,128)(2,1)S(1)}, bf16[256,384]{1,0:T(8,128)(2,1)S(1)}, u32[]{:S(2)}, u32[]{:S(2)}) %collective-permute-start.11) | collective-permute-done | bytes 196640 | tf_op jit(solution)/shard_map/ppermute | solution.py:471
  90.5 2.1 %collective-permute-start.15 = (bf16[192,2048]{1,0:T(8,128)(2,1)S(1)}, bf16[192,2048]{1,0:T(8,128)(2,1)S(1)}, u32[]{:S(2)}, u32[]{:S(2)}) collective-permute-start(bf16[192,2048]{1,0:T(8,128)(2,1)S(1)} %bitcast.51), channel_id=1, source_target_pairs={{0,12},{4,0},{8,4},{12,8},{1,13},{5,1},{9,5},{13,9},{2,14},{6,2},{... | collective-permute-start | bytes 2359304 | tf_op jit(solution)/shard_map/ppermute | solution.py:471
  92.6 5.5 %collective-permute-start.4 = (bf16[1024,384]{1,0:T(8,128)(2,1)}, bf16[1024,384]{1,0:T(8,128)(2,1)S(1)}, u32[]{:S(2)}, u32[]{:S(2)}) collective-permute-start(bf16[1024,384]{1,0:T(8,128)(2,1)} %get-tuple-element.187.refs_0_), channel_id=1, source_target_pairs={{0,16},{16,0},{1,17},{17,1},{2,18},{18,2},{3,19},{19,3},{4,20},{20... | collective-permute-start | bytes 2359304 | tf_op jit(solution)/shard_map/ppermute | solution.py:466
  98.2 1.0 slice.74
  99.3 2.5 %collective-permute-start.8 = (bf16[1024,384]{1,0:T(8,128)(2,1)}, bf16[1024,384]{1,0:T(8,128)(2,1)S(1)}, u32[]{:S(2)}, u32[]{:S(2)}) collective-permute-start(bf16[1024,384]{1,0:T(8,128)(2,1)} %collective-permute-done.2.refs_4_), channel_id=1, source_target_pairs={{0,16},{16,0},{1,17},{17,1},{2,18},{18,2},{3,19},{19,3},{4,20},{20... | collective-permute-start | bytes 2359304 | tf_op jit(solution)/shard_map/ppermute | solution.py:466
  101.9 6.6 %collective-permute-done.3.refs_3_ = bf16[512,384]{1,0:T(8,128)(2,1)S(1)} collective-permute-done((bf16[512,384]{1,0:T(8,128)(2,1)S(1)}, bf16[512,384]{1,0:T(8,128)(2,1)S(1)}, u32[]{:S(2)}, u32[]{:S(2)}) %collective-permute-start.3) | collective-permute-done | bytes 393248 | tf_op jit(solution)/shard_map/ppermute | solution.py:471
  108.5 2.4 %collective-permute-start.6 = (bf16[512,384]{1,0:T(8,128)(2,1)S(1)}, bf16[512,384]{1,0:T(8,128)(2,1)S(1)}, u32[]{:S(2)}, u32[]{:S(2)}) collective-permute-start(bf16[512,384]{1,0:T(8,128)(2,1)S(1)} %collective-permute-done.1.refs_2_), channel_id=1, source_target_pairs={{0,16},{16,0},{1,17},{17,1},{2,18},{18,2},{3,19},{19,3},{4,20},{20... | collective-permute-start | bytes 1179656 | tf_op jit(solution)/shard_map/ppermute | solution.py:466
  111.0 3.0 %collective-permute-start.16 = (bf16[96,2048]{1,0:T(8,128)(2,1)S(1)}, bf16[96,2048]{1,0:T(8,128)(2,1)S(1)}, u32[]{:S(2)}, u32[]{:S(2)}) collective-permute-start(bf16[96,2048]{1,0:T(8,128)(2,1)S(1)} %slice.76), channel_id=1, source_target_pairs={{0,12},{4,0},{8,4},{12,8},{1,13},{5,1},{9,5},{13,9},{2,14},{6,2},{... | collective-permute-start | bytes 1179656 | tf_op jit(solution)/shard_map/ppermute | solution.py:471
  114.0 0.7 reshape.299.refs_15_
  114.8 1.1 copy-done.6
  115.8 17.2 %shard_map.99.mine_ref = bf16[1024,768]{1,0:T(8,128)(2,1)} custom-call(s32[2]{0:T(128)S(1)} %pad_add_fusion.7.info_ref, bf16[1024,384]{1,0:T(8,128)(2,1)} %get-tuple-element.187.refs_0_, bf16[1024,384]{1,0:T(8,128)(2,1)S(1)} %collective-permute-done.refs_1_, bf16[512,384]{1,0:T(8,128)(2,1)S(1)} %collective-permute-done.1.refs_2_, ...), custom_call_target="tpu_custom_call" | custom-call | tf_op jit(solution)/shard_map/pallas_call | solution.py:260
  133.1 0.7 copy-done.2
  133.8 0.7 collective-permute-start.17
  134.6 3.4 %collective-permute-done.17.other_ref = bf16[1024,768]{1,0:T(8,128)(2,1)} collective-permute-done((bf16[1024,768]{1,0:T(8,128)(2,1)}, bf16[1024,768]{1,0:T(8,128)(2,1)}, u32[]{:S(2)}, u32[]{:S(2)}) %collective-permute-start.17) | collective-permute-done | bytes 1572896 | tf_op jit(solution)/shard_map/ppermute | solution.py:466
  137.9 5.5 %shard_map.100 = bf16[16,40,768]{2,1,0:T(8,128)(2,1)} custom-call(bf16[768,2048]{1,0:T(8,128)(2,1)S(1)} %copy-done.1, f32[8,128]{1,0:T(8,128)S(1)} %get-tuple-element.183.most_ref, bf16[1024,768]{1,0:T(8,128)(2,1)} %shard_map.99.mine_ref, bf16[1024,768]{1,0:T(8,128)(2,1)} %collective-permute-done.17.other_ref), custom_call_target="tpu_custom_call" | custom-call | tf_op jit(solution)/shard_map/pallas_call | solution.py:399
  143.4 4.5 %all-to-all-start.4 = ((bf16[16,40,768]{2,1,0:T(8,128)(2,1)}), bf16[16,40,768]{2,1,0:T(8,128)(2,1)}, u32[]{:S(2)}, u32[]{:S(2)}) async-start(bf16[16,40,768]{2,1,0:T(8,128)(2,1)} %shard_map.100), calls=%async_computation.4 | async-start | bytes 1966080 | tf_op jit(solution)/shard_map/all_to_all | solution.py:457
  148.3 0.1 slice_reduce_fusion
  148.4 0.5 broadcast_maximum_fusion
  148.9 0.6 broadcast_compare_fusion
  149.5 14.0 %shard_map.101 = (f32[16,8,128]{2,1,0:T(8,128)S(1)}, f32[128,768]{1,0:T(8,128)S(1)}) custom-call(s32[2]{0:T(128)S(1)} %pad_add_fusion.4.info_ref, bf16[1024,768]{1,0:T(8,128)(2,1)} %shard_map.99.mine_ref, bf16[1024,768]{1,0:T(8,128)(2,1)} %collective-permute-done.17.other_ref, s32[16,1,128]{2,1,0:T(1,128)S(1)} %fusion.1.local_ref, ...), custom_call_target="tpu_custom_call" | custom-call | tf_op jit(solution)/shard_map/pallas_call | solution.py:323
  163.5 0.6 copy-done.8
  164.1 1.5 gather_fusion.3
  165.7 0.7 gather_fusion.4
  166.4 0.7 select_bitcast_fusion
  167.1 0.7 gather_fusion.5
  167.8 0.7 broadcast_select_fusion
  168.5 5.1 %all-to-all-done.4.got_ref = bf16[16,40,768]{2,1,0:T(8,128)(2,1)} async-done(((bf16[16,40,768]{2,1,0:T(8,128)(2,1)}), bf16[16,40,768]{2,1,0:T(8,128)(2,1)}, u32[]{:S(2)}, u32[]{:S(2)}) %all-to-all-start.4) | async-done | bytes 983072 | tf_op jit(solution)/shard_map/all_to_all | solution.py:457
  173.6 2.3 %shard_map.102 = f32[128,768]{1,0:T(8,128)S(1)} custom-call(s32[2]{0:T(128)} %copy-done.10, f32[128,128]{1,0:T(8,128)} %shard_map.97.counts_ref, bf16[16,40,768]{2,1,0:T(8,128)(2,1)} %all-to-all-done.4.got_ref), custom_call_target="tpu_custom_call" | custom-call | tf_op jit(solution)/shard_map/pallas_call | solution.py:447
  175.9 1.4 slice_reduce_fusion.2
  178.0 8.2 %all-to-all-start.5 = ((f32[16,8,128]{2,1,0:T(8,128)}), f32[16,8,128]{2,1,0:T(8,128)S(1)}, u32[]{:S(2)}, u32[]{:S(2)}) async-start(f32[16,8,128]{2,1,0:T(8,128)} %bitcast.28), calls=%async_computation.5 | async-start | bytes 131072 | tf_op jit(solution)/shard_map/all_to_all | solution.py:457
  186.3 0.9 divide_select_fusion
  187.1 8.8 %all-to-all-done.5 = f32[16,8,128]{2,1,0:T(8,128)S(1)} async-done(((f32[16,8,128]{2,1,0:T(8,128)}), f32[16,8,128]{2,1,0:T(8,128)S(1)}, u32[]{:S(2)}, u32[]{:S(2)}) %all-to-all-start.5) | async-done | bytes 65568 | tf_op jit(solution)/shard_map/all_to_all | solution.py:457
  196.0 0.5 add_subtract_fusion
  (97 shorter events, 1.4 us)
Async XLA Ops:
  0.6 33.2 %copy-start.16 = (s32[2048]{0:T(1024)S(1)}, s32[2048]{0:T(1024)}, u32[]{:S(2)}) copy-start(s32[2048]{0:T(1024)} %param.14) | copy-start | bytes 24580
  0.7 0.9 copy-start.4
  1.7 0.9 copy-start.7
  2.6 43.2 %copy-start.11 = (bf16[1908,768]{1,0:T(8,128)(2,1)S(1)}, bf16[1908,768]{1,0:T(8,128)(2,1)}, u32[]{:S(2)}) copy-start(bf16[1908,768]{1,0:T(8,128)(2,1)} %table_ref.1) | copy-start | bytes 8792068
  8.3 34.9 %all-to-all-start.2 = ((bf16[16,80,384]{2,1,0:T(8,128)(2,1)}), bf16[16,80,384]{2,1,0:T(8,128)(2,1)}, u32[]{:S(2)}, u32[]{:S(2)}) async-start(bf16[16,80,384]{2,1,0:T(8,128)(2,1)} %get-tuple-element.179), calls=%async_computation.2 | async-start | bytes 1966080 | tf_op jit(solution)/shard_map/all_to_all | solution.py:457
  18.4 0.6 copy-start.20
  19.0 0.6 copy-start.26
  19.0 26.7 %copy-start.23 = (pred[2]{0:T(512)(128)(4,1)}, pred[2]{0:T(512)(128)(4,1)S(1)}, u32[]{:S(2)}) copy-start(pred[2]{0:T(512)(128)(4,1)S(1)} %get-tuple-element.237) | copy-start | bytes 10
  19.7 26.0 %copy-start.21 = (s32[1024]{0:T(1024)}, s32[1024]{0:T(1024)S(1)}, u32[]{:S(2)}) copy-start(s32[1024]{0:T(1024)S(1)} %pad_clamp_fusion.1) | copy-start | bytes 12292
  20.3 0.5 copy-start.29
  20.8 24.9 %copy-start.22 = (s32[1024]{0:T(1024)}, s32[1024]{0:T(1024)S(1)}, u32[]{:S(2)}) copy-start(s32[1024]{0:T(1024)S(1)} %pad_clamp_fusion) | copy-start | bytes 12292
  21.4 24.4 %copy-start.18 = (s32[2,2,4,128]{3,2,1,0:T(4,128)}, s32[2,2,4,128]{3,2,1,0:T(4,128)S(1)}, u32[]{:S(2)}) copy-start(s32[2,2,4,128]{3,2,1,0:T(4,128)S(1)} %gather_fusion.2) | copy-start | bytes 24580
  22.1 23.7 %copy-start.10 = (s32[2]{0:T(128)}, s32[2]{0:T(128)S(1)}, u32[]{:S(2)}) copy-start(s32[2]{0:T(128)S(1)} %broadcast.392.info_ref) | copy-start | bytes 28
  27.7 1.6 copy-start
  45.7 0.9 copy-start.17
  46.7 67.3 %copy-start.28 = (f32[768]{0:T(1024)S(1)}, f32[768]{0:T(1024)}, u32[]{:S(2)}) copy-start(f32[768]{0:T(1024)} %param.18) | copy-start | bytes 9220
  47.6 31.5 %all-to-all-start.3 = ((bf16[4,48,2048]{2,1,0:T(8,128)(2,1)}), bf16[4,48,2048]{2,1,0:T(8,128)(2,1)S(1)}, u32[]{:S(2)}, u32[]{:S(2)}) async-start(bf16[4,48,2048]{2,1,0:T(8,128)(2,1)} %broadcast_in_dim.83), calls=%async_computation.3 | async-start | bytes 1572864 | tf_op jit(solution)/shard_map/all_to_all | solution.py:457
  51.1 31.7 %collective-permute-start = (bf16[1024,384]{1,0:T(8,128)(2,1)}, bf16[1024,384]{1,0:T(8,128)(2,1)S(1)}, u32[]{:S(2)}, u32[]{:S(2)}) collective-permute-start(bf16[1024,384]{1,0:T(8,128)(2,1)} %get-tuple-element.187.refs_0_), channel_id=1, source_target_pairs={{0,32},{32,64},{64,96},{96,0},{1,33},{33,65},{65,97},{97,1},{2,34}... | collective-permute-start | bytes 2359304 | tf_op jit(solution)/shard_map/ppermute | solution.py:471
  52.4 45.7 %collective-permute-start.2 = (bf16[1024,384]{1,0:T(8,128)(2,1)}, bf16[1024,384]{1,0:T(8,128)(2,1)}, u32[]{:S(2)}, u32[]{:S(2)}) collective-permute-start(bf16[1024,384]{1,0:T(8,128)(2,1)} %get-tuple-element.187.refs_0_), channel_id=1, source_target_pairs={{0,96},{32,0},{64,32},{96,64},{1,97},{33,1},{65,33},{97,65},{2,98}... | collective-permute-start | bytes 2359304 | tf_op jit(solution)/shard_map/ppermute | solution.py:471
  54.9 21.0 %collective-permute-start.9 = (bf16[256,384]{1,0:T(8,128)(2,1)S(1)}, bf16[256,384]{1,0:T(8,128)(2,1)S(1)}, u32[]{:S(2)}, u32[]{:S(2)}) collective-permute-start(bf16[256,384]{1,0:T(8,128)(2,1)S(1)} %slice.54), channel_id=1, source_target_pairs={{0,128},{128,0},{1,129},{129,1},{2,130},{130,2},{3,131},{131,3},{4... | collective-permute-start | bytes 589832 | tf_op jit(solution)/shard_map/ppermute | solution.py:466
  75.9 35.0 %copy-start.5 = (bf16[256,384]{1,0:T(8,128)(2,1)}, bf16[256,384]{1,0:T(8,128)(2,1)S(1)}, u32[]{:S(2)}) copy-start(bf16[256,384]{1,0:T(8,128)(2,1)S(1)} %collective-permute-done.9.refs_10_) | copy-start | bytes 589828
  79.1 20.2 %collective-permute-start.13 = (bf16[192,2048]{1,0:T(8,128)(2,1)S(1)}, bf16[192,2048]{1,0:T(8,128)(2,1)S(1)}, u32[]{:S(2)}, u32[]{:S(2)}) collective-permute-start(bf16[192,2048]{1,0:T(8,128)(2,1)S(1)} %bitcast.50), channel_id=1, source_target_pairs={{0,4},{4,8},{8,12},{12,0},{1,5},{5,9},{9,13},{13,1},{2,6},{6,10},{... | collective-permute-start | bytes 2359304 | tf_op jit(solution)/shard_map/ppermute | solution.py:471
  79.1 6.1 %collective-permute-start.10 = (bf16[256,384]{1,0:T(8,128)(2,1)S(1)}, bf16[256,384]{1,0:T(8,128)(2,1)S(1)}, u32[]{:S(2)}, u32[]{:S(2)}) collective-permute-start(bf16[256,384]{1,0:T(8,128)(2,1)S(1)} %collective-permute-done.9.refs_10_), channel_id=1, source_target_pairs={{0,32},{32,64},{64,96},{96,0},{1,33},{33,65},{65,97},{97,1},{2,34}... | collective-permute-start | bytes 589832 | tf_op jit(solution)/shard_map/ppermute | solution.py:471
  80.4 10.1 %collective-permute-start.11 = (bf16[256,384]{1,0:T(8,128)(2,1)S(1)}, bf16[256,384]{1,0:T(8,128)(2,1)S(1)}, u32[]{:S(2)}, u32[]{:S(2)}) collective-permute-start(bf16[256,384]{1,0:T(8,128)(2,1)S(1)} %collective-permute-done.9.refs_10_), channel_id=1, source_target_pairs={{0,64},{32,96},{64,0},{96,32},{1,65},{33,97},{65,1},{97,33},{2,66}... | collective-permute-start | bytes 589832 | tf_op jit(solution)/shard_map/ppermute | solution.py:471
  82.8 9.8 %collective-permute-start.12 = (bf16[256,384]{1,0:T(8,128)(2,1)S(1)}, bf16[256,384]{1,0:T(8,128)(2,1)S(1)}, u32[]{:S(2)}, u32[]{:S(2)}) collective-permute-start(bf16[256,384]{1,0:T(8,128)(2,1)S(1)} %collective-permute-done.9.refs_10_), channel_id=1, source_target_pairs={{0,96},{32,0},{64,32},{96,64},{1,97},{33,1},{65,33},{97,65},{2,98}... | collective-permute-start | bytes 589832 | tf_op jit(solution)/shard_map/ppermute | solution.py:471
  85.3 13.9 %collective-permute-start.1 = (bf16[512,384]{1,0:T(8,128)(2,1)S(1)}, bf16[512,384]{1,0:T(8,128)(2,1)S(1)}, u32[]{:S(2)}, u32[]{:S(2)}) collective-permute-start(bf16[512,384]{1,0:T(8,128)(2,1)S(1)} %slice.73), channel_id=1, source_target_pairs={{0,32},{32,64},{64,96},{96,0},{1,33},{33,65},{65,97},{97,1},{2,34}... | collective-permute-start | bytes 1179656 | tf_op jit(solution)/shard_map/ppermute | solution.py:471
  90.5 20.4 %collective-permute-start.15 = (bf16[192,2048]{1,0:T(8,128)(2,1)S(1)}, bf16[192,2048]{1,0:T(8,128)(2,1)S(1)}, u32[]{:S(2)}, u32[]{:S(2)}) collective-permute-start(bf16[192,2048]{1,0:T(8,128)(2,1)S(1)} %bitcast.51), channel_id=1, source_target_pairs={{0,12},{4,0},{8,4},{12,8},{1,13},{5,1},{9,5},{13,9},{2,14},{6,2},{... | collective-permute-start | bytes 2359304 | tf_op jit(solution)/shard_map/ppermute | solution.py:471
  92.6 18.3 %collective-permute-start.4 = (bf16[1024,384]{1,0:T(8,128)(2,1)}, bf16[1024,384]{1,0:T(8,128)(2,1)S(1)}, u32[]{:S(2)}, u32[]{:S(2)}) collective-permute-start(bf16[1024,384]{1,0:T(8,128)(2,1)} %get-tuple-element.187.refs_0_), channel_id=1, source_target_pairs={{0,16},{16,0},{1,17},{17,1},{2,18},{18,2},{3,19},{19,3},{4,20},{20... | collective-permute-start | bytes 2359304 | tf_op jit(solution)/shard_map/ppermute | solution.py:466
  98.1 12.9 %collective-permute-start.5 = (bf16[1024,384]{1,0:T(8,128)(2,1)S(1)}, bf16[1024,384]{1,0:T(8,128)(2,1)S(1)}, u32[]{:S(2)}, u32[]{:S(2)}) collective-permute-start(bf16[1024,384]{1,0:T(8,128)(2,1)S(1)} %collective-permute-done.refs_1_), channel_id=1, source_target_pairs={{0,16},{16,0},{1,17},{17,1},{2,18},{18,2},{3,19},{19,3},{4,20},{20... | collective-permute-start | bytes 2359304 | tf_op jit(solution)/shard_map/ppermute | solution.py:466
  99.2 9.2 %collective-permute-start.3 = (bf16[512,384]{1,0:T(8,128)(2,1)S(1)}, bf16[512,384]{1,0:T(8,128)(2,1)S(1)}, u32[]{:S(2)}, u32[]{:S(2)}) collective-permute-start(bf16[512,384]{1,0:T(8,128)(2,1)S(1)} %slice.74), channel_id=1, source_target_pairs={{0,96},{32,0},{64,32},{96,64},{1,97},{33,1},{65,33},{97,65},{2,98}... | collective-permute-start | bytes 1179656 | tf_op jit(solution)/shard_map/ppermute | solution.py:471
  99.3 15.4 %collective-permute-start.8 = (bf16[1024,384]{1,0:T(8,128)(2,1)}, bf16[1024,384]{1,0:T(8,128)(2,1)S(1)}, u32[]{:S(2)}, u32[]{:S(2)}) collective-permute-start(bf16[1024,384]{1,0:T(8,128)(2,1)} %collective-permute-done.2.refs_4_), channel_id=1, source_target_pairs={{0,16},{16,0},{1,17},{17,1},{2,18},{18,2},{3,19},{19,3},{4,20},{20... | collective-permute-start | bytes 2359304 | tf_op jit(solution)/shard_map/ppermute | solution.py:466
  108.5 6.3 %collective-permute-start.6 = (bf16[512,384]{1,0:T(8,128)(2,1)S(1)}, bf16[512,384]{1,0:T(8,128)(2,1)S(1)}, u32[]{:S(2)}, u32[]{:S(2)}) collective-permute-start(bf16[512,384]{1,0:T(8,128)(2,1)S(1)} %collective-permute-done.1.refs_2_), channel_id=1, source_target_pairs={{0,16},{16,0},{1,17},{17,1},{2,18},{18,2},{3,19},{19,3},{4,20},{20... | collective-permute-start | bytes 1179656 | tf_op jit(solution)/shard_map/ppermute | solution.py:466
  110.8 3.9 %collective-permute-start.7 = (bf16[512,384]{1,0:T(8,128)(2,1)S(1)}, bf16[512,384]{1,0:T(8,128)(2,1)S(1)}, u32[]{:S(2)}, u32[]{:S(2)}) collective-permute-start(bf16[512,384]{1,0:T(8,128)(2,1)S(1)} %collective-permute-done.3.refs_3_), channel_id=1, source_target_pairs={{0,16},{16,0},{1,17},{17,1},{2,18},{18,2},{3,19},{19,3},{4,20},{20... | collective-permute-start | bytes 1179656 | tf_op jit(solution)/shard_map/ppermute | solution.py:466
  110.9 22.1 %collective-permute-start.14 = (bf16[96,2048]{1,0:T(8,128)(2,1)S(1)}, bf16[96,2048]{1,0:T(8,128)(2,1)S(1)}, u32[]{:S(2)}, u32[]{:S(2)}) collective-permute-start(bf16[96,2048]{1,0:T(8,128)(2,1)S(1)} %slice.75), channel_id=1, source_target_pairs={{0,4},{4,8},{8,12},{12,0},{1,5},{5,9},{9,13},{13,1},{2,6},{6,10},{... | collective-permute-start | bytes 1179656 | tf_op jit(solution)/shard_map/ppermute | solution.py:471
  111.0 22.1 %collective-permute-start.16 = (bf16[96,2048]{1,0:T(8,128)(2,1)S(1)}, bf16[96,2048]{1,0:T(8,128)(2,1)S(1)}, u32[]{:S(2)}, u32[]{:S(2)}) collective-permute-start(bf16[96,2048]{1,0:T(8,128)(2,1)S(1)} %slice.76), channel_id=1, source_target_pairs={{0,12},{4,0},{8,4},{12,8},{1,13},{5,1},{9,5},{13,9},{2,14},{6,2},{... | collective-permute-start | bytes 1179656 | tf_op jit(solution)/shard_map/ppermute | solution.py:471
  114.7 23.2 %copy-start.1 = (bf16[768,2048]{1,0:T(8,128)(2,1)S(1)}, bf16[768,2048]{1,0:T(8,128)(2,1)}, u32[]{:S(2)}) copy-start(bf16[768,2048]{1,0:T(8,128)(2,1)} %copy-done) | copy-start | bytes 9437188
  114.8 1.1 copy-start.6
  133.0 14.9 %copy-start.19 = (s32[2,2,4,128]{3,2,1,0:T(4,128)S(1)}, s32[2,2,4,128]{3,2,1,0:T(4,128)}, u32[]{:S(2)}) copy-start(s32[2,2,4,128]{3,2,1,0:T(4,128)} %copy-done.18) | copy-start | bytes 24580
  133.0 15.0 %copy-start.24 = (pred[2]{0:T(512)(128)(4,1)S(1)}, pred[2]{0:T(512)(128)(4,1)}, u32[]{:S(2)}) copy-start(pred[2]{0:T(512)(128)(4,1)} %copy-done.23) | copy-start | bytes 10
  133.0 15.2 %copy-start.14 = (f32[128,128]{1,0:T(8,128)S(1)}, f32[128,128]{1,0:T(8,128)}, u32[]{:S(2)}) copy-start(f32[128,128]{1,0:T(8,128)} %shard_map.97.counts_ref) | copy-start | bytes 196612
  133.1 0.7 copy-start.2
  133.8 4.1 %collective-permute-start.17 = (bf16[1024,768]{1,0:T(8,128)(2,1)}, bf16[1024,768]{1,0:T(8,128)(2,1)}, u32[]{:S(2)}, u32[]{:S(2)}) collective-permute-start(bf16[1024,768]{1,0:T(8,128)(2,1)} %shard_map.99.mine_ref), channel_id=1, source_target_pairs={{0,16},{16,0},{1,17},{17,1},{2,18},{18,2},{3,19},{19,3},{4,20},{20... | collective-permute-start | bytes 4718600 | tf_op jit(solution)/shard_map/ppermute | solution.py:466
  134.6 14.9 %copy-start.3 = (bf16[96,2048]{1,0:T(8,128)(2,1)S(1)}, bf16[96,2048]{1,0:T(8,128)(2,1)}, u32[]{:S(2)}) copy-start(bf16[96,2048]{1,0:T(8,128)(2,1)} %copy-done.2) | copy-start | bytes 1179652
  143.4 30.2 %all-to-all-start.4 = ((bf16[16,40,768]{2,1,0:T(8,128)(2,1)}), bf16[16,40,768]{2,1,0:T(8,128)(2,1)}, u32[]{:S(2)}, u32[]{:S(2)}) async-start(bf16[16,40,768]{2,1,0:T(8,128)(2,1)} %shard_map.100), calls=%async_computation.4 | async-start | bytes 1966080 | tf_op jit(solution)/shard_map/all_to_all | solution.py:457
  149.5 16.1 %copy-start.27 = (pred[2]{0:T(512)(128)(4,1)S(1)}, pred[2]{0:T(512)(128)(4,1)}, u32[]{:S(2)}) copy-start(pred[2]{0:T(512)(128)(4,1)} %copy-done.26) | copy-start | bytes 10
  149.5 18.3 %copy-start.25 = (pred[2]{0:T(512)(128)(4,1)S(1)}, pred[2]{0:T(512)(128)(4,1)}, u32[]{:S(2)}) copy-start(pred[2]{0:T(512)(128)(4,1)} %copy-done.23) | copy-start | bytes 10
  163.5 0.6 copy-start.8
  178.0 8.3 %copy-start.30 = (f32[128]{0:T(128)S(1)}, f32[128]{0:T(128)}, u32[]{:S(2)}) copy-start(f32[128]{0:T(128)} %broadcast_maximum_fusion) | copy-start | bytes 1540
  178.0 8.3 %copy-start.31 = (pred[128]{0:T(512)(128)(4,1)S(1)}, pred[128]{0:T(512)(128)(4,1)}, u32[]{:S(2)}) copy-start(pred[128]{0:T(512)(128)(4,1)} %broadcast_compare_fusion) | copy-start | bytes 388
  178.0 18.0 %all-to-all-start.5 = ((f32[16,8,128]{2,1,0:T(8,128)}), f32[16,8,128]{2,1,0:T(8,128)S(1)}, u32[]{:S(2)}, u32[]{:S(2)}) async-start(f32[16,8,128]{2,1,0:T(8,128)} %bitcast.28), calls=%async_computation.5 | async-start | bytes 131072 | tf_op jit(solution)/shard_map/all_to_all | solution.py:457

commit v5 on v4

--- a/solution.py
+++ b/solution.py
@@ -77,42 +77,22 @@
     )
 
 
-def lists_with_weights_kernel(info_ref, ids_ref, table_ref, qkv_ref, wout_ref, rows_ref, count_ref, found_ref):
-    part = rows_ref.shape[2]
-    column = info_ref[2] * part
-    within = qkv_ref.shape[1]
-
-    def spread(piece):
-        for p in range(rows_ref.shape[0]):
-            rows_ref[p, 2 * LIST :, :] = piece
-
-    @pl.when(column < within)
-    def _():
-        spread(qkv_ref[:, pl.ds(pl.multiple_of(column, part), part)])
-
-    @pl.when(column >= within)
-    def _():
-        spread(wout_ref[:, pl.ds(pl.multiple_of(column - within, part), part)])
-
-    lists_kernel(info_ref, ids_ref, table_ref, rows_ref, count_ref, found_ref)
-
-
-def listed_rows(info, ids, table, weights=()):
+def listed_rows(info, ids, table):
     passages = ids.shape[0]
     half = table.shape[1] // 2
-    rows = 2 * LIST + (weights[0].shape[0] if weights else 0)
-    return pl.pallas_call(
-        lists_with_weights_kernel if weights else lists_kernel,
+    rows = 2 * LIST
+    return pl.pallas_call(
+        lists_kernel,
         out_shape=(
             jax.ShapeDtypeStruct((passages, rows, half), BF16),
             jax.ShapeDtypeStruct((8, 128), jnp.int32),
         ),
         in_specs=[pl.BlockSpec(memory_space=pltpu.SMEM)]
-        + [pl.BlockSpec(memory_space=pltpu.VMEM)] * (2 + len(weights)),
+        + [pl.BlockSpec(memory_space=pltpu.VMEM)] * 2,
         out_specs=(pl.BlockSpec(memory_space=pltpu.VMEM), pl.BlockSpec(memory_space=pltpu.VMEM)),
         scratch_shapes=[pltpu.VMEM((passages * LIST, 128), F32)],
         compiler_params=pltpu.CompilerParams(vmem_limit_bytes=40 << 20),
-    )(info, ids, table, *weights)
+    )(info, ids, table)
 
 
 def expand_kernel(info_ref, row_ref, got_ref, out_ref):
@@ -138,19 +118,16 @@
     place = owner_down[:, 0:1] * LIST + slot
     place = jnp.where((slot >= 0) & (slot < LIST), place, -1)
     hits = jnp.where(place == iota((SEQ, owners * LIST), 1), 1.0, 0.0).astype(BF16)
-    top = out_ref.shape[0] - 2 * SEQ
-    if top:
-        out_ref[0:top, :] = got_ref[:, 2 * LIST :, :].reshape(top, half)
     for side in range(2):
         rows = got_ref[:, side * LIST : (side + 1) * LIST, :].reshape(owners * LIST, half)
-        out_ref[top + side * SEQ : top + (side + 1) * SEQ, :] = dot(hits, rows).astype(BF16)
+        out_ref[side * SEQ : (side + 1) * SEQ, :] = dot(hits, rows).astype(BF16)
 
 
 def expanded(info, row, got):
-    owners, rows, half = got.shape
+    half = got.shape[2]
     return pl.pallas_call(
         expand_kernel,
-        out_shape=jax.ShapeDtypeStruct((owners * (rows - 2 * LIST) + 2 * SEQ, half), BF16),
+        out_shape=jax.ShapeDtypeStruct((2 * SEQ, half), BF16),
         in_specs=[
             pl.BlockSpec(memory_space=pltpu.SMEM),
             pl.BlockSpec(memory_space=pltpu.VMEM),
@@ -172,33 +149,24 @@
 
 
 def encode_kernel(info_ref, *refs):
-    rings, fars = refs[0:10], refs[10:14]
-    gain_ref, bias_ref, out_ref = refs[14:17]
-    x_ref, w_ref, packed_ref, scores_ref, probs_ref, context_ref, sems = refs[17:]
-    x_size = len(fars)
+    rings, pieces = refs[0:10], refs[10:18]
+    gain_ref, bias_ref, out_ref = refs[18:21]
+    x_ref, w_ref, packed_ref, scores_ref, probs_ref, context_ref, sems = refs[21:]
+    x_size = 4
     core, at_x = info_ref[0], info_ref[1]
     depth, part = w_ref.shape[1:]
-    joined = (depth + 2 * SEQ) // 2
     sources, targets = [], []
-
-    def tokens_to(chunk, passage, ref, row):
-        for side in range(2):
-            sources.append(ref.at[pl.ds(row + side * SEQ, SEQ), :])
-            targets.append(x_ref.at[chunk, pl.ds(passage * SEQ, SEQ), pl.ds(side * part, part)])
-
     for ref, (core_at, (back, first, count)) in zip(
         rings, [(c, r) for c in (core, 1 - core) for r in RING], strict=True
     ):
         place = core_at * x_size + lax.rem(at_x - back + x_size, x_size)
-        start = first * joined
-        rows = min(count * joined, depth - start)
-        sources.append(ref.at[pl.ds(0, rows), :])
-        targets.append(w_ref.at[place, pl.ds(start, rows), :])
-    for ref, (back, first, count) in zip(rings[0:5], RING, strict=True):
-        if (first + count) * joined > depth:
-            tokens_to(back, 0, ref, depth - first * joined)
-    for back, ref in enumerate(fars):
-        tokens_to(back, 1, ref, 0)
+        sources.append(ref)
+        targets.append(w_ref.at[place, pl.ds(first * (depth // 2), count * (depth // 2)), :])
+    for k, ref in enumerate(pieces):
+        for side in range(2):
+            sources.append(ref.at[pl.ds(side * SEQ, SEQ), :])
+            rows = pl.ds(k // x_size * SEQ, SEQ)
+            targets.append(x_ref.at[k % x_size, rows, pl.ds(side * part, part)])
     put(sources, targets, sems)
     tokens, width = x_ref.shape[1:]
     left = iota((SEQ, 2 * HEAD), 1) < HEAD
@@ -253,15 +221,15 @@
     lax.fori_loop(0, x_size, step, 0)
 
 
-def encoded(info, rings, fars, gain, bias):
-    part = fars[0].shape[1]
-    tokens, width, chunks = 2 * SEQ, 2 * part, len(fars)
+def encoded(info, rings, pieces, gain, bias):
+    part = pieces[0].shape[1]
+    tokens, width, chunks = 2 * SEQ, 2 * part, len(pieces) // 2
     pairs = tokens // SEQ * HEADS // 2
     return pl.pallas_call(
         encode_kernel,
         out_shape=jax.ShapeDtypeStruct((chunks * tokens, width), BF16),
         in_specs=[pl.BlockSpec(memory_space=pltpu.SMEM)]
-        + [pl.BlockSpec(memory_space=pl.ANY)] * (len(rings) + chunks)
+        + [pl.BlockSpec(memory_space=pl.ANY)] * (len(rings) + len(pieces))
         + [pl.BlockSpec(memory_space=pltpu.VMEM)] * 2,
         out_specs=pl.BlockSpec(memory_space=pltpu.VMEM),
         scratch_shapes=[
@@ -271,16 +239,17 @@
             pltpu.VMEM((pairs, SEQ, 2 * SEQ), F32),
             pltpu.VMEM((pairs, SEQ, 2 * SEQ), BF16),
             pltpu.VMEM((tokens, width), BF16),
-            pltpu.SemaphoreType.DMA((len(rings) + 4 * chunks,)),
+            pltpu.SemaphoreType.DMA((len(rings) + 2 * len(pieces),)),
         ],
         compiler_params=pltpu.CompilerParams(vmem_limit_bytes=40 << 20),
-    )(info, *rings, *fars, gain.reshape(1, width), bias.reshape(1, width))
+    )(info, *rings, *pieces, gain.reshape(1, width), bias.reshape(1, width))
 
 
 def score_kernel(info_ref, mine_ref, other_ref, local_ref, *refs):
     parts = refs[0:5]
     out_ref, old_ref, cent_ref, sems = refs[5:]
     step = pl.program_id(0)
+    half = pl.num_programs(0) // 2
 
     @pl.when(step == 0)
     def _():
@@ -292,20 +261,26 @@
             targets.append(cent_ref.at[pl.ds(start, count * (rows_of // 2)), :])
         put(parts, targets, sems)
 
-    rows = mine_ref.shape[0]
     block = cent_ref.shape[1]
-    half = pl.num_programs(0) // 2
-    x = jnp.where(step < half, mine_ref[...], other_ref[...])
-    s = dot(x, cent_ref[...])
-    peak = jnp.max(s, axis=1, keepdims=True)
-    mass = jnp.sum(jnp.exp(s - peak), axis=1, keepdims=True)
-    local = jnp.concatenate(
-        [jnp.broadcast_to(local_ref[b], (SEQ, SEQ)).T[:, 0:1] for b in range(rows // SEQ)], axis=0
-    )
-    picked = jnp.sum(jnp.where(local == iota((rows, block), 1), s, 0.0), axis=1, keepdims=True)
-    both = jnp.where(iota((rows, 128), 1) == 0, peak + jnp.log(mass), picked)
-    for b in range(rows // SEQ):
-        out_ref[b] = both[b * SEQ : (b + 1) * SEQ, :].T[0:8, :]
+    span = 2 * SEQ
+    for n in range(mine_ref.shape[0] // span):
+        rows = slice(n * span, (n + 1) * span)
+        s = dot(jnp.where(step < half, mine_ref[rows, :], other_ref[rows, :]), cent_ref[...])
+        peak = jnp.max(s, axis=1, keepdims=True)
+        mass = jnp.sum(jnp.exp(s - peak), axis=1, keepdims=True)
+        local = jnp.concatenate(
+            [jnp.broadcast_to(local_ref[2 * n + z], (SEQ, SEQ)).T[:, 0:1] for z in range(2)], axis=0
+        )
+        picked = jnp.sum(jnp.where(local == iota((span, block), 1), s, 0.0), axis=1, keepdims=True)
+        both = jnp.where(iota((span, 128), 1) == 0, peak + jnp.log(mass), picked)
+        x_size = info_ref[5]
+        per_step = mine_ref.shape[0] // span
+        back = lax.rem(step, half) * per_step + n
+        x = lax.rem(info_ref[3] - back + x_size, x_size)
+        core = jnp.where(step < half, info_ref[2], 1 - info_ref[2])
+        for z in range(2):
+            zh = info_ref[4] if z == 0 else 1 - info_ref[4]
+            out_ref[zh * (2 * x_size) + x * 2 + core] = both[z * SEQ : (z + 1) * SEQ, :].T[0:8, :]
 
     @pl.when(step == pl.num_programs(0) - 1)
     def _():
@@ -317,7 +292,7 @@
 def scored(info, mine, other, local, parts):
     tokens, width = mine.shape
     block = parts[0].shape[1]
-    step = 2 * SEQ
+    step = 4 * SEQ
     per = step // SEQ
     half = tokens // step
     return pl.pallas_call(
@@ -335,14 +310,14 @@
         ]
         + [pl.BlockSpec(memory_space=pl.ANY)] * len(parts),
         out_specs=(
-            pl.BlockSpec((per, 8, SEQ), lambda i: (i, 0, 0)),
+            pl.BlockSpec((2 * tokens // SEQ, 8, SEQ), lambda i: (0, 0, 0)),
             pl.BlockSpec((SEQ, width), lambda i: (0, 0)),
         ),
         scratch_shapes=[
             pltpu.VMEM((width, block), BF16),
             pltpu.SemaphoreType.DMA((len(parts),)),
         ],
-        compiler_params=pltpu.CompilerParams(vmem_limit_bytes=40 << 20),
+        compiler_params=pltpu.CompilerParams(vmem_limit_bytes=48 << 20),
     )(info, mine, other, local.reshape(2 * tokens // SEQ, 1, SEQ), *parts)
 
 
@@ -428,7 +403,7 @@
     )(info, assign)
 
 
-def unpack_kernel(info_ref, counts_ref, got_ref, out_ref):
+def unpack_kernel(info_ref, counts_ref, got_ref, out_ref, most_ref):
     slabs, _, width = got_ref.shape
     counts = counts_ref[...]
     present = jnp.where(counts > 0.5, 1.0, 0.0).astype(BF16)
@@ -441,15 +416,20 @@
         parts.append(jnp.where(chosen, 1.0, 0.0))
     hits = jnp.concatenate(parts, axis=1).astype(BF16)
     out_ref[...] = dot(hits, got_ref[...].reshape(slabs * BLOCK, width))
+    most = jnp.max(got_ref[:, SLOTS, 0:128].astype(F32), axis=0, keepdims=True)
+    most_ref[...] = jnp.broadcast_to(most, most_ref.shape).astype(jnp.int32)
 
 
 def unpacked_sums(info, counts, got):
     return pl.pallas_call(
         unpack_kernel,
-        out_shape=jax.ShapeDtypeStruct((128, got.shape[2]), F32),
+        out_shape=(
+            jax.ShapeDtypeStruct((128, got.shape[2]), F32),
+            jax.ShapeDtypeStruct((8, 128), jnp.int32),
+        ),
         in_specs=[pl.BlockSpec(memory_space=pltpu.SMEM)]
         + [pl.BlockSpec(memory_space=pltpu.VMEM)] * 2,
-        out_specs=pl.BlockSpec(memory_space=pltpu.VMEM),
+        out_specs=(pl.BlockSpec(memory_space=pltpu.VMEM), pl.BlockSpec(memory_space=pltpu.VMEM)),
     )(info, counts, got)
 
 
@@ -501,7 +481,7 @@
     at_x = lax.axis_index("x")
 
     def info_of(*values):
-        return jnp.stack(values).astype(jnp.int32)
+        return jnp.stack([jnp.asarray(v, jnp.int32) for v in values])
 
     by_dev = assignments.reshape(2, x_size, 2, fs_size, SEQ)
     of_slab = lax.dynamic_index_in_dim(by_dev, fs_rank, 3, keepdims=False)
@@ -516,59 +496,64 @@
         assignments.reshape(dp_size, fs_size, SEQ),
     )
 
+    part = (w_qkv.shape[1] + w_out.shape[1]) // (2 * x_size)
+    both = jnp.concatenate([w_qkv, w_out], axis=1)
+    piece = lax.dynamic_slice_in_dim(both, (core * x_size + at_x) * part, part, 1)
+    column = gathered(piece, FS).reshape(width, part)
+
     my_row = lax.dynamic_slice_in_dim(ids, fs_rank, 1, 0)
-    my_column = core * x_size + at_x
-    sent, most = listed_rows(info_of(fs_rank, zero, my_column), ids, embed_table, (w_qkv, w_out))
+    sent, most = listed_rows(info_of(fs_rank, zero), ids, embed_table)
+    sent, column = lax.optimization_barrier((sent, column))
+    w_back, w_ahead = neighbours(column, "x")
+    rings = [column, w_back, *far_halves(w_back, w_ahead, "x"), w_ahead]
     got = exchanged(sent, FS)
     got, chosen, counts, my_row = lax.optimization_barrier((got, chosen, counts, my_row))
-    ring = expanded(info_of(fs_rank, zero, vocab), my_row, got)
+    inputs = expanded(info_of(fs_rank, zero, vocab), my_row, got)
 
     def more_rows(state):
         turn, acc = state
-        again, _ = listed_rows(info_of(fs_rank, turn, my_column), ids, embed_table)
-        extra = expanded(info_of(fs_rank, turn, vocab), my_row, exchanged(again, FS))
-        return turn + 1, acc.at[width:, :].add(extra)
+        again, _ = listed_rows(info_of(fs_rank, turn), ids, embed_table)
+        return turn + 1, acc + expanded(info_of(fs_rank, turn, vocab), my_row, exchanged(again, FS))
 
     most = most[0, 0]
-    _, ring = lax.while_loop(lambda state: state[0] * LIST < most, more_rows, (jnp.int32(1), ring))
-
-    far = swapped(ring[width:], "zh")
-    back, ahead = neighbours(ring, "x")
-    rings = [ring, back, *far_halves(back, ahead, "x"), ahead]
-    fars = [far] + [turned(far, "x", k) for k in range(1, x_size)]
-    rings += [swapped(piece, "core") for piece in rings]
-
-    shard, _ = lax.optimization_barrier((centroids_t, ring))
+    _, inputs = lax.while_loop(lambda state: state[0] * LIST < most, more_rows, (jnp.int32(1), inputs))
+
+    inputs, *rings = lax.optimization_barrier((inputs, *rings))
+    far = swapped(inputs, "zh")
+    pieces = [inputs] + [turned(inputs, "x", k) for k in range(1, x_size)]
+    far, *pieces = lax.optimization_barrier((far, *pieces))
+    pieces += [far] + [turned(far, "x", k) for k in range(1, x_size)]
+    rings += [swapped(w, "core") for w in rings]
+
+    shard, _ = lax.optimization_barrier((centroids_t, far))
     near = gathered(shard, "zl").reshape(-1, block)
-    fars[0], near = lax.optimization_barrier((fars[0], near))
+    pieces[0], near = lax.optimization_barrier((pieces[0], near))
     back, ahead = neighbours(near, "y")
     far_low, far_high = far_halves(back, ahead, "y")
 
-    mine = encoded(info_of(core, at_x), rings, fars, ln_gain, ln_bias)
-    mine, far_low, far_high = lax.optimization_barrier((mine, far_low, far_high))
+    mine = encoded(info_of(core, at_x), rings, pieces, ln_gain, ln_bias)
+    mine, back, ahead = lax.optimization_barrier((mine, back, ahead))
     other = swapped(mine, "core")
 
     def one_turn(turn):
         info = info_of(zero, turn)
         got = exchanged(packed_sums(choices(info, local, fs_size), mine, other), FS)
-        return unpacked_sums(info, counts, got)
+        return unpacked_sums(info, counts, got)[0]
 
     packed = packed_sums(chosen, mine, other)
     packed, mine, other = lax.optimization_barrier((packed, mine, other))
     got = exchanged(packed, FS)
 
     stats, previous = scored(
-        info_of(lax.axis_index("y"), fs_rank),
+        info_of(lax.axis_index("y"), fs_rank, *here, x_size),
         mine,
         other,
         local,
         [near, back, far_low, far_high, ahead],
     )
-    stats = backwards(stats.reshape(2, x_size, 2, 8, SEQ), here)
-    stats = jnp.transpose(stats, (2, 1, 0, 3, 4)).reshape(dp_size, 8, SEQ)
     stats, got = lax.optimization_barrier((stats, got))
-    sums = unpacked_sums(info_of(zero, zero), counts, got)
-    widest = jnp.max(got[:, SLOTS, 0:1].astype(F32)).astype(jnp.int32)
+    sums, widest = unpacked_sums(info_of(zero, zero), counts, got)
+    widest = widest[0, 0]
     _, sums = lax.while_loop(
         lambda state: state[0] * SLOTS < widest,
         lambda state: (state[0] + 1, state[1] + one_turn(state[0])),

time: 197 us -> 205 us (1.041)
  starting transfers between devices: 53.9 us -> 65 us
  local copies, waits for them, and re-layouts: 17 us -> 21.8 us
  waiting for transfers between devices: 59.2 us -> 54.9 us
  other arithmetic: 6.72 us -> 4.34 us
    ppermute x7, waiting for transfers between devices: 20.1 us -> 4.94 us  [swapped(): return lax.ppermute(shard, axis, [(0, 1), (1, 0)])]
    ppermute x11 -> x14, waiting for transfers between devices: 13.1 us -> 24.2 us  [turned(): lax.ppermute(shard, axis, [(i, (i + by) % devices) for i in range(devices)])]
    ppermute x11 -> x14, starting transfers between devices: 12.8 us -> 18.4 us  [turned(): lax.ppermute(shard, axis, [(i, (i + by) % devices) for i in range(devices)])]
    unnamed x56 -> x52, local copies, waits for them, and re-layouts: 7.09 us -> 12.3 us
    all_to_all x4 -> x5, starting transfers between devices: 25.5 us -> 30.1 us  [exchanged(): return lax.all_to_all(blocks, axis, 0, 0, tiled=True)]
    gather x7 -> x4, local copies, waits for them, and re-layouts: 4.57 us -> 1.72 us  [backwards(): values = jnp.take(values, (at - jnp.arange(size)) % size, axis=dim)]
    all_to_all x4 -> x5, waiting for transfers between devices: 26 us -> 25.8 us  [exchanged(): return lax.all_to_all(blocks, axis, 0, 0, tiled=True)]
  transfers between devices with their start and end apart: 22 -> 26, of which waited for: 9 -> 11; matrix products, arithmetic and copies ran while one was open for 7% -> 4% of each run, Pallas kernels for 21% -> 23%
where the time goes in v5:
time: 205 us; the launch traced here: 204 us
  starting transfers between devices  65 us (32%)
  Pallas kernels  55.4 us (27%)
  waiting for transfers between devices  54.9 us (27%)
  local copies, waits for them, and re-layouts  21.8 us (11%)
  other arithmetic  4.34 us (2%)
    all_to_all x5, starting transfers between devices, exchanged(): return lax.all_to_all(blocks, axis, 0, 0, tiled=True)  30.1 us
    all_to_all x5, waiting for transfers between devices, exchanged(): return lax.all_to_all(blocks, axis, 0, 0, tiled=True)  25.8 us
    ppermute x14, waiting for transfers between devices, turned(): lax.ppermute(shard, axis, [(i, (i + by) % devices) for i in range(devices)])  24.2 us
    ppermute x14, starting transfers between devices, turned(): lax.ppermute(shard, axis, [(i, (i + by) % devices) for i in range(devices)])  18.4 us
    pallas_call x1, Pallas kernels, encoded(): pl.pallas_call(encode_kernel, out_shape=jax.ShapeDtypeStruct((chunks * to...  17 us
    ppermute x7, starting transfers between devices, swapped(): return lax.ppermute(shard, axis, [(0, 1), (1, 0)])  16.5 us
    pallas_call x1, Pallas kernels, scored(): pl.pallas_call(score_kernel, grid=(2 * half,), out_shape=(jax.ShapeDtypeS...  13.3 us
    unnamed x52, local copies, waits for them, and re-layouts  12.3 us
  transfers between devices with their start and end apart: 26, of which 11 were waited for; matrix products, arithmetic and copies ran while one was open for 4% of the time, Pallas kernels for 23%

profile of v5, /device:TPU:1, one launch (start us, length us, event | category | flops | bytes accessed | tf_op | source)
XLA Modules:
  0.0 203.6 jit_solution(8046888861750787337)
XLA Ops:
  0.6 0.8 fusion
  1.5 0.9 broadcast_in_dim.56
  2.3 9.2 %all-to-all-start.2 = ((bf16[16,48,384]{2,1,0:T(8,128)(2,1)}), bf16[16,48,384]{2,1,0:T(8,128)(2,1)S(1)}, u32[]{:S(2)}, u32[]{:S(2)}) async-start(bf16[16,48,384]{2,1,0:T(8,128)(2,1)} %broadcast_in_dim.56), calls=%async_computation.2 | async-start | bytes 1179648 | tf_op jit(solution)/shard_map/all_to_all | solution.py:437
  11.5 0.9 constant_dynamic-slice_fusion.1
  12.4 0.6 gather_fusion
  13.1 0.6 gather_fusion.1
  13.8 5.3 %shard_map.95 = (bf16[16,32,384]{2,1,0:T(8,128)(2,1)}, s32[8,128]{1,0:T(8,128)S(1)}) custom-call(s32[2]{0:T(128)S(1)} %pad_add_fusion.3.info_ref, s32[16,128]{1,0:T(8,128)} %bitcast.52, bf16[1908,768]{1,0:T(8,128)(2,1)} %table_ref.1), custom_call_target="tpu_custom_call" | custom-call | tf_op jit(solution)/shard_map/pallas_call | solution.py:84
  19.1 9.6 %all-to-all-done.2 = bf16[16,48,384]{2,1,0:T(8,128)(2,1)S(1)} async-done(((bf16[16,48,384]{2,1,0:T(8,128)(2,1)}), bf16[16,48,384]{2,1,0:T(8,128)(2,1)S(1)}, u32[]{:S(2)}, u32[]{:S(2)}) %all-to-all-start.2) | async-done | bytes 589856 | tf_op jit(solution)/shard_map/all_to_all | solution.py:437
  28.7 1.2 collective-permute-start
  29.9 1.5 collective-permute-start.2
  31.3 4.0 %all-to-all-start.3 = ((bf16[16,32,384]{2,1,0:T(8,128)(2,1)}), bf16[16,32,384]{2,1,0:T(8,128)(2,1)S(1)}, u32[]{:S(2)}, u32[]{:S(2)}) async-start(bf16[16,32,384]{2,1,0:T(8,128)(2,1)} %get-tuple-element.120), calls=%async_computation.3 | async-start | bytes 786432 | tf_op jit(solution)/shard_map/all_to_all | solution.py:437
  35.4 0.6 gather_fusion.2
  36.6 5.6 %shard_map.96 = (bf16[768,2048]{1,0:T(8,128)(2,1)S(1)}, f32[8,128]{1,0:T(8,128)S(1)}) custom-call(s32[2]{0:T(128)S(1)} %broadcast_29_info_ref.2.info_ref, s32[1,2048]{1,0:T(1,128)S(1)} %bitcast.50), custom_call_target="tpu_custom_call" | custom-call | tf_op jit(solution)/shard_map/pallas_call | solution.py:350
  42.2 1.6 copy-done
  43.8 4.5 %shard_map.97.counts_ref = f32[128,128]{1,0:T(8,128)} custom-call(s32[1]{0:T(128)} %bitcast.19.info_ref, s32[16,16,128]{2,1,0:T(8,128)} %bitcast.56), custom_call_target="tpu_custom_call" | custom-call | tf_op jit(solution)/shard_map/pallas_call | solution.py:398
  48.3 0.6 pad_add_fusion.5.info_ref
  49.0 0.8 slice.43
  49.8 2.6 %collective-permute-start.3 = (bf16[384,384]{1,0:T(8,128)(2,1)}, bf16[384,384]{1,0:T(8,128)(2,1)S(1)}, u32[]{:S(2)}, u32[]{:S(2)}) collective-permute-start(bf16[384,384]{1,0:T(8,128)(2,1)} %slice.43), channel_id=1, source_target_pairs={{0,96},{32,0},{64,32},{96,64},{1,97},{33,1},{65,33},{97,65},{2,98}... | collective-permute-start | bytes 884744 | tf_op jit(solution)/shard_map/ppermute | solution.py:451
  52.5 0.7 copy-done.23
  53.2 1.5 shard_map.98
  54.8 0.6 while.20
  55.3 1.5 collective-permute-done.1.refs_2_
  56.9 4.2 %collective-permute-start.9 = (bf16[256,384]{1,0:T(8,128)(2,1)S(1)}, bf16[256,384]{1,0:T(8,128)(2,1)}, u32[]{:S(2)}, u32[]{:S(2)}) collective-permute-start(bf16[256,384]{1,0:T(8,128)(2,1)S(1)} %get-tuple-element.139.refs_10_), channel_id=1, source_target_pairs={{0,128},{128,0},{1,129},{129,1},{2,130},{130,2},{3,131},{131,3},{4... | collective-permute-start | bytes 589832 | tf_op jit(solution)/shard_map/ppermute | solution.py:446
  61.2 0.6 collective-permute-start.10
  61.8 3.9 %collective-permute-start.11 = (bf16[256,384]{1,0:T(8,128)(2,1)S(1)}, bf16[256,384]{1,0:T(8,128)(2,1)S(1)}, u32[]{:S(2)}, u32[]{:S(2)}) collective-permute-start(bf16[256,384]{1,0:T(8,128)(2,1)S(1)} %get-tuple-element.139.refs_10_), channel_id=1, source_target_pairs={{0,64},{32,96},{64,0},{96,32},{1,65},{33,97},{65,1},{97,33},{2,66}... | collective-permute-start | bytes 589832 | tf_op jit(solution)/shard_map/ppermute | solution.py:451
  65.7 2.3 %collective-permute-done.10.refs_11_ = bf16[256,384]{1,0:T(8,128)(2,1)S(1)} collective-permute-done((bf16[256,384]{1,0:T(8,128)(2,1)S(1)}, bf16[256,384]{1,0:T(8,128)(2,1)S(1)}, u32[]{:S(2)}, u32[]{:S(2)}) %collective-permute-start.10) | collective-permute-done | bytes 196640 | tf_op jit(solution)/shard_map/ppermute | solution.py:451
  67.9 3.2 %collective-permute-done.11.refs_12_ = bf16[256,384]{1,0:T(8,128)(2,1)S(1)} collective-permute-done((bf16[256,384]{1,0:T(8,128)(2,1)S(1)}, bf16[256,384]{1,0:T(8,128)(2,1)S(1)}, u32[]{:S(2)}, u32[]{:S(2)}) %collective-permute-start.11) | collective-permute-done | bytes 196640 | tf_op jit(solution)/shard_map/ppermute | solution.py:451
  71.1 0.7 copy-done.16
  71.9 1.9 broadcast_in_dim.61
  73.8 4.1 %all-to-all-start.4 = ((bf16[4,48,2048]{2,1,0:T(8,128)(2,1)}), bf16[4,48,2048]{2,1,0:T(8,128)(2,1)S(1)}, u32[]{:S(2)}, u32[]{:S(2)}) async-start(bf16[4,48,2048]{2,1,0:T(8,128)(2,1)} %broadcast_in_dim.61), calls=%async_computation.4 | async-start | bytes 1572864 | tf_op jit(solution)/shard_map/all_to_all | solution.py:437
  77.8 5.0 %collective-permute-start.6 = (bf16[384,384]{1,0:T(8,128)(2,1)S(1)}, bf16[384,384]{1,0:T(8,128)(2,1)S(1)}, u32[]{:S(2)}, u32[]{:S(2)}) collective-permute-start(bf16[384,384]{1,0:T(8,128)(2,1)S(1)} %collective-permute-done.1.refs_2_), channel_id=1, source_target_pairs={{0,16},{16,0},{1,17},{17,1},{2,18},{18,2},{3,19},{19,3},{4,20},{20... | collective-permute-start | bytes 884744 | tf_op jit(solution)/shard_map/ppermute | solution.py:446
  83.0 2.9 %collective-permute-start.14 = (bf16[256,384]{1,0:T(8,128)(2,1)}, bf16[256,384]{1,0:T(8,128)(2,1)}, u32[]{:S(2)}, u32[]{:S(2)}) collective-permute-start(bf16[256,384]{1,0:T(8,128)(2,1)} %collective-permute-done.9.refs_14_), channel_id=1, source_target_pairs={{0,64},{32,96},{64,0},{96,32},{1,65},{33,97},{65,1},{97,33},{2,66}... | collective-permute-start | bytes 589832 | tf_op jit(solution)/shard_map/ppermute | solution.py:451
  86.0 7.3 %all-to-all-done.4 = bf16[4,48,2048]{2,1,0:T(8,128)(2,1)S(1)} async-done(((bf16[4,48,2048]{2,1,0:T(8,128)(2,1)}), bf16[4,48,2048]{2,1,0:T(8,128)(2,1)S(1)}, u32[]{:S(2)}, u32[]{:S(2)}) %all-to-all-start.4) | async-done | bytes 786464 | tf_op jit(solution)/shard_map/all_to_all | solution.py:437
  93.3 0.7 copy-done.8
  94.0 1.1 collective-permute-start.16
  95.2 0.7 copy-done.10
  95.9 1.5 collective-permute-start.17
  97.4 6.2 %collective-permute-start.4 = (bf16[768,384]{1,0:T(8,128)(2,1)S(1)}, bf16[768,384]{1,0:T(8,128)(2,1)S(1)}, u32[]{:S(2)}, u32[]{:S(2)}) collective-permute-start(bf16[768,384]{1,0:T(8,128)(2,1)S(1)} %bitcast.48), channel_id=1, source_target_pairs={{0,16},{16,0},{1,17},{17,1},{2,18},{18,2},{3,19},{19,3},{4,20},{20... | collective-permute-start | bytes 1769480 | tf_op jit(solution)/shard_map/ppermute | solution.py:446
  104.1 0.7 reshape.269.refs_18_
  104.8 0.7 reshape.270.refs_19_
  105.6 1.3 collective-permute-done.5.refs_6_
  107.1 1.1 copy-done.3
  108.2 1.0 copy-done.5
  109.2 1.0 copy-done.7
  110.1 1.0 copy-done.9
  111.1 1.0 copy-done.11
  112.0 0.9 copy-done.13
  113.0 0.9 copy-done.15
  113.9 0.9 copy-done.17
  114.8 17.0 %shard_map.99.mine_ref = bf16[1024,768]{1,0:T(8,128)(2,1)} custom-call(s32[2]{0:T(128)S(1)} %pad_add_fusion.4.info_ref, bf16[768,384]{1,0:T(8,128)(2,1)S(1)} %bitcast.49, bf16[768,384]{1,0:T(8,128)(2,1)S(1)} %collective-permute-done.refs_1_, bf16[384,384]{1,0:T(8,128)(2,1)S(1)} %copy-done.5, bf16[384,384]{1,0:T(8,128)(2,1)S(1)} %copy-done.7, ...), custom_call_target="tpu_custom_call" | custom-call | tf_op jit(solution)/shard_map/pallas_call | solution.py:228
  132.3 3.4 %collective-permute-done.18.other_ref = bf16[1024,768]{1,0:T(8,128)(2,1)} collective-permute-done((bf16[1024,768]{1,0:T(8,128)(2,1)}, bf16[1024,768]{1,0:T(8,128)(2,1)}, u32[]{:S(2)}, u32[]{:S(2)}) %collective-permute-start.18) | collective-permute-done | bytes 1572896 | tf_op jit(solution)/shard_map/ppermute | solution.py:446
  135.7 5.4 %shard_map.100 = bf16[16,40,768]{2,1,0:T(8,128)(2,1)} custom-call(bf16[768,2048]{1,0:T(8,128)(2,1)S(1)} %copy-done.1, f32[8,128]{1,0:T(8,128)S(1)} %get-tuple-element.124.most_ref, bf16[1024,768]{1,0:T(8,128)(2,1)} %shard_map.99.mine_ref, bf16[1024,768]{1,0:T(8,128)(2,1)} %collective-permute-done.18.other_ref), custom_call_target="tpu_custom_call" | custom-call | tf_op jit(solution)/shard_map/pallas_call | solution.py:374
  141.2 4.6 %all-to-all-start.5 = ((bf16[16,40,768]{2,1,0:T(8,128)(2,1)}), bf16[16,40,768]{2,1,0:T(8,128)(2,1)}, u32[]{:S(2)}, u32[]{:S(2)}) async-start(bf16[16,40,768]{2,1,0:T(8,128)(2,1)} %shard_map.100), calls=%async_computation.5 | async-start | bytes 1966080 | tf_op jit(solution)/shard_map/all_to_all | solution.py:437
  146.0 0.9 slice_reduce_fusion
  147.0 1.3 collective-permute-start.19
  148.3 1.5 collective-permute-start.20
  149.9 17.1 %collective-permute-done.19.refs_2_ = bf16[96,2048]{1,0:T(8,128)(2,1)S(1)} collective-permute-done((bf16[96,2048]{1,0:T(8,128)(2,1)S(1)}, bf16[96,2048]{1,0:T(8,128)(2,1)S(1)}, u32[]{:S(2)}, u32[]{:S(2)}) %collective-permute-start.19) | collective-permute-done | bytes 393248 | tf_op jit(solution)/shard_map/ppermute | solution.py:451
  167.0 13.3 %shard_map.101 = (f32[16,8,128]{2,1,0:T(8,128)}, f32[128,768]{1,0:T(8,128)S(1)}) custom-call(s32[6]{0:T(128)S(1)} %stack.59.info_ref, bf16[1024,768]{1,0:T(8,128)(2,1)} %shard_map.99.mine_ref, bf16[1024,768]{1,0:T(8,128)(2,1)} %collective-permute-done.18.other_ref, s32[16,1,128]{2,1,0:T(1,128)S(1)} %fusion.2.local_ref, bf16[192,2048]{1,0:T(8,128)(2,1)S(1)} %bitcast.45, ...), custom_call_target="tpu_custom_call" | custom-call | tf_op jit(solution)/shard_map/pallas_call | solution.py:298
  180.3 2.8 %shard_map.102 = (f32[128,768]{1,0:T(8,128)S(1)}, s32[8,128]{1,0:T(8,128)}) custom-call(s32[2]{0:T(128)} %copy-done.19, f32[128,128]{1,0:T(8,128)} %shard_map.97.counts_ref, bf16[16,40,768]{2,1,0:T(8,128)(2,1)} %all-to-all-done.5.got_ref), custom_call_target="tpu_custom_call" | custom-call | tf_op jit(solution)/shard_map/pallas_call | solution.py:424
  183.2 1.2 slice.35
  184.4 0.7 while.21
  185.0 8.3 %all-to-all-start.6 = ((f32[16,8,128]{2,1,0:T(8,128)}), f32[16,8,128]{2,1,0:T(8,128)S(1)}, u32[]{:S(2)}, u32[]{:S(2)}) async-start(f32[16,8,128]{2,1,0:T(8,128)} %get-tuple-element.151), calls=%async_computation.6 | async-start | bytes 131072 | tf_op jit(solution)/shard_map/all_to_all | solution.py:437
  193.3 0.9 divide_select_fusion
  194.2 8.9 %all-to-all-done.6 = f32[16,8,128]{2,1,0:T(8,128)S(1)} async-done(((f32[16,8,128]{2,1,0:T(8,128)}), f32[16,8,128]{2,1,0:T(8,128)S(1)}, u32[]{:S(2)}, u32[]{:S(2)}) %all-to-all-start.6) | async-done | bytes 65568 | tf_op jit(solution)/shard_map/all_to_all | solution.py:437
  (96 shorter events, 3.7 us)
Async XLA Ops:
  1.5 46.8 %copy-start.24 = (s32[2048]{0:T(1024)S(1)}, s32[2048]{0:T(1024)}, u32[]{:S(2)}) copy-start(s32[2048]{0:T(1024)} %param.12) | copy-start | bytes 24580
  2.3 26.3 %all-to-all-start.2 = ((bf16[16,48,384]{2,1,0:T(8,128)(2,1)}), bf16[16,48,384]{2,1,0:T(8,128)(2,1)S(1)}, u32[]{:S(2)}, u32[]{:S(2)}) async-start(bf16[16,48,384]{2,1,0:T(8,128)(2,1)} %broadcast_in_dim.56), calls=%async_computation.2 | async-start | bytes 1179648 | tf_op jit(solution)/shard_map/all_to_all | solution.py:437
  13.0 41.7 %copy-start.27 = (pred[2]{0:T(512)(128)(4,1)}, pred[2]{0:T(512)(128)(4,1)S(1)}, u32[]{:S(2)}) copy-start(pred[2]{0:T(512)(128)(4,1)S(1)} %get-tuple-element.190) | copy-start | bytes 10
  28.7 20.2 %collective-permute-start = (bf16[768,384]{1,0:T(8,128)(2,1)S(1)}, bf16[768,384]{1,0:T(8,128)(2,1)S(1)}, u32[]{:S(2)}, u32[]{:S(2)}) collective-permute-start(bf16[768,384]{1,0:T(8,128)(2,1)S(1)} %bitcast.46), channel_id=1, source_target_pairs={{0,32},{32,64},{64,96},{96,0},{1,33},{33,65},{65,97},{97,1},{2,34}... | collective-permute-start | bytes 1769480 | tf_op jit(solution)/shard_map/ppermute | solution.py:451
  29.9 19.1 %collective-permute-start.2 = (bf16[768,384]{1,0:T(8,128)(2,1)S(1)}, bf16[768,384]{1,0:T(8,128)(2,1)S(1)}, u32[]{:S(2)}, u32[]{:S(2)}) collective-permute-start(bf16[768,384]{1,0:T(8,128)(2,1)S(1)} %bitcast.47), channel_id=1, source_target_pairs={{0,96},{32,0},{64,32},{96,64},{1,97},{33,1},{65,33},{97,65},{2,98}... | collective-permute-start | bytes 1769480 | tf_op jit(solution)/shard_map/ppermute | solution.py:451
  31.3 21.1 %all-to-all-start.3 = ((bf16[16,32,384]{2,1,0:T(8,128)(2,1)}), bf16[16,32,384]{2,1,0:T(8,128)(2,1)S(1)}, u32[]{:S(2)}, u32[]{:S(2)}) async-start(bf16[16,32,384]{2,1,0:T(8,128)(2,1)} %get-tuple-element.120), calls=%async_computation.3 | async-start | bytes 786432 | tf_op jit(solution)/shard_map/all_to_all | solution.py:437
  36.0 18.8 %copy-start.25 = (s32[2,2,4,128]{3,2,1,0:T(4,128)}, s32[2,2,4,128]{3,2,1,0:T(4,128)S(1)}, u32[]{:S(2)}) copy-start(s32[2,2,4,128]{3,2,1,0:T(4,128)S(1)} %gather_fusion.2) | copy-start | bytes 24580
  36.6 18.2 %copy-start.19 = (s32[2]{0:T(128)}, s32[2]{0:T(128)S(1)}, u32[]{:S(2)}) copy-start(s32[2]{0:T(128)S(1)} %broadcast_29_info_ref.2.info_ref) | copy-start | bytes 28
  42.2 1.6 copy-start
  48.9 7.9 %collective-permute-start.1 = (bf16[384,384]{1,0:T(8,128)(2,1)S(1)}, bf16[384,384]{1,0:T(8,128)(2,1)S(1)}, u32[]{:S(2)}, u32[]{:S(2)}) collective-permute-start(bf16[384,384]{1,0:T(8,128)(2,1)S(1)} %slice.42), channel_id=1, source_target_pairs={{0,32},{32,64},{64,96},{96,0},{1,33},{33,65},{65,97},{97,1},{2,34}... | collective-permute-start | bytes 884744 | tf_op jit(solution)/shard_map/ppermute | solution.py:451
  49.0 5.7 %copy-start.2 = (bf16[768,384]{1,0:T(8,128)(2,1)}, bf16[768,384]{1,0:T(8,128)(2,1)S(1)}, u32[]{:S(2)}) copy-start(bf16[768,384]{1,0:T(8,128)(2,1)S(1)} %collective-permute-done.2.refs_4_) | copy-start | bytes 1769476
  49.8 7.1 %collective-permute-start.3 = (bf16[384,384]{1,0:T(8,128)(2,1)}, bf16[384,384]{1,0:T(8,128)(2,1)S(1)}, u32[]{:S(2)}, u32[]{:S(2)}) collective-permute-start(bf16[384,384]{1,0:T(8,128)(2,1)} %slice.43), channel_id=1, source_target_pairs={{0,96},{32,0},{64,32},{96,64},{1,97},{33,1},{65,33},{97,65},{2,98}... | collective-permute-start | bytes 884744 | tf_op jit(solution)/shard_map/ppermute | solution.py:451
  52.5 0.7 copy-start.23
  55.3 22.5 %copy-start.22 = (bf16[256,384]{1,0:T(8,128)(2,1)}, bf16[256,384]{1,0:T(8,128)(2,1)S(1)}, u32[]{:S(2)}) copy-start(bf16[256,384]{1,0:T(8,128)(2,1)S(1)} %get-tuple-element.139.refs_10_) | copy-start | bytes 589828
  56.8 36.5 %copy-start.4 = (bf16[384,384]{1,0:T(8,128)(2,1)}, bf16[384,384]{1,0:T(8,128)(2,1)S(1)}, u32[]{:S(2)}) copy-start(bf16[384,384]{1,0:T(8,128)(2,1)S(1)} %collective-permute-done.1.refs_2_) | copy-start | bytes 884740
  56.9 38.2 %copy-start.6 = (bf16[384,384]{1,0:T(8,128)(2,1)}, bf16[384,384]{1,0:T(8,128)(2,1)S(1)}, u32[]{:S(2)}) copy-start(bf16[384,384]{1,0:T(8,128)(2,1)S(1)} %collective-permute-done.3.refs_3_) | copy-start | bytes 884740
  56.9 8.7 %collective-permute-start.9 = (bf16[256,384]{1,0:T(8,128)(2,1)S(1)}, bf16[256,384]{1,0:T(8,128)(2,1)}, u32[]{:S(2)}, u32[]{:S(2)}) collective-permute-start(bf16[256,384]{1,0:T(8,128)(2,1)S(1)} %get-tuple-element.139.refs_10_), channel_id=1, source_target_pairs={{0,128},{128,0},{1,129},{129,1},{2,130},{130,2},{3,131},{131,3},{4... | collective-permute-start | bytes 589832 | tf_op jit(solution)/shard_map/ppermute | solution.py:446
  61.2 6.8 %collective-permute-start.10 = (bf16[256,384]{1,0:T(8,128)(2,1)S(1)}, bf16[256,384]{1,0:T(8,128)(2,1)S(1)}, u32[]{:S(2)}, u32[]{:S(2)}) collective-permute-start(bf16[256,384]{1,0:T(8,128)(2,1)S(1)} %get-tuple-element.139.refs_10_), channel_id=1, source_target_pairs={{0,32},{32,64},{64,96},{96,0},{1,33},{33,65},{65,97},{97,1},{2,34}... | collective-permute-start | bytes 589832 | tf_op jit(solution)/shard_map/ppermute | solution.py:451
  61.8 9.3 %collective-permute-start.11 = (bf16[256,384]{1,0:T(8,128)(2,1)S(1)}, bf16[256,384]{1,0:T(8,128)(2,1)S(1)}, u32[]{:S(2)}, u32[]{:S(2)}) collective-permute-start(bf16[256,384]{1,0:T(8,128)(2,1)S(1)} %get-tuple-element.139.refs_10_), channel_id=1, source_target_pairs={{0,64},{32,96},{64,0},{96,32},{1,65},{33,97},{65,1},{97,33},{2,66}... | collective-permute-start | bytes 589832 | tf_op jit(solution)/shard_map/ppermute | solution.py:451
  65.6 5.5 %collective-permute-start.12 = (bf16[256,384]{1,0:T(8,128)(2,1)S(1)}, bf16[256,384]{1,0:T(8,128)(2,1)S(1)}, u32[]{:S(2)}, u32[]{:S(2)}) collective-permute-start(bf16[256,384]{1,0:T(8,128)(2,1)S(1)} %get-tuple-element.139.refs_10_), channel_id=1, source_target_pairs={{0,96},{32,0},{64,32},{96,64},{1,97},{33,1},{65,33},{97,65},{2,98}... | collective-permute-start | bytes 589832 | tf_op jit(solution)/shard_map/ppermute | solution.py:451
  67.9 5.8 %copy-start.12 = (bf16[256,384]{1,0:T(8,128)(2,1)}, bf16[256,384]{1,0:T(8,128)(2,1)S(1)}, u32[]{:S(2)}) copy-start(bf16[256,384]{1,0:T(8,128)(2,1)S(1)} %collective-permute-done.10.refs_11_) | copy-start | bytes 589828
  71.1 2.6 %copy-start.14 = (bf16[256,384]{1,0:T(8,128)(2,1)}, bf16[256,384]{1,0:T(8,128)(2,1)S(1)}, u32[]{:S(2)}) copy-start(bf16[256,384]{1,0:T(8,128)(2,1)S(1)} %collective-permute-done.11.refs_12_) | copy-start | bytes 589828
  71.1 0.7 copy-start.16
  73.8 19.5 %all-to-all-start.4 = ((bf16[4,48,2048]{2,1,0:T(8,128)(2,1)}), bf16[4,48,2048]{2,1,0:T(8,128)(2,1)S(1)}, u32[]{:S(2)}, u32[]{:S(2)}) async-start(bf16[4,48,2048]{2,1,0:T(8,128)(2,1)} %broadcast_in_dim.61), calls=%async_computation.4 | async-start | bytes 1572864 | tf_op jit(solution)/shard_map/all_to_all | solution.py:437
  77.8 15.5 %collective-permute-start.6 = (bf16[384,384]{1,0:T(8,128)(2,1)S(1)}, bf16[384,384]{1,0:T(8,128)(2,1)S(1)}, u32[]{:S(2)}, u32[]{:S(2)}) collective-permute-start(bf16[384,384]{1,0:T(8,128)(2,1)S(1)} %collective-permute-done.1.refs_2_), channel_id=1, source_target_pairs={{0,16},{16,0},{1,17},{17,1},{2,18},{18,2},{3,19},{19,3},{4,20},{20... | collective-permute-start | bytes 884744 | tf_op jit(solution)/shard_map/ppermute | solution.py:446
  82.9 12.3 %collective-permute-start.7 = (bf16[384,384]{1,0:T(8,128)(2,1)S(1)}, bf16[384,384]{1,0:T(8,128)(2,1)S(1)}, u32[]{:S(2)}, u32[]{:S(2)}) collective-permute-start(bf16[384,384]{1,0:T(8,128)(2,1)S(1)} %collective-permute-done.3.refs_3_), channel_id=1, source_target_pairs={{0,16},{16,0},{1,17},{17,1},{2,18},{18,2},{3,19},{19,3},{4,20},{20... | collective-permute-start | bytes 884744 | tf_op jit(solution)/shard_map/ppermute | solution.py:446
  83.0 14.5 %collective-permute-start.13 = (bf16[256,384]{1,0:T(8,128)(2,1)}, bf16[256,384]{1,0:T(8,128)(2,1)}, u32[]{:S(2)}, u32[]{:S(2)}) collective-permute-start(bf16[256,384]{1,0:T(8,128)(2,1)} %collective-permute-done.9.refs_14_), channel_id=1, source_target_pairs={{0,32},{32,64},{64,96},{96,0},{1,33},{33,65},{65,97},{97,1},{2,34}... | collective-permute-start | bytes 589832 | tf_op jit(solution)/shard_map/ppermute | solution.py:451
  83.0 20.6 %collective-permute-start.14 = (bf16[256,384]{1,0:T(8,128)(2,1)}, bf16[256,384]{1,0:T(8,128)(2,1)}, u32[]{:S(2)}, u32[]{:S(2)}) collective-permute-start(bf16[256,384]{1,0:T(8,128)(2,1)} %collective-permute-done.9.refs_14_), channel_id=1, source_target_pairs={{0,64},{32,96},{64,0},{96,32},{1,65},{33,97},{65,1},{97,33},{2,66}... | collective-permute-start | bytes 589832 | tf_op jit(solution)/shard_map/ppermute | solution.py:451
  85.9 17.8 %collective-permute-start.15 = (bf16[256,384]{1,0:T(8,128)(2,1)}, bf16[256,384]{1,0:T(8,128)(2,1)}, u32[]{:S(2)}, u32[]{:S(2)}) collective-permute-start(bf16[256,384]{1,0:T(8,128)(2,1)} %collective-permute-done.9.refs_14_), channel_id=1, source_target_pairs={{0,96},{32,0},{64,32},{96,64},{1,97},{33,1},{65,33},{97,65},{2,98}... | collective-permute-start | bytes 589832 | tf_op jit(solution)/shard_map/ppermute | solution.py:451
  93.3 0.7 copy-start.8
  94.0 37.8 %collective-permute-start.16 = (bf16[192,2048]{1,0:T(8,128)(2,1)S(1)}, bf16[192,2048]{1,0:T(8,128)(2,1)S(1)}, u32[]{:S(2)}, u32[]{:S(2)}) collective-permute-start(bf16[192,2048]{1,0:T(8,128)(2,1)S(1)} %bitcast.43), channel_id=1, source_target_pairs={{0,4},{4,8},{8,12},{12,0},{1,5},{5,9},{9,13},{13,1},{2,6},{6,10},{... | collective-permute-start | bytes 2359304 | tf_op jit(solution)/shard_map/ppermute | solution.py:451
  95.2 0.7 copy-start.10
  95.9 36.0 %collective-permute-start.17 = (bf16[192,2048]{1,0:T(8,128)(2,1)S(1)}, bf16[192,2048]{1,0:T(8,128)(2,1)S(1)}, u32[]{:S(2)}, u32[]{:S(2)}) collective-permute-start(bf16[192,2048]{1,0:T(8,128)(2,1)S(1)} %bitcast.44), channel_id=1, source_target_pairs={{0,12},{4,0},{8,4},{12,8},{1,13},{5,1},{9,5},{13,9},{2,14},{6,2},{... | collective-permute-start | bytes 2359304 | tf_op jit(solution)/shard_map/ppermute | solution.py:451
  97.4 8.1 %collective-permute-start.4 = (bf16[768,384]{1,0:T(8,128)(2,1)S(1)}, bf16[768,384]{1,0:T(8,128)(2,1)S(1)}, u32[]{:S(2)}, u32[]{:S(2)}) collective-permute-start(bf16[768,384]{1,0:T(8,128)(2,1)S(1)} %bitcast.48), channel_id=1, source_target_pairs={{0,16},{16,0},{1,17},{17,1},{2,18},{18,2},{3,19},{19,3},{4,20},{20... | collective-permute-start | bytes 1769480 | tf_op jit(solution)/shard_map/ppermute | solution.py:446
  103.6 3.3 %collective-permute-start.5 = (bf16[768,384]{1,0:T(8,128)(2,1)S(1)}, bf16[768,384]{1,0:T(8,128)(2,1)S(1)}, u32[]{:S(2)}, u32[]{:S(2)}) collective-permute-start(bf16[768,384]{1,0:T(8,128)(2,1)S(1)} %collective-permute-done.refs_1_), channel_id=1, source_target_pairs={{0,16},{16,0},{1,17},{17,1},{2,18},{18,2},{3,19},{19,3},{4,20},{20... | collective-permute-start | bytes 1769480 | tf_op jit(solution)/shard_map/ppermute | solution.py:446
  103.7 3.4 %collective-permute-start.8 = (bf16[768,384]{1,0:T(8,128)(2,1)}, bf16[768,384]{1,0:T(8,128)(2,1)S(1)}, u32[]{:S(2)}, u32[]{:S(2)}) collective-permute-start(bf16[768,384]{1,0:T(8,128)(2,1)} %copy-done.2), channel_id=1, source_target_pairs={{0,16},{16,0},{1,17},{17,1},{2,18},{18,2},{3,19},{19,3},{4,20},{20... | collective-permute-start | bytes 1769480 | tf_op jit(solution)/shard_map/ppermute | solution.py:446
  105.6 30.1 %copy-start.1 = (bf16[768,2048]{1,0:T(8,128)(2,1)S(1)}, bf16[768,2048]{1,0:T(8,128)(2,1)}, u32[]{:S(2)}) copy-start(bf16[768,2048]{1,0:T(8,128)(2,1)} %copy-done) | copy-start | bytes 9437188
  107.1 1.1 copy-start.3
  108.2 1.0 copy-start.5
  109.2 1.0 copy-start.7
  110.1 1.0 copy-start.9
  111.1 1.0 copy-start.11
  112.0 0.9 copy-start.13
  113.0 0.9 copy-start.15
  113.9 0.9 copy-start.17
  131.8 13.9 %copy-start.26 = (s32[2,2,4,128]{3,2,1,0:T(4,128)S(1)}, s32[2,2,4,128]{3,2,1,0:T(4,128)}, u32[]{:S(2)}) copy-start(s32[2,2,4,128]{3,2,1,0:T(4,128)} %copy-done.25) | copy-start | bytes 24580
  131.8 13.9 %copy-start.28 = (pred[2]{0:T(512)(128)(4,1)S(1)}, pred[2]{0:T(512)(128)(4,1)}, u32[]{:S(2)}) copy-start(pred[2]{0:T(512)(128)(4,1)} %copy-done.27) | copy-start | bytes 10
  131.9 3.8 %collective-permute-start.18 = (bf16[1024,768]{1,0:T(8,128)(2,1)}, bf16[1024,768]{1,0:T(8,128)(2,1)}, u32[]{:S(2)}, u32[]{:S(2)}) collective-permute-start(bf16[1024,768]{1,0:T(8,128)(2,1)} %shard_map.99.mine_ref), channel_id=1, source_target_pairs={{0,16},{16,0},{1,17},{17,1},{2,18},{18,2},{3,19},{19,3},{4,20},{20... | collective-permute-start | bytes 4718600 | tf_op jit(solution)/shard_map/ppermute | solution.py:446
  141.2 39.2 %all-to-all-start.5 = ((bf16[16,40,768]{2,1,0:T(8,128)(2,1)}), bf16[16,40,768]{2,1,0:T(8,128)(2,1)}, u32[]{:S(2)}, u32[]{:S(2)}) async-start(bf16[16,40,768]{2,1,0:T(8,128)(2,1)} %shard_map.100), calls=%async_computation.5 | async-start | bytes 1966080 | tf_op jit(solution)/shard_map/all_to_all | solution.py:437
  147.0 20.0 %collective-permute-start.19 = (bf16[96,2048]{1,0:T(8,128)(2,1)S(1)}, bf16[96,2048]{1,0:T(8,128)(2,1)S(1)}, u32[]{:S(2)}, u32[]{:S(2)}) collective-permute-start(bf16[96,2048]{1,0:T(8,128)(2,1)S(1)} %slice.44), channel_id=1, source_target_pairs={{0,4},{4,8},{8,12},{12,0},{1,5},{5,9},{9,13},{13,1},{2,6},{6,10},{... | collective-permute-start | bytes 1179656 | tf_op jit(solution)/shard_map/ppermute | solution.py:451
  148.3 18.6 %collective-permute-start.20 = (bf16[96,2048]{1,0:T(8,128)(2,1)S(1)}, bf16[96,2048]{1,0:T(8,128)(2,1)S(1)}, u32[]{:S(2)}, u32[]{:S(2)}) collective-permute-start(bf16[96,2048]{1,0:T(8,128)(2,1)S(1)} %slice.45), channel_id=1, source_target_pairs={{0,12},{4,0},{8,4},{12,8},{1,13},{5,1},{9,5},{13,9},{2,14},{6,2},{... | collective-permute-start | bytes 1179656 | tf_op jit(solution)/shard_map/ppermute | solution.py:451
  185.0 18.0 %all-to-all-start.6 = ((f32[16,8,128]{2,1,0:T(8,128)}), f32[16,8,128]{2,1,0:T(8,128)S(1)}, u32[]{:S(2)}, u32[]{:S(2)}) async-start(f32[16,8,128]{2,1,0:T(8,128)} %get-tuple-element.151), calls=%async_computation.6 | async-start | bytes 131072 | tf_op jit(solution)/shard_map/all_to_all | solution.py:437
